TPU v7x, 32 devices: a whole 2x2x4 slice. The times are simulated.
32 devices in a mesh: fsdp: 8 (over y, x, core), tp: 4 (over z).
Axes of the slice: x: 2, y: 2, z: 4, core: 2. Of those that a mesh axis runs over, the one named last changes fastest.
Arguments:
- tokens_in: bfloat16 [2, 2560, 2048], P(None, ('fsdp', 'tp')), may hold values from -6 to 6
- out_grad: bfloat16 [2, 2560, 2048], P(None, ('fsdp', 'tp')), may hold values from -6 to 6
- segment_ids: int32 [2, 2560], P(None, 'fsdp'), may hold values from 0 to 2, as said below
- expert_ids: int32 [2, 2560, 2], P(None, 'fsdp'), may hold values from 0 to 3, all different within a row; in each aligned block of 320 rows (0 to 319, 320 to 639, ..., all dimensions but the last counted through in order) at most 200 rows name the same one
- attn_gain: bfloat16 [2048], P(('fsdp', 'tp')), may hold values from 0.5 to 1.5
- w_query: bfloat16 [2048, 2048], P('fsdp', 'tp'), may hold values from -0.1875 to 0.1875
- w_key: bfloat16 [2048, 2048], P('fsdp', 'tp'), may hold values from -0.1875 to 0.1875
- w_value: bfloat16 [2048, 2048], P('fsdp', 'tp'), may hold values from -0.125 to 0.125
- w_output: bfloat16 [2048, 2048], P('tp', 'fsdp'), may hold values from -0.5 to 0.5
- ffn_gain: bfloat16 [2048], P(('fsdp', 'tp')), may hold values from 0.5 to 1.5
- w_router: bfloat16 [2048, 4], P(('fsdp', 'tp')), may hold values from -0.125 to 0.125
- w_gate: bfloat16 [4, 2048, 5632], P(None, 'fsdp', 'tp'), may hold values from -0.125 to 0.125
- w_up: bfloat16 [4, 2048, 5632], P(None, 'fsdp', 'tp'), may hold values from -0.125 to 0.125
- w_down: bfloat16 [4, 5632, 2048], P(None, 'tp', 'fsdp'), may hold values from -0.15625 to 0.15625
Outputs:
- output: bfloat16 [2, 2560, 2048], P(None, ('fsdp', 'tp'))
- input_grad: bfloat16 [2, 2560, 2048], P(None, ('fsdp', 'tp'))
- attn_gain_grad: float32 [2048], P(('fsdp', 'tp'))
- w_query_grad: float32 [2048, 2048], P('fsdp', 'tp')
- w_key_grad: float32 [2048, 2048], P('fsdp', 'tp')
- w_value_grad: float32 [2048, 2048], P('fsdp', 'tp')
- w_output_grad: float32 [2048, 2048], P('tp', 'fsdp')
- ffn_gain_grad: float32 [2048], P(('fsdp', 'tp'))
- w_router_grad: float32 [2048, 4], P(('fsdp', 'tp'))
- w_gate_grad: float32 [4, 2048, 5632], P(None, 'fsdp', 'tp')
- w_up_grad: float32 [4, 2048, 5632], P(None, 'fsdp', 'tp')
- w_down_grad: float32 [4, 5632, 2048], P(None, 'tp', 'fsdp')
Inputs may be any that keep to these rules, and one draw needn't show every extreme that they name: `expert_ids`: each row names two different experts. In each aligned block of 320 rows (one group of a micro-batch) no expert is named by more than 200 rows, a bound that some block reaches. `segment_ids`: in each aligned block of 320 rows (one group of a micro-batch) the first 192 rows have segment 0; the other rows hold segments 1 to 2 in order, never falling, each with one row or more.
All inputs are finite; a program needn't handle non-finite values.
Results may differ from a plain program's by a relative error of at most 0.025.
Values may be sent and summed in bfloat16 or wider, within the bound.
No kernel may reach another device: no remote copies, remote signals or barrier semaphores. Data moves between devices by JAX's collectives and lax.ppermute only.
A program may use at most 384 MiB of HBM per device.

v0:
```python
import math

import jax
import jax.numpy as jnp
from jax import lax
from jax.sharding import PartitionSpec as P


HD = 128
CAP = 200
PAIR = 2
EPSILON = 1e-05
MASKED = -1e30
HIGHEST = lax.Precision.HIGHEST
BF16 = jnp.bfloat16
F32 = jnp.float32


def inverse_rms(values):
    return lax.rsqrt(jnp.mean(values * values, axis=-1, keepdims=True) + EPSILON)


def norm_backward(inputs, gain, grad_out):
    inv_scale = inverse_rms(inputs)
    gain_grad = jnp.sum(grad_out * inputs * inv_scale, axis=(0, 1))
    scaled = grad_out * gain
    input_grad = inv_scale * scaled - inputs * (inv_scale * inv_scale * inv_scale) * jnp.mean(
        scaled * inputs, axis=-1, keepdims=True
    )
    return (input_grad, gain_grad)


def rotary_tables(segments, head_dim):
    row_index = jnp.arange(segments.shape[1], dtype=jnp.int32)[None, :]
    earlier = jnp.sum((segments[:, None, :] < segments[:, :, None]).astype(jnp.int32), axis=2)
    prompt_rows = jnp.sum((segments == 0).astype(jnp.int32), axis=1, keepdims=True)
    position = row_index - earlier + jnp.where(segments > 0, prompt_rows, 0)
    frequency = 10000.0 ** (-(jnp.arange(head_dim // 2, dtype=F32) * 2.0) / head_dim)
    angles = position.astype(F32)[:, :, None] * frequency[None, None, :]
    return (jnp.cos(angles)[:, :, None, :], jnp.sin(angles)[:, :, None, :])


def rotate(values, cosine_table, sine_table):
    half_dim = values.shape[-1] // 2
    first_half = values[..., :half_dim]
    second_half = values[..., half_dim:]
    return jnp.concatenate(
        [
            first_half * cosine_table - second_half * sine_table,
            second_half * cosine_table + first_half * sine_table,
        ],
        axis=-1,
    )


def attend_mask(segments):
    row_index = jnp.arange(segments.shape[1], dtype=jnp.int32)
    causal = (row_index[None, :] <= row_index[:, None])[None]
    same_doc = (segments[:, None, :] == 0) | (segments[:, None, :] == segments[:, :, None])
    return causal & same_doc


def tp_gather(own):
    count = lax.axis_size("tp")
    rank = lax.axis_index("tp")
    micro, rows, width = own.shape
    full = jnp.zeros((micro, count * rows, width), own.dtype)
    pieces = [own] + [
        lax.ppermute(own, "tp", [(i, (i + k) % count) for i in range(count)])
        for k in range(1, count)
    ]
    for k, piece in enumerate(pieces):
        place = lax.rem(rank - k + count, count) * rows
        full = lax.dynamic_update_slice_in_dim(full, piece, place, 1)
    return full


def tp_scatter(part):
    count = lax.axis_size("tp")
    rank = lax.axis_index("tp")
    rows = part.shape[1] // count
    total = lax.dynamic_slice_in_dim(part, rank * rows, rows, 1).astype(F32)
    for k in range(1, count):
        place = lax.rem(rank + k, count) * rows
        piece = lax.dynamic_slice_in_dim(part, place, rows, 1)
        got = lax.ppermute(piece, "tp", [(i, (i + k) % count) for i in range(count)])
        total = total + got.astype(F32)
    return total


def dot(spec, a, b):
    return jnp.einsum(spec, a, b, preferred_element_type=F32)


def per_device(
    tokens_in,
    out_grad,
    segment_ids,
    expert_ids,
    attn_gain,
    w_query,
    w_key,
    w_value,
    w_output,
    ffn_gain,
    w_router,
    w_gate,
    w_up,
    w_down,
):
    tensor_count = lax.axis_size("tp")
    tensor_rank = lax.axis_index("tp")
    micro, own_rows, width = tokens_in.shape
    group_rows = own_rows * tensor_count
    experts = w_gate.shape[0]
    units = w_gate.shape[2]
    head_width = w_query.shape[1]
    heads = head_width // HD
    query_scale = 1.0 / math.sqrt(HD)
    rows = micro * group_rows
    slots = micro * CAP

    own_small = jnp.concatenate([attn_gain[:, None], ffn_gain[:, None], w_router], axis=1)
    small_rows, small_width = own_small.shape
    shard_rows = w_query.shape[0]
    own_small = jnp.pad(own_small, ((0, shard_rows - small_rows), (0, HD - small_width)))
    attn_set = lax.all_gather(
        jnp.concatenate([w_query, w_key, w_value, w_output.T, own_small], axis=1),
        "fsdp",
        axis=0,
        tiled=True,
    )
    span = 3 * units
    pair_sets = []
    for pair in range(experts // PAIR):
        held = []
        for e in range(pair * PAIR, (pair + 1) * PAIR):
            held += [w_gate[e], w_up[e], w_down[e].T]
        pair_sets.append(lax.all_gather(jnp.concatenate(held, axis=1), "fsdp", axis=0, tiled=True))
    small = attn_set[:, 4 * head_width :].reshape(-1, shard_rows, HD)[:, :small_rows]
    small = tp_gather(small).reshape(width, HD)
    gain_one = small[:, 0].astype(F32)
    gain_two = small[:, 1].astype(F32)
    router = small[:, 2:small_width]

    tokens_full = tp_gather(tokens_in).astype(F32)
    hidden_one = (tokens_full * inverse_rms(tokens_full) * gain_one).astype(BF16)
    hidden_one = hidden_one.reshape(rows, width)
    cosine_table, sine_table = rotary_tables(segment_ids, HD)
    allowed = attend_mask(segment_ids)
    qkv = dot("td,de->te", hidden_one, attn_set[:, : 3 * head_width])
    four = (micro, group_rows, heads, HD)
    query_raw = qkv[:, :head_width].reshape(four)
    key_raw = qkv[:, head_width : 2 * head_width].reshape(four)
    values_low = qkv[:, 2 * head_width :].reshape(four).astype(BF16)
    query_rot = (rotate(query_raw, cosine_table, sine_table) * query_scale).astype(BF16)
    keys_rot = rotate(key_raw, cosine_table, sine_table).astype(BF16)
    scores = dot("mqhd,mkhd->mhqk", query_rot, keys_rot)
    scores = jnp.where(allowed[:, None], scores, MASKED)
    exps = jnp.exp(scores - jnp.max(scores, axis=-1, keepdims=True))
    probs = exps / jnp.sum(exps, axis=-1, keepdims=True)
    probs_low = probs.astype(BF16)
    context = dot("mhqk,mkhd->mqhd", probs_low, values_low).reshape(rows, head_width).astype(BF16)
    attn_part = dot("te,de->td", context, attn_set[:, 3 * head_width : 4 * head_width]).astype(BF16)
    inputs = tokens_in.astype(F32)
    middle = inputs + tp_scatter(attn_part.reshape(micro, group_rows, width))
    normed_two = (middle * inverse_rms(middle) * gain_two).astype(BF16)
    hidden_two = tp_gather(normed_two)
    grad_full = tp_gather(out_grad)

    logits = dot("mtd,de->mte", hidden_two, router)
    named = jnp.any(
        expert_ids[:, :, :, None] == jnp.arange(experts, dtype=jnp.int32), axis=2
    )
    chosen = jnp.where(named, logits, MASKED)
    chosen_exp = jnp.where(named, jnp.exp(chosen - jnp.max(chosen, axis=-1, keepdims=True)), 0.0)
    gates = chosen_exp / jnp.sum(chosen_exp, axis=-1, keepdims=True)
    row_index = jnp.arange(group_rows, dtype=jnp.int32)
    before = (row_index[None, :] < row_index[:, None]).astype(BF16)
    slot_of = dot("ts,mse->met", before, named.astype(BF16)).astype(jnp.int32)
    slot_of = jnp.where(jnp.swapaxes(named, 1, 2), slot_of, -1)
    picks = slot_of[:, :, None, :] == jnp.arange(CAP, dtype=jnp.int32)[None, None, :, None]
    slot_gates = jnp.sum(
        jnp.where(picks, jnp.swapaxes(gates, 1, 2)[:, :, None, :], 0.0), axis=-1, keepdims=True
    )
    picks_low = picks.astype(BF16)

    weighted_outs = []
    gate_grad_slots = []
    routed_grads = []
    pair_grads = []
    pieces = []
    for e in range(experts):
        weights = pair_sets[e // PAIR]
        start = e % PAIR * span
        gate_up = weights[:, start : start + 2 * units]
        down = weights[:, start + 2 * units : start + span]
        pick = picks_low[:, e]
        if e and e % PAIR == 0:
            pick, packed = lax.optimization_barrier((pick, jnp.concatenate(pieces, axis=1)))
            pair_grads.append(lax.psum_scatter(packed, "fsdp", scatter_dimension=0, tiled=True))
            pieces = []
        routed = dot("mst,mtd->msd", pick, hidden_two).astype(BF16).reshape(slots, width)
        grad_slot = dot("mst,mtd->msd", pick, grad_full)
        slot_gate = slot_gates[:, e]
        slot_grad = (slot_gate * grad_slot).astype(BF16).reshape(slots, width)
        pre = dot("sd,df->sf", routed, gate_up)
        gate_pre = pre[:, :units]
        up_pre = pre[:, units:]
        gate_sigmoid = jax.nn.sigmoid(gate_pre)
        silu = gate_pre * gate_sigmoid
        activated = (silu * up_pre).astype(BF16)
        expert_out = dot("sf,df->sd", activated, down).reshape(micro, CAP, width)
        weighted_outs.append((slot_gate * expert_out).astype(BF16))
        gate_grad_slots.append(jnp.sum(expert_out * grad_slot, axis=-1))
        act_grad = dot("sd,df->sf", slot_grad, down)
        pre_grad = jnp.concatenate(
            [
                (act_grad * up_pre * gate_sigmoid * (1.0 + gate_pre * (1.0 - gate_sigmoid))).astype(
                    BF16
                ),
                (act_grad * silu).astype(BF16),
            ],
            axis=1,
        )
        pieces.append(dot("sd,sf->df", routed, pre_grad).astype(BF16))
        pieces.append(dot("sd,sf->df", slot_grad, activated).astype(BF16))
        routed_grads.append(
            dot("sf,df->sd", pre_grad, gate_up).astype(BF16).reshape(micro, CAP, width)
        )
    picks_low, packed = lax.optimization_barrier((picks_low, jnp.concatenate(pieces, axis=1)))
    pair_grads.append(lax.psum_scatter(packed, "fsdp", scatter_dimension=0, tiled=True))
    flat_picks = picks_low.reshape(micro, experts * CAP, group_rows)
    token_grad = dot("mst,msd->mtd", flat_picks, jnp.concatenate(routed_grads, axis=1))
    gate_grad_part = jnp.sum(
        jnp.where(picks, jnp.stack(gate_grad_slots, axis=1)[:, :, :, None], 0.0), axis=2
    )
    gate_grad_part = jnp.pad(jnp.swapaxes(gate_grad_part, 1, 2), ((0, 0), (0, 0), (0, HD - experts)))
    summed = tp_scatter(jnp.concatenate([token_grad, gate_grad_part], axis=-1).astype(BF16))
    moe_part = dot("mst,msd->mtd", flat_picks, jnp.concatenate(weighted_outs, axis=1))
    output = (middle + tp_scatter(moe_part.astype(BF16))).astype(BF16)

    gates_own = lax.dynamic_slice_in_dim(gates, tensor_rank * own_rows, own_rows, 1)
    gate_grad = summed[:, :, width : width + experts]
    logit_grad = gates_own * (
        gate_grad - jnp.sum(gates_own * gate_grad, axis=-1, keepdims=True)
    )
    router_grad = jnp.einsum(
        "mtd,mte->de", normed_two.astype(F32), logit_grad, precision=HIGHEST
    )
    hidden_two_grad = summed[:, :, :width] + jnp.einsum(
        "mte,de->mtd", logit_grad, router.astype(F32), precision=HIGHEST
    )
    middle_norm_grad, gain_two_grad = norm_backward(middle, gain_two, hidden_two_grad)
    middle_grad = middle_norm_grad + out_grad.astype(F32)

    attn_grad = tp_gather(middle_grad.astype(BF16)).reshape(rows, width)
    context_grad = dot("td,de->te", attn_grad, attn_set[:, 3 * head_width : 4 * head_width])
    context_grad = context_grad.astype(BF16).reshape(four)
    prob_grad = dot("mqhd,mkhd->mhqk", context_grad, values_low)
    row_delta = jnp.sum(probs * prob_grad, axis=-1, keepdims=True)
    score_grad = (probs * (prob_grad - row_delta)).astype(BF16)
    query_grad = rotate(
        dot("mhqk,mkhd->mqhd", score_grad, keys_rot) * query_scale, cosine_table, -sine_table
    )
    key_grad = rotate(dot("mhqk,mqhd->mkhd", score_grad, query_rot), cosine_table, -sine_table)
    value_grad = dot("mhqk,mqhd->mkhd", probs_low, context_grad)
    qkv_grad = jnp.concatenate(
        [item.astype(BF16).reshape(rows, head_width) for item in (query_grad, key_grad, value_grad)],
        axis=1,
    )
    hidden_part = dot("te,de->td", qkv_grad, attn_set[:, : 3 * head_width]).astype(BF16)
    hidden_one_grad = tp_scatter(hidden_part.reshape(micro, group_rows, width))
    inner_grad, gain_one_grad = norm_backward(inputs, gain_one, hidden_one_grad)
    input_grad = (middle_grad + inner_grad).astype(BF16)
    small_part = jnp.concatenate(
        [gain_one_grad[:, None], gain_two_grad[:, None], router_grad], axis=1
    )
    attn_packed = jnp.concatenate(
        [
            dot("td,te->de", hidden_one, qkv_grad).astype(BF16),
            dot("td,te->de", attn_grad, context).astype(BF16),
            jnp.pad(small_part, ((0, 0), (0, HD - small_width))).astype(BF16),
        ],
        axis=1,
    )
    attn_packed, pair_grads = lax.optimization_barrier((attn_packed, pair_grads))
    attn_grads = lax.psum_scatter(attn_packed, "fsdp", scatter_dimension=0, tiled=True)
    small_grads = tp_scatter(attn_grads[None, :, 4 * head_width :])[0]
    attn_grads = attn_grads.astype(F32)
    expert_grads = [
        item[:, e * span : (e + 1) * span] for item in pair_grads for e in range(PAIR)
    ]
    return (
        output,
        input_grad,
        small_grads[:, 0],
        attn_grads[:, :head_width],
        attn_grads[:, head_width : 2 * head_width],
        attn_grads[:, 2 * head_width : 3 * head_width],
        attn_grads[:, 3 * head_width : 4 * head_width].T,
        small_grads[:, 1],
        small_grads[:, 2:small_width],
        jnp.stack([item[:, :units] for item in expert_grads]).astype(F32),
        jnp.stack([item[:, units : 2 * units] for item in expert_grads]).astype(F32),
        jnp.stack([item[:, 2 * units :].T for item in expert_grads]).astype(F32),
    )


def solution(mesh):
    return jax.shard_map(
        per_device,
        mesh=mesh,
        in_specs=(
            P(None, ("fsdp", "tp"), None),
            P(None, ("fsdp", "tp"), None),
            P(None, "fsdp"),
            P(None, "fsdp", None),
            P(("fsdp", "tp")),
            P("fsdp", "tp"),
            P("fsdp", "tp"),
            P("fsdp", "tp"),
            P("tp", "fsdp"),
            P(("fsdp", "tp")),
            P(("fsdp", "tp"), None),
            P(None, "fsdp", "tp"),
            P(None, "fsdp", "tp"),
            P(None, "tp", "fsdp"),
        ),
        out_specs=(
            P(None, ("fsdp", "tp"), None),
            P(None, ("fsdp", "tp"), None),
            P(("fsdp", "tp")),
            P("fsdp", "tp"),
            P("fsdp", "tp"),
            P("fsdp", "tp"),
            P("tp", "fsdp"),
            P(("fsdp", "tp")),
            P(("fsdp", "tp"), None),
            P(None, "fsdp", "tp"),
            P(None, "fsdp", "tp"),
            P(None, "tp", "fsdp"),
        ),
        check_vma=False,
    )
```

profile of v0, /device:TPU:0, one launch (start us, length us, event | category | flops | bytes accessed | tf_op | source)
XLA Modules:
  0.0 1036.4 jit_solution(9366301624663593010)
XLA Ops:
  60.3 35.0 %collective-permute-done = bf16[2,80,2048]{2,1,0:T(8,128)(2,1)} collective-permute-done((bf16[2,80,2048]{2,1,0:T(8,128)(2,1)S(1)}, bf16[2,80,2048]{2,1,0:T(8,128)(2,1)}, u32[]{:S(2)}, u32[]{:S(2)}) %collective-permute-start) | collective-permute-done | bytes 655392 | tf_op jit(solution)/shard_map/ppermute | solution.py:69
  96.4 52.8 %collective-permute-done.1 = bf16[2,80,2048]{2,1,0:T(8,128)(2,1)} collective-permute-done((bf16[2,80,2048]{2,1,0:T(8,128)(2,1)S(1)}, bf16[2,80,2048]{2,1,0:T(8,128)(2,1)}, u32[]{:S(2)}, u32[]{:S(2)}) %collective-permute-start.1) | collective-permute-done | bytes 655392 | tf_op jit(solution)/shard_map/ppermute | solution.py:69
  165.6 10.2 collective-permute-done.3
  175.8 21.8 %dynamic_update_slice.65 = bf16[8,256,128]{1,0,2:T(8,128)(2,1)} dynamic-update-slice(bf16[8,256,128]{1,0,2:T(8,128)(2,1)} %dynamic_update_slice.64, bf16[8,64,128]{1,0,2:T(8,128)(2,1)} %collective-permute-done.3, s32[]{:T(128)} %constant.60.clone.1, s32[]{:T(128)S(6)} %select_n.99, s32[]{:T(128)} %constant.60.clone.1) | dynamic-update-slice | bytes 262148 | tf_op jit(solution)/shard_map/dynamic_update_slice | solution.py:74
  202.4 22.4 %dynamic_update_slice.67 = bf16[8,256,128]{1,0,2:T(8,128)(2,1)} dynamic-update-slice(bf16[8,256,128]{1,0,2:T(8,128)(2,1)} %dynamic_update_slice.66, bf16[8,64,128]{1,0,2:T(8,128)(2,1)} %collective-permute-done.5, s32[]{:T(128)} %constant.60.clone.1, s32[]{:T(128)S(6)} %select_n.101, s32[]{:T(128)} %constant.60.clone.1) | dynamic-update-slice | bytes 262148 | tf_op jit(solution)/shard_map/dynamic_update_slice | solution.py:74
  228.1 7.5 fusion.36
  262.6 7.2 collective-permute-start.7
  278.2 18.9 %collective-permute-start.14 = (bf16[2,80,2048]{2,1,0:T(8,128)(2,1)}, bf16[2,80,2048]{2,1,0:T(8,128)(2,1)S(1)}, u32[]{:S(2)}, u32[]{:S(2)}) collective-permute-start(bf16[2,80,2048]{2,1,0:T(8,128)(2,1)} %param.15), channel_id=1, source_target_pairs={{0,3},{1,0},{2,1},{3,2},{4,7},{5,4},{6,5},{7,6},{8,11},{9,8},{10,9... | collective-permute-start | bytes 1966088 | tf_op jit(solution)/shard_map/ppermute | solution.py:69
  297.1 21.7 %collective-permute-done.7 = bf16[2,80,2048]{2,1,0:T(8,128)(2,1)S(1)} collective-permute-done((bf16[2,80,2048]{2,1,0:T(8,128)(2,1)S(1)}, bf16[2,80,2048]{2,1,0:T(8,128)(2,1)S(1)}, u32[]{:S(2)}, u32[]{:S(2)}) %collective-permute-start.7) | collective-permute-done | bytes 655392 | tf_op jit(solution)/shard_map/ppermute | solution.py:86
  321.2 18.9 %collective-permute-start.9 = (bf16[2,80,2048]{2,1,0:T(8,128)(2,1)S(1)}, bf16[2,80,2048]{2,1,0:T(8,128)(2,1)S(1)}, u32[]{:S(2)}, u32[]{:S(2)}) collective-permute-start(bf16[2,80,2048]{2,1,0:T(8,128)(2,1)S(1)} %get-tuple-element.98), channel_id=1, source_target_pairs={{0,1},{1,2},{2,3},{3,0},{4,5},{5,6},{6,7},{7,4},{8,9},{9,10},{10,1... | collective-permute-start | bytes 1966088 | tf_op jit(solution)/shard_map/ppermute | solution.py:69
  346.4 12.2 %collective-permute-done.9 = bf16[2,80,2048]{2,1,0:T(8,128)(2,1)S(1)} collective-permute-done((bf16[2,80,2048]{2,1,0:T(8,128)(2,1)S(1)}, bf16[2,80,2048]{2,1,0:T(8,128)(2,1)S(1)}, u32[]{:S(2)}, u32[]{:S(2)}) %collective-permute-start.9) | collective-permute-done | bytes 655392 | tf_op jit(solution)/shard_map/ppermute | solution.py:69
  358.6 25.3 %collective-permute-done.10 = bf16[2,80,2048]{2,1,0:T(8,128)(2,1)S(1)} collective-permute-done((bf16[2,80,2048]{2,1,0:T(8,128)(2,1)S(1)}, bf16[2,80,2048]{2,1,0:T(8,128)(2,1)S(1)}, u32[]{:S(2)}, u32[]{:S(2)}) %collective-permute-start.10) | collective-permute-done | bytes 655392 | tf_op jit(solution)/shard_map/ppermute | solution.py:69
  402.2 8.7 fusion.11
  410.9 6.1 multiply_convert_fusion.17
  417.1 5.7 convolution_convert_fusion.7
  422.7 8.8 fusion.15
  431.6 6.1 multiply_convert_fusion.20
  443.0 8.9 convolution_convert_fusion.3
  451.9 8.9 convolution_convert_fusion.2
  460.8 23.8 %pad_maximum_fusion = bf16[2048,8448]{1,0:T(8,128)(2,1)} fusion(bf16[2048,1408]{1,0:T(8,128)(2,1)} %convolution_convert_fusion.7, bf16[2048,2816]{1,0:T(8,128)(2,1)} %convolution_convert_fusion.2, bf16[2048,1408]{1,0:T(8,128)(2,1)} %convolution_convert_fusion.8, bf16[2048,2816]{1,0:T(8,128)(2,1)} %convolution_convert_fusion.3), kind=kLoop, calls=%fused_computation.1 | loop fusion | flops 138412032 | bytes 69206016 | tf_op jit(solution)/shard_map/concatenate | solution.py:200
  494.6 9.1 fusion.3
  503.8 8.3 multiply_convert_fusion.11
  517.4 9.6 fusion.7
  526.9 7.2 multiply_convert_fusion.14
  534.2 5.5 convolution_convert_fusion.6
  539.7 8.9 convolution_convert_fusion.1
  548.6 8.9 convolution_convert_fusion
  557.6 24.5 %pad_maximum_fusion.1 = bf16[2048,8448]{1,0:T(8,128)(2,1)} fusion(bf16[2048,1408]{1,0:T(8,128)(2,1)} %convolution_convert_fusion.5, bf16[2048,2816]{1,0:T(8,128)(2,1)} %convolution_convert_fusion, bf16[2048,1408]{1,0:T(8,128)(2,1)} %convolution_convert_fusion.6, bf16[2048,2816]{1,0:T(8,128)(2,1)} %convolution_convert_fusion.1), kind=kLoop, calls=%fused_computation.2 | loop fusion | flops 138412032 | bytes 69206016 | tf_op jit(solution)/shard_map/concatenate | solution.py:231
  611.7 10.0 fusion.78
  621.7 9.7 fusion.72
  631.5 9.7 fusion.69
  641.3 9.8 fusion.75
  657.6 15.8 %collective-permute-start.18 = (bf16[2,80,2176]{2,1,0:T(8,128)(2,1)}, bf16[2,80,2176]{2,1,0:T(8,128)(2,1)}, u32[]{:S(2)}, u32[]{:S(2)}) collective-permute-start(bf16[2,80,2176]{2,1,0:T(8,128)(2,1)} %get-tuple-element.153), channel_id=1, source_target_pairs={{0,1},{1,2},{2,3},{3,0},{4,5},{5,6},{6,7},{7,4},{8,9},{9,10},{10,1... | collective-permute-start | bytes 2088968 | tf_op jit(solution)/shard_map/ppermute | solution.py:86
  676.6 13.3 %collective-permute-done.18 = bf16[2,80,2176]{2,1,0:T(8,128)(2,1)} collective-permute-done((bf16[2,80,2176]{2,1,0:T(8,128)(2,1)}, bf16[2,80,2176]{2,1,0:T(8,128)(2,1)}, u32[]{:S(2)}, u32[]{:S(2)}) %collective-permute-start.18) | collective-permute-done | bytes 696352 | tf_op jit(solution)/shard_map/ppermute | solution.py:86
  689.9 14.7 %collective-permute-done.20 = bf16[2,80,2176]{2,1,0:T(8,128)(2,1)} collective-permute-done((bf16[2,80,2176]{2,1,0:T(8,128)(2,1)S(1)}, bf16[2,80,2176]{2,1,0:T(8,128)(2,1)}, u32[]{:S(2)}, u32[]{:S(2)}) %collective-permute-start.20) | collective-permute-done | bytes 696352 | tf_op jit(solution)/shard_map/ppermute | solution.py:86
  704.6 27.0 %collective-permute-done.19 = bf16[2,80,2176]{2,1,0:T(8,128)(2,1)} collective-permute-done((bf16[2,80,2176]{2,1,0:T(8,128)(2,1)S(1)}, bf16[2,80,2176]{2,1,0:T(8,128)(2,1)}, u32[]{:S(2)}, u32[]{:S(2)}) %collective-permute-start.19) | collective-permute-done | bytes 696352 | tf_op jit(solution)/shard_map/ppermute | solution.py:86
  744.5 14.6 %collective-permute-done.21 = bf16[2,80,2048]{2,1,0:T(8,128)(2,1)S(1)} collective-permute-done((bf16[2,80,2048]{2,1,0:T(8,128)(2,1)S(1)}, bf16[2,80,2048]{2,1,0:T(8,128)(2,1)S(1)}, u32[]{:S(2)}, u32[]{:S(2)}) %collective-permute-start.21) | collective-permute-done | bytes 655392 | tf_op jit(solution)/shard_map/ppermute | solution.py:69
  759.2 26.6 %collective-permute-done.22 = bf16[2,80,2048]{2,1,0:T(8,128)(2,1)S(1)} collective-permute-done((bf16[2,80,2048]{2,1,0:T(8,128)(2,1)S(1)}, bf16[2,80,2048]{2,1,0:T(8,128)(2,1)S(1)}, u32[]{:S(2)}, u32[]{:S(2)}) %collective-permute-start.22) | collective-permute-done | bytes 655392 | tf_op jit(solution)/shard_map/ppermute | solution.py:69
  810.4 14.3 %collective-permute-start.24 = (bf16[2,80,2048]{2,1,0:T(8,128)(2,1)S(1)}, bf16[2,80,2048]{2,1,0:T(8,128)(2,1)S(1)}, u32[]{:S(2)}, u32[]{:S(2)}) collective-permute-start(bf16[2,80,2048]{2,1,0:T(8,128)(2,1)S(1)} %get-tuple-element.156), channel_id=1, source_target_pairs={{0,1},{1,2},{2,3},{3,0},{4,5},{5,6},{6,7},{7,4},{8,9},{9,10},{10,1... | collective-permute-start | bytes 1966088 | tf_op jit(solution)/shard_map/ppermute | solution.py:86
  828.1 5.7 convolution_convert_fusion.4
  833.8 5.9 collective-permute-done.24
  839.8 14.1 %collective-permute-done.26 = bf16[2,80,2048]{2,1,0:T(8,128)(2,1)S(1)} collective-permute-done((bf16[2,80,2048]{2,1,0:T(8,128)(2,1)S(1)}, bf16[2,80,2048]{2,1,0:T(8,128)(2,1)S(1)}, u32[]{:S(2)}, u32[]{:S(2)}) %collective-permute-start.26) | collective-permute-done | bytes 655392 | tf_op jit(solution)/shard_map/ppermute | solution.py:86
  853.9 25.6 %collective-permute-done.25 = bf16[2,80,2048]{2,1,0:T(8,128)(2,1)S(1)} collective-permute-done((bf16[2,80,2048]{2,1,0:T(8,128)(2,1)S(1)}, bf16[2,80,2048]{2,1,0:T(8,128)(2,1)S(1)}, u32[]{:S(2)}, u32[]{:S(2)}) %collective-permute-start.25) | collective-permute-done | bytes 655392 | tf_op jit(solution)/shard_map/ppermute | solution.py:86
  885.4 36.1 %reduce-scatter.6.cloned.1.call-done = bf16[256,8448]{1,0:T(8,128)(2,1)} async-done(((bf16[2048,8448]{1,0:T(8,128)(2,1)}), bf16[256,8448]{1,0:T(8,128)(2,1)}) %reduce-scatter.6.cloned.1.call-update) | async-done | bytes 4325392 | tf_op jit(solution)/shard_map/reduce_scatter | solution.py:232
  934.2 15.3 %collective-permute-done.15 = bf16[2,80,2048]{2,1,0:T(8,128)(2,1)} collective-permute-done((bf16[2,80,2048]{2,1,0:T(8,128)(2,1)}, bf16[2,80,2048]{2,1,0:T(8,128)(2,1)}, u32[]{:S(2)}, u32[]{:S(2)}) %collective-permute-start.15) | collective-permute-done | bytes 655392 | tf_op jit(solution)/shard_map/ppermute | solution.py:86
  949.6 12.1 %collective-permute-done.17 = bf16[2,80,2048]{2,1,0:T(8,128)(2,1)} collective-permute-done((bf16[2,80,2048]{2,1,0:T(8,128)(2,1)}, bf16[2,80,2048]{2,1,0:T(8,128)(2,1)}, u32[]{:S(2)}, u32[]{:S(2)}) %collective-permute-start.17) | collective-permute-done | bytes 655392 | tf_op jit(solution)/shard_map/ppermute | solution.py:86
  961.7 28.7 %collective-permute-done.16 = bf16[2,80,2048]{2,1,0:T(8,128)(2,1)} collective-permute-done((bf16[2,80,2048]{2,1,0:T(8,128)(2,1)}, bf16[2,80,2048]{2,1,0:T(8,128)(2,1)}, u32[]{:S(2)}, u32[]{:S(2)}) %collective-permute-start.16) | collective-permute-done | bytes 655392 | tf_op jit(solution)/shard_map/ppermute | solution.py:86
  1004.3 6.2 copy.339
  (449 shorter events, 292.1 us)
Async XLA Ops:
  7.2 145.8 %all-gather.4.cloned.1.call-start = ((), (), s32[]{:S(2)}) async-start(), calls=%async_computation.3 | async-start | bytes 10027008 | tf_op jit(solution)/shard_map/all_gather | solution.py:127
  16.8 385.3 %all-gather.6.cloned.1.call-start = ((), (), s32[]{:S(2)}) async-start(), calls=%async_computation.4 | async-start | bytes 38928384 | tf_op jit(solution)/shard_map/all_gather | solution.py:139
  44.9 449.8 %all-gather.8.cloned.1.call-start = ((), (), s32[]{:S(2)}) async-start(), calls=%async_computation.5 | async-start | bytes 38928384 | tf_op jit(solution)/shard_map/all_gather | solution.py:139
  45.6 839.8 %reduce-scatter.4.cloned.1.call-start = ((), (), s32[]{:S(2)}) async-start(), calls=%async_computation.6 | async-start | bytes 38928384 | tf_op jit(solution)/shard_map/reduce_scatter | solution.py:201
  45.6 299.0 %collective-permute-start.13 = (bf16[2,80,2048]{2,1,0:T(8,128)(2,1)}, bf16[2,80,2048]{2,1,0:T(8,128)(2,1)}, u32[]{:S(2)}, u32[]{:S(2)}) collective-permute-start(bf16[2,80,2048]{2,1,0:T(8,128)(2,1)} %param.15), channel_id=1, source_target_pairs={{0,2},{1,3},{2,0},{3,1},{4,6},{5,7},{6,4},{7,5},{8,10},{9,11},{10,... | collective-permute-start | bytes 1966088 | tf_op jit(solution)/shard_map/ppermute | solution.py:69
  49.8 290.2 %collective-permute-start.12 = (bf16[2,80,2048]{2,1,0:T(8,128)(2,1)}, bf16[2,80,2048]{2,1,0:T(8,128)(2,1)}, u32[]{:S(2)}, u32[]{:S(2)}) collective-permute-start(bf16[2,80,2048]{2,1,0:T(8,128)(2,1)} %param.15), channel_id=1, source_target_pairs={{0,1},{1,2},{2,3},{3,0},{4,5},{5,6},{6,7},{7,4},{8,9},{9,10},{10,1... | collective-permute-start | bytes 1966088 | tf_op jit(solution)/shard_map/ppermute | solution.py:69
  51.4 43.9 %collective-permute-start = (bf16[2,80,2048]{2,1,0:T(8,128)(2,1)S(1)}, bf16[2,80,2048]{2,1,0:T(8,128)(2,1)}, u32[]{:S(2)}, u32[]{:S(2)}) collective-permute-start(bf16[2,80,2048]{2,1,0:T(8,128)(2,1)S(1)} %copy-done.9), channel_id=1, source_target_pairs={{0,1},{1,2},{2,3},{3,0},{4,5},{5,6},{6,7},{7,4},{8,9},{9,10},{10,1... | collective-permute-start | bytes 1966088 | tf_op jit(solution)/shard_map/ppermute | solution.py:69
  51.4 99.1 %collective-permute-start.2 = (bf16[2,80,2048]{2,1,0:T(8,128)(2,1)S(1)}, bf16[2,80,2048]{2,1,0:T(8,128)(2,1)}, u32[]{:S(2)}, u32[]{:S(2)}) collective-permute-start(bf16[2,80,2048]{2,1,0:T(8,128)(2,1)S(1)} %copy-done.9), channel_id=1, source_target_pairs={{0,3},{1,0},{2,1},{3,2},{4,7},{5,4},{6,5},{7,6},{8,11},{9,8},{10,9... | collective-permute-start | bytes 1966088 | tf_op jit(solution)/shard_map/ppermute | solution.py:69
  55.2 94.0 %collective-permute-start.1 = (bf16[2,80,2048]{2,1,0:T(8,128)(2,1)S(1)}, bf16[2,80,2048]{2,1,0:T(8,128)(2,1)}, u32[]{:S(2)}, u32[]{:S(2)}) collective-permute-start(bf16[2,80,2048]{2,1,0:T(8,128)(2,1)S(1)} %copy-done.9), channel_id=1, source_target_pairs={{0,2},{1,3},{2,0},{3,1},{4,6},{5,7},{6,4},{7,5},{8,10},{9,11},{10,... | collective-permute-start | bytes 1966088 | tf_op jit(solution)/shard_map/ppermute | solution.py:69
  58.8 332.1 %copy-start.64 = (s32[2,4,320]{2,0,1:T(2,128)}, s32[2,4,320]{2,0,1:T(2,128)S(1)}, u32[]{:S(2)}) copy-start(s32[2,4,320]{2,0,1:T(2,128)S(1)} %copy.302) | copy-start | bytes 30724
  154.3 48.1 %collective-permute-start.5 = (bf16[8,64,128]{1,0,2:T(8,128)(2,1)S(1)}, bf16[8,64,128]{1,0,2:T(8,128)(2,1)}, u32[]{:S(2)}, u32[]{:S(2)}) collective-permute-start(bf16[8,64,128]{1,0,2:T(8,128)(2,1)S(1)} %slice.324), channel_id=1, source_target_pairs={{0,3},{1,0},{2,1},{3,2},{4,7},{5,4},{6,5},{7,6},{8,11},{9,8},{10,9... | collective-permute-start | bytes 393224 | tf_op jit(solution)/shard_map/ppermute | solution.py:69
  157.9 39.7 %collective-permute-start.4 = (bf16[8,64,128]{1,0,2:T(8,128)(2,1)S(1)}, bf16[8,64,128]{1,0,2:T(8,128)(2,1)}, u32[]{:S(2)}, u32[]{:S(2)}) collective-permute-start(bf16[8,64,128]{1,0,2:T(8,128)(2,1)S(1)} %slice.324), channel_id=1, source_target_pairs={{0,2},{1,3},{2,0},{3,1},{4,6},{5,7},{6,4},{7,5},{8,10},{9,11},{10,... | collective-permute-start | bytes 393224 | tf_op jit(solution)/shard_map/ppermute | solution.py:69
  157.9 17.9 %collective-permute-start.3 = (bf16[8,64,128]{1,0,2:T(8,128)(2,1)S(1)}, bf16[8,64,128]{1,0,2:T(8,128)(2,1)}, u32[]{:S(2)}, u32[]{:S(2)}) collective-permute-start(bf16[8,64,128]{1,0,2:T(8,128)(2,1)S(1)} %slice.324), channel_id=1, source_target_pairs={{0,1},{1,2},{2,3},{3,0},{4,5},{5,6},{6,7},{7,4},{8,9},{9,10},{10,1... | collective-permute-start | bytes 393224 | tf_op jit(solution)/shard_map/ppermute | solution.py:69
  226.0 94.9 %copy-start.62 = (f32[2048,1]{0,1:T(1,128)}, f32[2048,1]{0,1:T(1,128)S(1)}, u32[]{:S(2)}) copy-start(f32[2048,1]{0,1:T(1,128)S(1)} %get-tuple-element.183) | copy-start | bytes 24580
  258.7 19.5 %collective-permute-start.6 = (bf16[2,80,2048]{2,1,0:T(8,128)(2,1)S(1)}, bf16[2,80,2048]{2,1,0:T(8,128)(2,1)S(1)}, u32[]{:S(2)}, u32[]{:S(2)}) collective-permute-start(bf16[2,80,2048]{2,1,0:T(8,128)(2,1)S(1)} %get-tuple-element.162), channel_id=1, source_target_pairs={{0,1},{1,2},{2,3},{3,0},{4,5},{5,6},{6,7},{7,4},{8,9},{9,10},{10,1... | collective-permute-start | bytes 1966088 | tf_op jit(solution)/shard_map/ppermute | solution.py:86
  258.8 38.3 %collective-permute-start.8 = (bf16[2,80,2048]{2,1,0:T(8,128)(2,1)S(1)}, bf16[2,80,2048]{2,1,0:T(8,128)(2,1)S(1)}, u32[]{:S(2)}, u32[]{:S(2)}) collective-permute-start(bf16[2,80,2048]{2,1,0:T(8,128)(2,1)S(1)} %get-tuple-element.163), channel_id=1, source_target_pairs={{0,3},{1,0},{2,1},{3,2},{4,7},{5,4},{6,5},{7,6},{8,11},{9,8},{10,9... | collective-permute-start | bytes 1966088 | tf_op jit(solution)/shard_map/ppermute | solution.py:86
  262.6 56.2 %collective-permute-start.7 = (bf16[2,80,2048]{2,1,0:T(8,128)(2,1)S(1)}, bf16[2,80,2048]{2,1,0:T(8,128)(2,1)S(1)}, u32[]{:S(2)}, u32[]{:S(2)}) collective-permute-start(bf16[2,80,2048]{2,1,0:T(8,128)(2,1)S(1)} %get-tuple-element.164), channel_id=1, source_target_pairs={{0,2},{1,3},{2,0},{3,1},{4,6},{5,7},{6,4},{7,5},{8,10},{9,11},{10,... | collective-permute-start | bytes 1966088 | tf_op jit(solution)/shard_map/ppermute | solution.py:86
  278.2 68.1 %collective-permute-start.14 = (bf16[2,80,2048]{2,1,0:T(8,128)(2,1)}, bf16[2,80,2048]{2,1,0:T(8,128)(2,1)S(1)}, u32[]{:S(2)}, u32[]{:S(2)}) collective-permute-start(bf16[2,80,2048]{2,1,0:T(8,128)(2,1)} %param.15), channel_id=1, source_target_pairs={{0,3},{1,0},{2,1},{3,2},{4,7},{5,4},{6,5},{7,6},{8,11},{9,8},{10,9... | collective-permute-start | bytes 1966088 | tf_op jit(solution)/shard_map/ppermute | solution.py:69
  321.1 37.5 %copy-start.40 = (bf16[2,80,2048]{2,1,0:T(8,128)(2,1)}, bf16[2,80,2048]{2,1,0:T(8,128)(2,1)S(1)}, u32[]{:S(2)}) copy-start(bf16[2,80,2048]{2,1,0:T(8,128)(2,1)S(1)} %get-tuple-element.98) | copy-start | bytes 1966084
  321.2 37.4 %collective-permute-start.9 = (bf16[2,80,2048]{2,1,0:T(8,128)(2,1)S(1)}, bf16[2,80,2048]{2,1,0:T(8,128)(2,1)S(1)}, u32[]{:S(2)}, u32[]{:S(2)}) collective-permute-start(bf16[2,80,2048]{2,1,0:T(8,128)(2,1)S(1)} %get-tuple-element.98), channel_id=1, source_target_pairs={{0,1},{1,2},{2,3},{3,0},{4,5},{5,6},{6,7},{7,4},{8,9},{9,10},{10,1... | collective-permute-start | bytes 1966088 | tf_op jit(solution)/shard_map/ppermute | solution.py:69
  341.2 42.8 %collective-permute-start.10 = (bf16[2,80,2048]{2,1,0:T(8,128)(2,1)S(1)}, bf16[2,80,2048]{2,1,0:T(8,128)(2,1)S(1)}, u32[]{:S(2)}, u32[]{:S(2)}) collective-permute-start(bf16[2,80,2048]{2,1,0:T(8,128)(2,1)S(1)} %get-tuple-element.98), channel_id=1, source_target_pairs={{0,2},{1,3},{2,0},{3,1},{4,6},{5,7},{6,4},{7,5},{8,10},{9,11},{10,... | collective-permute-start | bytes 1966088 | tf_op jit(solution)/shard_map/ppermute | solution.py:69
  345.8 38.2 %collective-permute-start.11 = (bf16[2,80,2048]{2,1,0:T(8,128)(2,1)S(1)}, bf16[2,80,2048]{2,1,0:T(8,128)(2,1)S(1)}, u32[]{:S(2)}, u32[]{:S(2)}) collective-permute-start(bf16[2,80,2048]{2,1,0:T(8,128)(2,1)S(1)} %get-tuple-element.98), channel_id=1, source_target_pairs={{0,3},{1,0},{2,1},{3,2},{4,7},{5,4},{6,5},{7,6},{8,11},{9,8},{10,9... | collective-permute-start | bytes 1966088 | tf_op jit(solution)/shard_map/ppermute | solution.py:69
  346.3 37.8 %copy-start = (bf16[2,320,2048]{2,1,0:T(8,128)(2,1)}, bf16[2,320,2048]{2,1,0:T(8,128)(2,1)S(1)}, u32[]{:S(2)}) copy-start(bf16[2,320,2048]{2,1,0:T(8,128)(2,1)S(1)} %constant_dynamic-update-slice_fusion.7) | copy-start | bytes 7864324
  417.0 34.9 %copy-start.91 = (bf16[400,1408]{1,0:T(8,128)(2,1)}, bf16[400,1408]{1,0:T(8,128)(2,1)S(1)}, u32[]{:S(2)}) copy-start(bf16[400,1408]{1,0:T(8,128)(2,1)S(1)} %get-tuple-element.107) | copy-start | bytes 3379204
  484.6 436.9 %reduce-scatter.6.cloned.1.call-start = ((), (), s32[]{:S(2)}) async-start(), calls=%async_computation.7 | async-start | bytes 38928384 | tf_op jit(solution)/shard_map/reduce_scatter | solution.py:232
  512.0 36.6 %copy-start.103 = (bf16[400,1408]{1,0:T(8,128)(2,1)}, bf16[400,1408]{1,0:T(8,128)(2,1)S(1)}, u32[]{:S(2)}) copy-start(bf16[400,1408]{1,0:T(8,128)(2,1)S(1)} %get-tuple-element.109) | copy-start | bytes 3379204
  582.0 435.9 %reduce-scatter.8.cloned.1.call-start = ((), (), s32[]{:S(2)}) async-start(), calls=%async_computation.8 | async-start | bytes 10027008 | tf_op jit(solution)/shard_map/reduce_scatter | solution.py:288
  611.6 39.4 %copy-start.54 = (bf16[2,4,200,320]{3,2,1,0:T(8,128)(2,1)}, bf16[2,4,200,320]{3,2,1,0:T(8,128)(2,1)S(1)}, u32[]{:S(2)}) copy-start(bf16[2,4,200,320]{3,2,1,0:T(8,128)(2,1)S(1)} %copy.321) | copy-start | bytes 3072004
  657.6 76.7 %copy-start.4 = (f32[2,80,2048]{2,1,0:T(8,128)S(1)}, f32[2,80,2048]{2,1,0:T(8,128)}, u32[]{:S(2)}) copy-start(f32[2,80,2048]{2,1,0:T(8,128)} %copy-done.3) | copy-start | bytes 3932164
  657.6 76.7 %copy-start.63 = (f32[2048,1]{0,1:T(1,128)S(1)}, f32[2048,1]{0,1:T(1,128)}, u32[]{:S(2)}) copy-start(f32[2048,1]{0,1:T(1,128)} %copy-done.62) | copy-start | bytes 24580
  657.6 76.7 %copy-start.74 = (f32[2,80]{1,0:T(2,128)S(1)}, f32[2,80]{1,0:T(2,128)}, u32[]{:S(2)}) copy-start(f32[2,80]{1,0:T(2,128)} %copy-done.73) | copy-start | bytes 1924
  657.6 32.3 %collective-permute-start.18 = (bf16[2,80,2176]{2,1,0:T(8,128)(2,1)}, bf16[2,80,2176]{2,1,0:T(8,128)(2,1)}, u32[]{:S(2)}, u32[]{:S(2)}) collective-permute-start(bf16[2,80,2176]{2,1,0:T(8,128)(2,1)} %get-tuple-element.153), channel_id=1, source_target_pairs={{0,1},{1,2},{2,3},{3,0},{4,5},{5,6},{6,7},{7,4},{8,9},{9,10},{10,1... | collective-permute-start | bytes 2088968 | tf_op jit(solution)/shard_map/ppermute | solution.py:86
  673.4 31.2 %collective-permute-start.20 = (bf16[2,80,2176]{2,1,0:T(8,128)(2,1)S(1)}, bf16[2,80,2176]{2,1,0:T(8,128)(2,1)}, u32[]{:S(2)}, u32[]{:S(2)}) collective-permute-start(bf16[2,80,2176]{2,1,0:T(8,128)(2,1)S(1)} %get-tuple-element.154), channel_id=1, source_target_pairs={{0,3},{1,0},{2,1},{3,2},{4,7},{5,4},{6,5},{7,6},{8,11},{9,8},{10,9... | collective-permute-start | bytes 2088968 | tf_op jit(solution)/shard_map/ppermute | solution.py:86
  673.4 58.2 %collective-permute-start.19 = (bf16[2,80,2176]{2,1,0:T(8,128)(2,1)S(1)}, bf16[2,80,2176]{2,1,0:T(8,128)(2,1)}, u32[]{:S(2)}, u32[]{:S(2)}) collective-permute-start(bf16[2,80,2176]{2,1,0:T(8,128)(2,1)S(1)} %get-tuple-element.155), channel_id=1, source_target_pairs={{0,2},{1,3},{2,0},{3,1},{4,6},{5,7},{6,4},{7,5},{8,10},{9,11},{10,... | collective-permute-start | bytes 2088968 | tf_op jit(solution)/shard_map/ppermute | solution.py:86
  738.3 20.8 %collective-permute-start.21 = (bf16[2,80,2048]{2,1,0:T(8,128)(2,1)S(1)}, bf16[2,80,2048]{2,1,0:T(8,128)(2,1)S(1)}, u32[]{:S(2)}, u32[]{:S(2)}) collective-permute-start(bf16[2,80,2048]{2,1,0:T(8,128)(2,1)S(1)} %get-tuple-element.92), channel_id=1, source_target_pairs={{0,1},{1,2},{2,3},{3,0},{4,5},{5,6},{6,7},{7,4},{8,9},{9,10},{10,1... | collective-permute-start | bytes 1966088 | tf_op jit(solution)/shard_map/ppermute | solution.py:69
  740.3 45.5 %collective-permute-start.22 = (bf16[2,80,2048]{2,1,0:T(8,128)(2,1)S(1)}, bf16[2,80,2048]{2,1,0:T(8,128)(2,1)S(1)}, u32[]{:S(2)}, u32[]{:S(2)}) collective-permute-start(bf16[2,80,2048]{2,1,0:T(8,128)(2,1)S(1)} %get-tuple-element.92), channel_id=1, source_target_pairs={{0,2},{1,3},{2,0},{3,1},{4,6},{5,7},{6,4},{7,5},{8,10},{9,11},{10,... | collective-permute-start | bytes 1966088 | tf_op jit(solution)/shard_map/ppermute | solution.py:69
  744.0 41.9 %collective-permute-start.23 = (bf16[2,80,2048]{2,1,0:T(8,128)(2,1)S(1)}, bf16[2,80,2048]{2,1,0:T(8,128)(2,1)S(1)}, u32[]{:S(2)}, u32[]{:S(2)}) collective-permute-start(bf16[2,80,2048]{2,1,0:T(8,128)(2,1)S(1)} %get-tuple-element.92), channel_id=1, source_target_pairs={{0,3},{1,0},{2,1},{3,2},{4,7},{5,4},{6,5},{7,6},{8,11},{9,8},{10,9... | collective-permute-start | bytes 1966088 | tf_op jit(solution)/shard_map/ppermute | solution.py:69
  810.4 29.4 %collective-permute-start.24 = (bf16[2,80,2048]{2,1,0:T(8,128)(2,1)S(1)}, bf16[2,80,2048]{2,1,0:T(8,128)(2,1)S(1)}, u32[]{:S(2)}, u32[]{:S(2)}) collective-permute-start(bf16[2,80,2048]{2,1,0:T(8,128)(2,1)S(1)} %get-tuple-element.156), channel_id=1, source_target_pairs={{0,1},{1,2},{2,3},{3,0},{4,5},{5,6},{6,7},{7,4},{8,9},{9,10},{10,1... | collective-permute-start | bytes 1966088 | tf_op jit(solution)/shard_map/ppermute | solution.py:86
  824.7 29.2 %collective-permute-start.26 = (bf16[2,80,2048]{2,1,0:T(8,128)(2,1)S(1)}, bf16[2,80,2048]{2,1,0:T(8,128)(2,1)S(1)}, u32[]{:S(2)}, u32[]{:S(2)}) collective-permute-start(bf16[2,80,2048]{2,1,0:T(8,128)(2,1)S(1)} %get-tuple-element.157), channel_id=1, source_target_pairs={{0,3},{1,0},{2,1},{3,2},{4,7},{5,4},{6,5},{7,6},{8,11},{9,8},{10,9... | collective-permute-start | bytes 1966088 | tf_op jit(solution)/shard_map/ppermute | solution.py:86
  824.7 54.8 %collective-permute-start.25 = (bf16[2,80,2048]{2,1,0:T(8,128)(2,1)S(1)}, bf16[2,80,2048]{2,1,0:T(8,128)(2,1)S(1)}, u32[]{:S(2)}, u32[]{:S(2)}) collective-permute-start(bf16[2,80,2048]{2,1,0:T(8,128)(2,1)S(1)} %get-tuple-element.158), channel_id=1, source_target_pairs={{0,2},{1,3},{2,0},{3,1},{4,6},{5,7},{6,4},{7,5},{8,10},{9,11},{10,... | collective-permute-start | bytes 1966088 | tf_op jit(solution)/shard_map/ppermute | solution.py:86
  828.1 51.4 %copy-start.10 = (bf16[2,80,2048]{2,1,0:T(8,128)(2,1)S(1)}, bf16[2,80,2048]{2,1,0:T(8,128)(2,1)}, u32[]{:S(2)}) copy-start(bf16[2,80,2048]{2,1,0:T(8,128)(2,1)} %param.14) | copy-start | bytes 1966084
  828.1 51.4 %copy-start.67 = (f32[2048,1]{0,1:T(1,128)S(1)}, f32[2048,1]{0,1:T(1,128)}, u32[]{:S(2)}) copy-start(f32[2048,1]{0,1:T(1,128)} %copy-done.66) | copy-start | bytes 24580
  929.8 19.8 %collective-permute-start.15 = (bf16[2,80,2048]{2,1,0:T(8,128)(2,1)}, bf16[2,80,2048]{2,1,0:T(8,128)(2,1)}, u32[]{:S(2)}, u32[]{:S(2)}) collective-permute-start(bf16[2,80,2048]{2,1,0:T(8,128)(2,1)} %get-tuple-element.159), channel_id=1, source_target_pairs={{0,1},{1,2},{2,3},{3,0},{4,5},{5,6},{6,7},{7,4},{8,9},{9,10},{10,1... | collective-permute-start | bytes 1966088 | tf_op jit(solution)/shard_map/ppermute | solution.py:86
  931.3 30.4 %collective-permute-start.17 = (bf16[2,80,2048]{2,1,0:T(8,128)(2,1)}, bf16[2,80,2048]{2,1,0:T(8,128)(2,1)}, u32[]{:S(2)}, u32[]{:S(2)}) collective-permute-start(bf16[2,80,2048]{2,1,0:T(8,128)(2,1)} %get-tuple-element.160), channel_id=1, source_target_pairs={{0,3},{1,0},{2,1},{3,2},{4,7},{5,4},{6,5},{7,6},{8,11},{9,8},{10,9... | collective-permute-start | bytes 1966088 | tf_op jit(solution)/shard_map/ppermute | solution.py:86
  933.7 56.7 %collective-permute-start.16 = (bf16[2,80,2048]{2,1,0:T(8,128)(2,1)}, bf16[2,80,2048]{2,1,0:T(8,128)(2,1)}, u32[]{:S(2)}, u32[]{:S(2)}) collective-permute-start(bf16[2,80,2048]{2,1,0:T(8,128)(2,1)} %get-tuple-element.161), channel_id=1, source_target_pairs={{0,2},{1,3},{2,0},{3,1},{4,6},{5,7},{6,4},{7,5},{8,10},{9,11},{10,... | collective-permute-start | bytes 1966088 | tf_op jit(solution)/shard_map/ppermute | solution.py:86
  1019.0 9.1 collective-permute-start.27
  1019.1 9.1 collective-permute-start.29
  1022.9 5.3 collective-permute-start.28
  (98 other events, 531.0 us)
Sparse Core Ops, SparseCore 0:
  17.0 60.9 all-gather.3
  80.4 173.1 all-gather.5
  256.1 173.1 all-gather.7
  484.8 222.3 reduce-scatter.3
  710.7 210.7 reduce-scatter.5
  924.9 73.8 reduce-scatter.7
where the time goes:
time: 1040 us
  waiting for transfers between devices  396 us (38%)
  matrix products  255 us (25%)
  local copies, waits for them, and re-layouts  156 us (15%)
  starting transfers between devices  114 us (11%)
  other arithmetic  98.6 us (9%)
  between operations  16.3 us (2%)
    dot_general x47, matrix products, dot(): return jnp.einsum(spec, a, b, preferred_element_type=F32)  249 us
    ppermute x15, waiting for transfers between devices, tp_scatter(): lax.ppermute(piece, 'tp', [(i, (i + k) % count) for i in range(count)])  182 us
    ppermute x15, waiting for transfers between devices, tp_gather(): lax.ppermute(own, 'tp', [(i, (i + k) % count) for i in range(count)])  177 us
    dynamic_update_slice x18, local copies, waits for them, and re-layouts, tp_gather(): full = lax.dynamic_update_slice_in_dim(full, piece, place, 1)  62.1 us
    ppermute x15, starting transfers between devices, tp_gather(): lax.ppermute(own, 'tp', [(i, (i + k) % count) for i in range(count)])  61.5 us
    unnamed x252, local copies, waits for them, and re-layouts  55.2 us
    ppermute x15, starting transfers between devices, tp_scatter(): lax.ppermute(piece, 'tp', [(i, (i + k) % count) for i in range(count)])  52.6 us
    concatenate x2, other arithmetic, per_device(): jnp.concatenate(pieces, axis=1)  48.2 us
  transfers between devices with their start and end apart: 36, of which 19 were waited for; matrix products, arithmetic and copies ran while one was open for 47% of the time, Pallas kernels for 0%

commit v1 on v0

--- a/solution.py
+++ b/solution.py
@@ -22,12 +22,11 @@
 
 def norm_backward(inputs, gain, grad_out):
     inv_scale = inverse_rms(inputs)
-    gain_grad = jnp.sum(grad_out * inputs * inv_scale, axis=(0, 1))
     scaled = grad_out * gain
     input_grad = inv_scale * scaled - inputs * (inv_scale * inv_scale * inv_scale) * jnp.mean(
         scaled * inputs, axis=-1, keepdims=True
     )
-    return (input_grad, gain_grad)
+    return input_grad
 
 
 def rotary_tables(segments, head_dim):
@@ -60,11 +59,13 @@
     return causal & same_doc
 
 
-def tp_gather(own):
+def tp_gather(own, after=None):
     count = lax.axis_size("tp")
     rank = lax.axis_index("tp")
     micro, rows, width = own.shape
     full = jnp.zeros((micro, count * rows, width), own.dtype)
+    if after is not None:
+        full, _ = lax.optimization_barrier((full, after))
     pieces = [own] + [
         lax.ppermute(own, "tp", [(i, (i + k) % count) for i in range(count)])
         for k in range(1, count)
@@ -73,6 +74,46 @@
         place = lax.rem(rank - k + count, count) * rows
         full = lax.dynamic_update_slice_in_dim(full, piece, place, 1)
     return full
+
+
+def tp_gather_small(own):
+    count = lax.axis_size("tp")
+    rank = lax.axis_index("tp")
+    pieces = [own] + [
+        lax.ppermute(own, "tp", [(i, (i + k) % count) for i in range(count)])
+        for k in range(1, count)
+    ]
+    ordered = []
+    for place in range(count):
+        value = pieces[0]
+        for k in range(1, count):
+            value = jnp.where(lax.rem(rank - k + count, count) == place, pieces[k], value)
+        ordered.append(value)
+    return jnp.stack(ordered)
+
+
+def fsdp_gather(own):
+    count = lax.axis_size("fsdp")
+    if count != 8:
+        full = lax.all_gather(own, "fsdp", axis=0, tiled=True)
+        return full, own
+    rank = lax.axis_index("fsdp")
+    odd = lax.rem(rank, 2) == 1
+
+    def swap(value, bits):
+        return lax.ppermute(value, "fsdp", [(i, i ^ bits(i)) for i in range(count)])
+
+    near = swap(own, lambda i: 2)
+    far = swap(own, lambda i: 4)
+    held = [(0, own), (2, near), (4, far)]
+    passed = jnp.where(odd, near, far)
+    held.append((6, swap(passed, lambda i: 4 if i % 2 else 2)))
+    full = jnp.zeros((count,) + own.shape, own.dtype)
+    for bits, value in held:
+        full = lax.dynamic_update_index_in_dim(full, value, rank ^ bits, 0)
+        other = swap(value, lambda i: 1)
+        full = lax.dynamic_update_index_in_dim(full, other, rank ^ (bits | 1), 0)
+    return full.reshape(count * own.shape[0], own.shape[1]), passed
 
 
 def tp_scatter(part):
@@ -124,11 +165,8 @@
     small_rows, small_width = own_small.shape
     shard_rows = w_query.shape[0]
     own_small = jnp.pad(own_small, ((0, shard_rows - small_rows), (0, HD - small_width)))
-    attn_set = lax.all_gather(
-        jnp.concatenate([w_query, w_key, w_value, w_output.T, own_small], axis=1),
-        "fsdp",
-        axis=0,
-        tiled=True,
+    attn_set, passed = fsdp_gather(
+        jnp.concatenate([w_query, w_key, w_value, w_output.T, own_small], axis=1)
     )
     span = 3 * units
     pair_sets = []
@@ -136,14 +174,18 @@
         held = []
         for e in range(pair * PAIR, (pair + 1) * PAIR):
             held += [w_gate[e], w_up[e], w_down[e].T]
-        pair_sets.append(lax.all_gather(jnp.concatenate(held, axis=1), "fsdp", axis=0, tiled=True))
+        if pair:
+            held, _ = lax.optimization_barrier((held, joined))
+        joined = jnp.concatenate(held, axis=1)
+        pair_sets.append(lax.all_gather(joined, "fsdp", axis=0, tiled=True))
     small = attn_set[:, 4 * head_width :].reshape(-1, shard_rows, HD)[:, :small_rows]
-    small = tp_gather(small).reshape(width, HD)
+    small = tp_gather_small(small.reshape(-1, HD))
+    small = small.reshape(tensor_count, -1, small_rows, HD).swapaxes(0, 1).reshape(width, HD)
     gain_one = small[:, 0].astype(F32)
     gain_two = small[:, 1].astype(F32)
     router = small[:, 2:small_width]
 
-    tokens_full = tp_gather(tokens_in).astype(F32)
+    tokens_full = tp_gather(tokens_in, passed).astype(F32)
     hidden_one = (tokens_full * inverse_rms(tokens_full) * gain_one).astype(BF16)
     hidden_one = hidden_one.reshape(rows, width)
     cosine_table, sine_table = rotary_tables(segment_ids, HD)
@@ -197,7 +239,15 @@
         down = weights[:, start + 2 * units : start + span]
         pick = picks_low[:, e]
         if e and e % PAIR == 0:
-            pick, packed = lax.optimization_barrier((pick, jnp.concatenate(pieces, axis=1)))
+            pick, packed, weighted_outs, gate_grad_slots, routed_grads = lax.optimization_barrier(
+                (
+                    pick,
+                    jnp.concatenate(pieces, axis=1),
+                    weighted_outs,
+                    gate_grad_slots,
+                    routed_grads,
+                )
+            )
             pair_grads.append(lax.psum_scatter(packed, "fsdp", scatter_dimension=0, tiled=True))
             pieces = []
         routed = dot("mst,mtd->msd", pick, hidden_two).astype(BF16).reshape(slots, width)
@@ -238,7 +288,6 @@
     gate_grad_part = jnp.pad(jnp.swapaxes(gate_grad_part, 1, 2), ((0, 0), (0, 0), (0, HD - experts)))
     summed = tp_scatter(jnp.concatenate([token_grad, gate_grad_part], axis=-1).astype(BF16))
     moe_part = dot("mst,msd->mtd", flat_picks, jnp.concatenate(weighted_outs, axis=1))
-    output = (middle + tp_scatter(moe_part.astype(BF16))).astype(BF16)
 
     gates_own = lax.dynamic_slice_in_dim(gates, tensor_rank * own_rows, own_rows, 1)
     gate_grad = summed[:, :, width : width + experts]
@@ -251,10 +300,13 @@
     hidden_two_grad = summed[:, :, :width] + jnp.einsum(
         "mte,de->mtd", logit_grad, router.astype(F32), precision=HIGHEST
     )
-    middle_norm_grad, gain_two_grad = norm_backward(middle, gain_two, hidden_two_grad)
-    middle_grad = middle_norm_grad + out_grad.astype(F32)
+    gain_two_grad = jnp.sum(hidden_two_grad * middle * inverse_rms(middle), axis=(0, 1))
+    middle_grad = norm_backward(middle, gain_two, hidden_two_grad) + out_grad.astype(F32)
 
     attn_grad = tp_gather(middle_grad.astype(BF16)).reshape(rows, width)
+    moe_low, middle_late, _ = lax.optimization_barrier((moe_part.astype(BF16), middle, attn_grad))
+    moe_own = tp_scatter(moe_low)
+    output = (middle_late + moe_own).astype(BF16)
     context_grad = dot("td,de->te", attn_grad, attn_set[:, 3 * head_width : 4 * head_width])
     context_grad = context_grad.astype(BF16).reshape(four)
     prob_grad = dot("mqhd,mkhd->mhqk", context_grad, values_low)
@@ -269,9 +321,11 @@
         [item.astype(BF16).reshape(rows, head_width) for item in (query_grad, key_grad, value_grad)],
         axis=1,
     )
-    hidden_part = dot("te,de->td", qkv_grad, attn_set[:, : 3 * head_width]).astype(BF16)
-    hidden_one_grad = tp_scatter(hidden_part.reshape(micro, group_rows, width))
-    inner_grad, gain_one_grad = norm_backward(inputs, gain_one, hidden_one_grad)
+    hidden_part = dot("te,de->td", qkv_grad, attn_set[:, : 3 * head_width])
+    hidden_part = hidden_part.reshape(micro, group_rows, width)
+    gain_one_grad = jnp.sum(hidden_part * tokens_full * inverse_rms(tokens_full), axis=(0, 1))
+    hidden_one_grad = tp_scatter(hidden_part.astype(BF16))
+    inner_grad = norm_backward(inputs, gain_one, hidden_one_grad)
     input_grad = (middle_grad + inner_grad).astype(BF16)
     small_part = jnp.concatenate(
         [gain_one_grad[:, None], gain_two_grad[:, None], router_grad], axis=1
@@ -284,7 +338,7 @@
         ],
         axis=1,
     )
-    attn_packed, pair_grads = lax.optimization_barrier((attn_packed, pair_grads))
+    attn_packed, pair_grads, output = lax.optimization_barrier((attn_packed, pair_grads, output))
     attn_grads = lax.psum_scatter(attn_packed, "fsdp", scatter_dimension=0, tiled=True)
     small_grads = tp_scatter(attn_grads[None, :, 4 * head_width :])[0]
     attn_grads = attn_grads.astype(F32)

time: 1040 us -> 1050 us (level)
  waiting for transfers between devices: 396 us -> 448 us
  local copies, waits for them, and re-layouts: 156 us -> 117 us
  starting transfers between devices: 114 us -> 97.9 us
    ppermute x15 -> x12, waiting for transfers between devices: 177 us -> 97.3 us  [tp_gather(): lax.ppermute(own, 'tp', [(i, (i + k) % count) for i in range(count)])]
    ppermute x0 -> x10, waiting for transfers between devices: none -> 78.6 us  [the longest x7 69.9 us: swap(): return lax.ppermute(value, 'fsdp', [(i, i ^ bits(i)) for i in range(count)])]
    dynamic_update_slice x18 -> x14, local copies, waits for them, and re-layouts: 62.1 us -> 5.86 us  [tp_gather(): full = lax.dynamic_update_slice_in_dim(full, piece, place, 1)]
    reduce_scatter x2, waiting for transfers between devices: 36.1 us -> 91.9 us  [per_device(): lax.psum_scatter(packed, 'fsdp', scatter_dimension=0, tiled=True)]
    ppermute x15 -> x12, starting transfers between devices: 61.5 us -> 47.4 us  [tp_gather(): lax.ppermute(own, 'tp', [(i, (i + k) % count) for i in range(count)])]
    ppermute x15, starting transfers between devices: 52.6 us -> 41.3 us  [tp_scatter(): lax.ppermute(piece, 'tp', [(i, (i + k) % count) for i in range(count)])]
    convert_element_type x0 -> x5, other arithmetic: none -> 10.6 us  [the longest x2 3.33 us: per_device(): weighted_outs.append((slot_gate * expert_out).astype(BF16))]
    unnamed x252 -> x272, local copies, waits for them, and re-layouts: 55.2 us -> 56.1 us
  transfers between devices with their start and end apart: 36 -> 42, of which waited for: 19 -> 25; matrix products, arithmetic and copies ran while one was open for 47% -> 42% of each run, Pallas kernels for 0% -> 0%
where the time goes in v1:
time: 1050 us; the launch traced here: 1040 us
  waiting for transfers between devices  448 us (43%)
  matrix products  256 us (24%)
  local copies, waits for them, and re-layouts  117 us (11%)
  other arithmetic  106 us (10%)
  starting transfers between devices  97.9 us (9%)
  between operations  16 us (2%)
    dot_general x47, matrix products, dot(): return jnp.einsum(spec, a, b, preferred_element_type=F32)  249 us
    ppermute x15, waiting for transfers between devices, tp_scatter(): lax.ppermute(piece, 'tp', [(i, (i + k) % count) for i in range(count)])  180 us
    ppermute x12, waiting for transfers between devices, tp_gather(): lax.ppermute(own, 'tp', [(i, (i + k) % count) for i in range(count)])  97.3 us
    reduce_scatter x2, waiting for transfers between devices, per_device(): lax.psum_scatter(packed, 'fsdp', scatter_dimension=0, tiled=True)  91.9 us
    ppermute x7, waiting for transfers between devices, swap(): return lax.ppermute(value, 'fsdp', [(i, i ^ bits(i)) for i in range(count)])  69.9 us
    unnamed x272, local copies, waits for them, and re-layouts  56.1 us
    concatenate x2, other arithmetic, per_device(): jnp.concatenate(pieces, axis=1)  48.5 us
    ppermute x12, starting transfers between devices, tp_gather(): lax.ppermute(own, 'tp', [(i, (i + k) % count) for i in range(count)])  47.4 us
  transfers between devices with their start and end apart: 42, of which 25 were waited for; matrix products, arithmetic and copies ran while one was open for 42% of the time, Pallas kernels for 0%

profile of v1, /device:TPU:0, one launch (start us, length us, event | category | flops | bytes accessed | tf_op | source)
XLA Modules:
  0.0 1040.5 jit_solution(11098049990194388063)
XLA Ops:
  64.8 41.2 %collective-permute-done.1 = bf16[256,2176]{1,0:T(8,128)(2,1)S(1)} collective-permute-done((bf16[256,2176]{1,0:T(8,128)(2,1)}, bf16[256,2176]{1,0:T(8,128)(2,1)S(1)}, u32[]{:S(2)}, u32[]{:S(2)}) %collective-permute-start.1) | collective-permute-done | bytes 1114144 | tf_op jit(solution)/shard_map/ppermute | solution.py:104
  112.5 10.6 %collective-permute-done.2 = bf16[2,80,2048]{2,1,0:T(8,128)(2,1)S(1)} collective-permute-done((bf16[2,80,2048]{2,1,0:T(8,128)(2,1)S(1)}, bf16[2,80,2048]{2,1,0:T(8,128)(2,1)S(1)}, u32[]{:S(2)}, u32[]{:S(2)}) %collective-permute-start.2) | collective-permute-done | bytes 655392 | tf_op jit(solution)/shard_map/ppermute | solution.py:70
  123.1 14.4 %collective-permute-start.4 = (bf16[2,80,2048]{2,1,0:T(8,128)(2,1)S(1)}, bf16[2,80,2048]{2,1,0:T(8,128)(2,1)S(1)}, u32[]{:S(2)}, u32[]{:S(2)}) collective-permute-start(bf16[2,80,2048]{2,1,0:T(8,128)(2,1)S(1)} %copy-done.16), channel_id=1, source_target_pairs={{0,3},{1,0},{2,1},{3,2},{4,7},{5,4},{6,5},{7,6},{8,11},{9,8},{10,9... | collective-permute-start | bytes 1966088 | tf_op jit(solution)/shard_map/ppermute | solution.py:70
  140.5 10.5 %collective-permute-done.4 = bf16[2,80,2048]{2,1,0:T(8,128)(2,1)S(1)} collective-permute-done((bf16[2,80,2048]{2,1,0:T(8,128)(2,1)S(1)}, bf16[2,80,2048]{2,1,0:T(8,128)(2,1)S(1)}, u32[]{:S(2)}, u32[]{:S(2)}) %collective-permute-start.4) | collective-permute-done | bytes 655392 | tf_op jit(solution)/shard_map/ppermute | solution.py:70
  151.8 25.3 %collective-permute-done.8 = bf16[256,2176]{1,0:T(8,128)(2,1)S(1)} collective-permute-done((bf16[256,2176]{1,0:T(8,128)(2,1)S(1)}, bf16[256,2176]{1,0:T(8,128)(2,1)S(1)}, u32[]{:S(2)}, u32[]{:S(2)}) %collective-permute-start.8) | collective-permute-done | bytes 1114144 | tf_op jit(solution)/shard_map/ppermute | solution.py:104
  239.4 12.3 %collective-permute-done.13 = bf16[2,80,2048]{2,1,0:T(8,128)(2,1)S(1)} collective-permute-done((bf16[2,80,2048]{2,1,0:T(8,128)(2,1)S(1)}, bf16[2,80,2048]{2,1,0:T(8,128)(2,1)S(1)}, u32[]{:S(2)}, u32[]{:S(2)}) %collective-permute-start.13) | collective-permute-done | bytes 655392 | tf_op jit(solution)/shard_map/ppermute | solution.py:127
  252.6 11.4 %collective-permute-done.15 = bf16[2,80,2048]{2,1,0:T(8,128)(2,1)S(1)} collective-permute-done((bf16[2,80,2048]{2,1,0:T(8,128)(2,1)S(1)}, bf16[2,80,2048]{2,1,0:T(8,128)(2,1)S(1)}, u32[]{:S(2)}, u32[]{:S(2)}) %collective-permute-start.15) | collective-permute-done | bytes 655392 | tf_op jit(solution)/shard_map/ppermute | solution.py:127
  264.1 27.5 %collective-permute-done.14 = bf16[2,80,2048]{2,1,0:T(8,128)(2,1)S(1)} collective-permute-done((bf16[2,80,2048]{2,1,0:T(8,128)(2,1)S(1)}, bf16[2,80,2048]{2,1,0:T(8,128)(2,1)S(1)}, u32[]{:S(2)}, u32[]{:S(2)}) %collective-permute-start.14) | collective-permute-done | bytes 655392 | tf_op jit(solution)/shard_map/ppermute | solution.py:127
  293.0 13.4 %collective-permute-start.16 = (bf16[2,80,2048]{2,1,0:T(8,128)(2,1)S(1)}, bf16[2,80,2048]{2,1,0:T(8,128)(2,1)S(1)}, u32[]{:S(2)}, u32[]{:S(2)}) collective-permute-start(bf16[2,80,2048]{2,1,0:T(8,128)(2,1)S(1)} %get-tuple-element.143), channel_id=1, source_target_pairs={{0,1},{1,2},{2,3},{3,0},{4,5},{5,6},{6,7},{7,4},{8,9},{9,10},{10,1... | collective-permute-start | bytes 1966088 | tf_op jit(solution)/shard_map/ppermute | solution.py:70
  312.7 12.3 %collective-permute-done.16 = bf16[2,80,2048]{2,1,0:T(8,128)(2,1)S(1)} collective-permute-done((bf16[2,80,2048]{2,1,0:T(8,128)(2,1)S(1)}, bf16[2,80,2048]{2,1,0:T(8,128)(2,1)S(1)}, u32[]{:S(2)}, u32[]{:S(2)}) %collective-permute-start.16) | collective-permute-done | bytes 655392 | tf_op jit(solution)/shard_map/ppermute | solution.py:70
  325.1 26.1 %collective-permute-done.17 = bf16[2,80,2048]{2,1,0:T(8,128)(2,1)S(1)} collective-permute-done((bf16[2,80,2048]{2,1,0:T(8,128)(2,1)S(1)}, bf16[2,80,2048]{2,1,0:T(8,128)(2,1)S(1)}, u32[]{:S(2)}, u32[]{:S(2)}) %collective-permute-start.17) | collective-permute-done | bytes 655392 | tf_op jit(solution)/shard_map/ppermute | solution.py:70
  370.7 8.7 fusion.11
  379.5 7.5 multiply_convert_fusion.17
  394.1 8.5 fusion.15
  402.6 6.2 multiply_convert_fusion.20
  408.8 6.0 fusion.55
  427.8 10.4 %fusion.71 = bf16[400,2048]{1,0:T(8,128)(2,1)} fusion(bf16[2048,8448]{0,1:T(8,128)(2,1)} %all-gather.3.cloned.1.call-done, bf16[400,1408]{1,0:T(8,128)(2,1)S(1)} %copy-done.115, bf16[400,1408]{1,0:T(8,128)(2,1)S(1)} %copy-done.114), kind=kOutput, calls=%fused_computation.100 | convolution fusion | flops 4619059200 | bytes 15425536 | tf_op jit(solution)/shard_map/sf,df->sd/dot_general | solution.py:133
  438.2 10.5 %fusion.68 = bf16[400,2048]{1,0:T(8,128)(2,1)} fusion(bf16[2048,8448]{0,1:T(8,128)(2,1)} %all-gather.3.cloned.1.call-done, bf16[400,1408]{1,0:T(8,128)(2,1)S(1)} %get-tuple-element.153, bf16[400,1408]{1,0:T(8,128)(2,1)S(1)} %get-tuple-element.152), kind=kOutput, calls=%fused_computation.99 | convolution fusion | flops 4619059200 | bytes 15425536 | tf_op jit(solution)/shard_map/sf,df->sd/dot_general | solution.py:133
  448.6 9.2 convolution_convert_fusion.3
  457.9 8.9 convolution_convert_fusion.2
  466.8 23.8 %pad_maximum_fusion = bf16[2048,8448]{1,0:T(8,128)(2,1)} fusion(bf16[2048,1408]{1,0:T(8,128)(2,1)} %convolution_convert_fusion.7, bf16[2048,2816]{1,0:T(8,128)(2,1)} %convolution_convert_fusion.2, bf16[2048,1408]{1,0:T(8,128)(2,1)} %convolution_convert_fusion.8, bf16[2048,2816]{1,0:T(8,128)(2,1)} %convolution_convert_fusion.3), kind=kLoop, calls=%fused_computation.1 | loop fusion | flops 138412032 | bytes 69206016 | tf_op jit(solution)/shard_map/concatenate | solution.py:245
  501.5 8.9 fusion.3
  510.5 7.4 multiply_convert_fusion.11
  517.9 5.3 convolution_convert_fusion.5
  523.2 10.0 fusion.7
  533.2 7.2 multiply_convert_fusion.14
  540.4 5.3 convolution_convert_fusion.6
  545.8 8.9 convolution_convert_fusion.1
  554.7 9.1 convolution_convert_fusion
  563.8 24.7 %pad_maximum_fusion.1 = bf16[2048,8448]{1,0:T(8,128)(2,1)} fusion(bf16[2048,1408]{1,0:T(8,128)(2,1)} %convolution_convert_fusion.5, bf16[2048,2816]{1,0:T(8,128)(2,1)} %convolution_convert_fusion, bf16[2048,1408]{1,0:T(8,128)(2,1)} %convolution_convert_fusion.6, bf16[2048,2816]{1,0:T(8,128)(2,1)} %convolution_convert_fusion.1), kind=kLoop, calls=%fused_computation.2 | loop fusion | flops 138412032 | bytes 69206016 | tf_op jit(solution)/shard_map/concatenate | solution.py:281
  588.6 5.6 fusion.43
  604.7 10.0 fusion.77
  614.8 9.9 fusion.74
  631.5 16.3 %collective-permute-start.22 = (bf16[2,80,2176]{2,1,0:T(8,128)(2,1)}, bf16[2,80,2176]{2,1,0:T(8,128)(2,1)}, u32[]{:S(2)}, u32[]{:S(2)}) collective-permute-start(bf16[2,80,2176]{2,1,0:T(8,128)(2,1)} %get-tuple-element.196), channel_id=1, source_target_pairs={{0,1},{1,2},{2,3},{3,0},{4,5},{5,6},{6,7},{7,4},{8,9},{9,10},{10,1... | collective-permute-start | bytes 2088968 | tf_op jit(solution)/shard_map/ppermute | solution.py:127
  651.1 12.9 %collective-permute-done.22 = bf16[2,80,2176]{2,1,0:T(8,128)(2,1)} collective-permute-done((bf16[2,80,2176]{2,1,0:T(8,128)(2,1)}, bf16[2,80,2176]{2,1,0:T(8,128)(2,1)}, u32[]{:S(2)}, u32[]{:S(2)}) %collective-permute-start.22) | collective-permute-done | bytes 696352 | tf_op jit(solution)/shard_map/ppermute | solution.py:127
  664.1 15.0 %collective-permute-done.24 = bf16[2,80,2176]{2,1,0:T(8,128)(2,1)} collective-permute-done((bf16[2,80,2176]{2,1,0:T(8,128)(2,1)}, bf16[2,80,2176]{2,1,0:T(8,128)(2,1)}, u32[]{:S(2)}, u32[]{:S(2)}) %collective-permute-start.24) | collective-permute-done | bytes 696352 | tf_op jit(solution)/shard_map/ppermute | solution.py:127
  679.0 24.1 %collective-permute-done.23 = bf16[2,80,2176]{2,1,0:T(8,128)(2,1)} collective-permute-done((bf16[2,80,2176]{2,1,0:T(8,128)(2,1)S(1)}, bf16[2,80,2176]{2,1,0:T(8,128)(2,1)}, u32[]{:S(2)}, u32[]{:S(2)}) %collective-permute-start.23) | collective-permute-done | bytes 696352 | tf_op jit(solution)/shard_map/ppermute | solution.py:127
  708.9 8.8 collective-permute-start.25
  722.5 24.5 %collective-permute-done.25 = bf16[2,80,2048]{2,1,0:T(8,128)(2,1)S(1)} collective-permute-done((bf16[2,80,2048]{2,1,0:T(8,128)(2,1)S(1)}, bf16[2,80,2048]{2,1,0:T(8,128)(2,1)S(1)}, u32[]{:S(2)}, u32[]{:S(2)}) %collective-permute-start.25) | collective-permute-done | bytes 655392 | tf_op jit(solution)/shard_map/ppermute | solution.py:70
  747.0 8.5 collective-permute-done.26
  773.9 9.0 collective-permute-start.28
  802.5 5.7 convolution_convert_fusion.4
  812.5 21.0 %collective-permute-done.29 = bf16[2,80,2048]{2,1,0:T(8,128)(2,1)} collective-permute-done((bf16[2,80,2048]{2,1,0:T(8,128)(2,1)}, bf16[2,80,2048]{2,1,0:T(8,128)(2,1)}, u32[]{:S(2)}, u32[]{:S(2)}) %collective-permute-start.29) | collective-permute-done | bytes 655392 | tf_op jit(solution)/shard_map/ppermute | solution.py:127
  836.5 91.9 %reduce-scatter.6.cloned.1.call-done = bf16[256,8448]{1,0:T(8,128)(2,1)} async-done(((bf16[2048,8448]{1,0:T(8,128)(2,1)}), bf16[256,8448]{1,0:T(8,128)(2,1)}) %reduce-scatter.6.cloned.1.call-update) | async-done | bytes 4325392 | tf_op jit(solution)/shard_map/reduce_scatter | solution.py:282
  938.6 15.3 %collective-permute-done.31 = bf16[2,80,2048]{2,1,0:T(8,128)(2,1)} collective-permute-done((bf16[2,80,2048]{2,1,0:T(8,128)(2,1)}, bf16[2,80,2048]{2,1,0:T(8,128)(2,1)}, u32[]{:S(2)}, u32[]{:S(2)}) %collective-permute-start.31) | collective-permute-done | bytes 655392 | tf_op jit(solution)/shard_map/ppermute | solution.py:127
  953.9 12.1 %collective-permute-done.33 = bf16[2,80,2048]{2,1,0:T(8,128)(2,1)} collective-permute-done((bf16[2,80,2048]{2,1,0:T(8,128)(2,1)}, bf16[2,80,2048]{2,1,0:T(8,128)(2,1)}, u32[]{:S(2)}, u32[]{:S(2)}) %collective-permute-start.33) | collective-permute-done | bytes 655392 | tf_op jit(solution)/shard_map/ppermute | solution.py:127
  966.0 28.7 %collective-permute-done.32 = bf16[2,80,2048]{2,1,0:T(8,128)(2,1)} collective-permute-done((bf16[2,80,2048]{2,1,0:T(8,128)(2,1)}, bf16[2,80,2048]{2,1,0:T(8,128)(2,1)}, u32[]{:S(2)}, u32[]{:S(2)}) %collective-permute-start.32) | collective-permute-done | bytes 655392 | tf_op jit(solution)/shard_map/ppermute | solution.py:127
  1008.7 6.2 copy.420
  (496 shorter events, 307.6 us)
Async XLA Ops:
  7.2 363.5 %all-gather.3.cloned.1.call-start = ((), (), s32[]{:S(2)}) async-start(), calls=%async_computation.3 | async-start | bytes 38928384 | tf_op jit(solution)/shard_map/all_gather | solution.py:180
  29.4 472.1 %all-gather.5.cloned.1.call-start = ((), (), s32[]{:S(2)}) async-start(), calls=%async_computation.4 | async-start | bytes 38928384 | tf_op jit(solution)/shard_map/all_gather | solution.py:180
  45.3 791.2 %reduce-scatter.4.cloned.1.call-start = ((), (), s32[]{:S(2)}) async-start(), calls=%async_computation.5 | async-start | bytes 38928384 | tf_op jit(solution)/shard_map/reduce_scatter | solution.py:251
  45.4 265.6 %collective-permute-start.20 = (bf16[2,80,2048]{2,1,0:T(8,128)(2,1)}, bf16[2,80,2048]{2,1,0:T(8,128)(2,1)}, u32[]{:S(2)}, u32[]{:S(2)}) collective-permute-start(bf16[2,80,2048]{2,1,0:T(8,128)(2,1)} %param.15), channel_id=1, source_target_pairs={{0,2},{1,3},{2,0},{3,1},{4,6},{5,7},{6,4},{7,5},{8,10},{9,11},{10,... | collective-permute-start | bytes 1966088 | tf_op jit(solution)/shard_map/ppermute | solution.py:70
  49.5 256.9 %collective-permute-start.19 = (bf16[2,80,2048]{2,1,0:T(8,128)(2,1)}, bf16[2,80,2048]{2,1,0:T(8,128)(2,1)}, u32[]{:S(2)}, u32[]{:S(2)}) collective-permute-start(bf16[2,80,2048]{2,1,0:T(8,128)(2,1)} %param.15), channel_id=1, source_target_pairs={{0,1},{1,2},{2,3},{3,0},{4,5},{5,6},{6,7},{7,4},{8,9},{9,10},{10,1... | collective-permute-start | bytes 1966088 | tf_op jit(solution)/shard_map/ppermute | solution.py:70
  55.0 51.0 %collective-permute-start.1 = (bf16[256,2176]{1,0:T(8,128)(2,1)}, bf16[256,2176]{1,0:T(8,128)(2,1)S(1)}, u32[]{:S(2)}, u32[]{:S(2)}) collective-permute-start(bf16[256,2176]{1,0:T(8,128)(2,1)} %pad_dynamic-update-slice_fusion), channel_id=1, source_target_pairs={{0,16},{4,20},{8,24},{12,28},{16,0},{20,4},{24,8},{28,12},{1,17},{... | collective-permute-start | bytes 3342344 | tf_op jit(solution)/shard_map/ppermute | solution.py:104
  56.6 50.9 %collective-permute-start = (bf16[256,2176]{1,0:T(8,128)(2,1)}, bf16[256,2176]{1,0:T(8,128)(2,1)S(1)}, u32[]{:S(2)}, u32[]{:S(2)}) collective-permute-start(bf16[256,2176]{1,0:T(8,128)(2,1)} %pad_dynamic-update-slice_fusion), channel_id=1, source_target_pairs={{0,8},{4,12},{8,0},{12,4},{16,24},{20,28},{24,16},{28,20},{1,9},{5... | collective-permute-start | bytes 3342344 | tf_op jit(solution)/shard_map/ppermute | solution.py:104
  58.1 79.5 %collective-permute-start.3 = (bf16[2,80,2048]{2,1,0:T(8,128)(2,1)S(1)}, bf16[2,80,2048]{2,1,0:T(8,128)(2,1)}, u32[]{:S(2)}, u32[]{:S(2)}) collective-permute-start(bf16[2,80,2048]{2,1,0:T(8,128)(2,1)S(1)} %copy-done.16), channel_id=1, source_target_pairs={{0,2},{1,3},{2,0},{3,1},{4,6},{5,7},{6,4},{7,5},{8,10},{9,11},{10,... | collective-permute-start | bytes 1966088 | tf_op jit(solution)/shard_map/ppermute | solution.py:70
  60.1 297.8 %copy-start.79 = (s32[2,4,320]{2,0,1:T(2,128)}, s32[2,4,320]{2,0,1:T(2,128)S(1)}, u32[]{:S(2)}) copy-start(s32[2,4,320]{2,0,1:T(2,128)S(1)} %copy.382) | copy-start | bytes 30724
  106.0 17.1 %collective-permute-start.2 = (bf16[2,80,2048]{2,1,0:T(8,128)(2,1)S(1)}, bf16[2,80,2048]{2,1,0:T(8,128)(2,1)S(1)}, u32[]{:S(2)}, u32[]{:S(2)}) collective-permute-start(bf16[2,80,2048]{2,1,0:T(8,128)(2,1)S(1)} %copy-done.16), channel_id=1, source_target_pairs={{0,1},{1,2},{2,3},{3,0},{4,5},{5,6},{6,7},{7,4},{8,9},{9,10},{10,1... | collective-permute-start | bytes 1966088 | tf_op jit(solution)/shard_map/ppermute | solution.py:70
  107.4 32.8 %collective-permute-start.5 = (bf16[256,2176]{1,0:T(8,128)(2,1)}, bf16[256,2176]{1,0:T(8,128)(2,1)S(1)}, u32[]{:S(2)}, u32[]{:S(2)}) collective-permute-start(bf16[256,2176]{1,0:T(8,128)(2,1)} %pad_dynamic-update-slice_fusion), channel_id=1, source_target_pairs={{0,4},{4,0},{8,12},{12,8},{16,20},{20,16},{24,28},{28,24},{1,5},{5... | collective-permute-start | bytes 3342344 | tf_op jit(solution)/shard_map/ppermute | solution.py:104
  123.1 27.9 %collective-permute-start.4 = (bf16[2,80,2048]{2,1,0:T(8,128)(2,1)S(1)}, bf16[2,80,2048]{2,1,0:T(8,128)(2,1)S(1)}, u32[]{:S(2)}, u32[]{:S(2)}) collective-permute-start(bf16[2,80,2048]{2,1,0:T(8,128)(2,1)S(1)} %copy-done.16), channel_id=1, source_target_pairs={{0,3},{1,0},{2,1},{3,2},{4,7},{5,4},{6,5},{7,6},{8,11},{9,8},{10,9... | collective-permute-start | bytes 1966088 | tf_op jit(solution)/shard_map/ppermute | solution.py:70
  137.5 39.6 %collective-permute-start.8 = (bf16[256,2176]{1,0:T(8,128)(2,1)S(1)}, bf16[256,2176]{1,0:T(8,128)(2,1)S(1)}, u32[]{:S(2)}, u32[]{:S(2)}) collective-permute-start(bf16[256,2176]{1,0:T(8,128)(2,1)S(1)} %broadcast_select_fusion), channel_id=1, source_target_pairs={{0,8},{4,20},{8,0},{12,28},{16,24},{20,4},{24,16},{28,12},{1,9},{5... | collective-permute-start | bytes 3342344 | tf_op jit(solution)/shard_map/ppermute | solution.py:104
  140.3 37.1 %collective-permute-start.7 = (bf16[256,2176]{1,0:T(8,128)(2,1)S(1)}, bf16[256,2176]{1,0:T(8,128)(2,1)S(1)}, u32[]{:S(2)}, u32[]{:S(2)}) collective-permute-start(bf16[256,2176]{1,0:T(8,128)(2,1)S(1)} %copy-done.22), channel_id=1, source_target_pairs={{0,4},{4,0},{8,12},{12,8},{16,20},{20,16},{24,28},{28,24},{1,5},{5... | collective-permute-start | bytes 3342344 | tf_op jit(solution)/shard_map/ppermute | solution.py:104
  151.0 26.1 %collective-permute-start.6 = (bf16[256,2176]{1,0:T(8,128)(2,1)S(1)}, bf16[256,2176]{1,0:T(8,128)(2,1)S(1)}, u32[]{:S(2)}, u32[]{:S(2)}) collective-permute-start(bf16[256,2176]{1,0:T(8,128)(2,1)S(1)} %copy-done.24), channel_id=1, source_target_pairs={{0,4},{4,0},{8,12},{12,8},{16,20},{20,16},{24,28},{28,24},{1,5},{5... | collective-permute-start | bytes 3342344 | tf_op jit(solution)/shard_map/ppermute | solution.py:104
  177.1 2.8 collective-permute-start.9
  180.1 8.3 collective-permute-start.12
  180.1 12.9 %collective-permute-start.11 = (bf16[512,128]{1,0:T(8,128)(2,1)S(1)}, bf16[512,128]{1,0:T(8,128)(2,1)S(1)}, u32[]{:S(2)}, u32[]{:S(2)}) collective-permute-start(bf16[512,128]{1,0:T(8,128)(2,1)S(1)} %bitcast.329), channel_id=1, source_target_pairs={{0,2},{1,3},{2,0},{3,1},{4,6},{5,7},{6,4},{7,5},{8,10},{9,11},{10,... | collective-permute-start | bytes 393224 | tf_op jit(solution)/shard_map/ppermute | solution.py:83
  182.0 11.0 %collective-permute-start.10 = (bf16[512,128]{1,0:T(8,128)(2,1)S(1)}, bf16[512,128]{1,0:T(8,128)(2,1)S(1)}, u32[]{:S(2)}, u32[]{:S(2)}) collective-permute-start(bf16[512,128]{1,0:T(8,128)(2,1)S(1)} %bitcast.330), channel_id=1, source_target_pairs={{0,3},{1,0},{2,1},{3,2},{4,7},{5,4},{6,5},{7,6},{8,11},{9,8},{10,9... | collective-permute-start | bytes 393224 | tf_op jit(solution)/shard_map/ppermute | solution.py:83
  193.3 158.1 %copy-start.13 = (bf16[8,4,64,128]{3,2,1,0:T(8,128)(2,1)}, bf16[8,4,64,128]{3,2,1,0:T(8,128)(2,1)S(1)}, u32[]{:S(2)}) copy-start(bf16[8,4,64,128]{3,2,1,0:T(8,128)(2,1)S(1)} %copy.374) | copy-start | bytes 1572868
  193.8 99.0 %copy-start.77 = (f32[2048]{0:T(1024)}, f32[2048]{0:T(1024)S(1)}, u32[]{:S(2)}) copy-start(f32[2048]{0:T(1024)S(1)} %get-tuple-element.134) | copy-start | bytes 24580
  232.2 19.5 %collective-permute-start.13 = (bf16[2,80,2048]{2,1,0:T(8,128)(2,1)S(1)}, bf16[2,80,2048]{2,1,0:T(8,128)(2,1)S(1)}, u32[]{:S(2)}, u32[]{:S(2)}) collective-permute-start(bf16[2,80,2048]{2,1,0:T(8,128)(2,1)S(1)} %get-tuple-element.205), channel_id=1, source_target_pairs={{0,1},{1,2},{2,3},{3,0},{4,5},{5,6},{6,7},{7,4},{8,9},{9,10},{10,1... | collective-permute-start | bytes 1966088 | tf_op jit(solution)/shard_map/ppermute | solution.py:127
  234.8 29.2 %collective-permute-start.15 = (bf16[2,80,2048]{2,1,0:T(8,128)(2,1)S(1)}, bf16[2,80,2048]{2,1,0:T(8,128)(2,1)S(1)}, u32[]{:S(2)}, u32[]{:S(2)}) collective-permute-start(bf16[2,80,2048]{2,1,0:T(8,128)(2,1)S(1)} %get-tuple-element.206), channel_id=1, source_target_pairs={{0,3},{1,0},{2,1},{3,2},{4,7},{5,4},{6,5},{7,6},{8,11},{9,8},{10,9... | collective-permute-start | bytes 1966088 | tf_op jit(solution)/shard_map/ppermute | solution.py:127
  236.1 55.4 %collective-permute-start.14 = (bf16[2,80,2048]{2,1,0:T(8,128)(2,1)S(1)}, bf16[2,80,2048]{2,1,0:T(8,128)(2,1)S(1)}, u32[]{:S(2)}, u32[]{:S(2)}) collective-permute-start(bf16[2,80,2048]{2,1,0:T(8,128)(2,1)S(1)} %get-tuple-element.207), channel_id=1, source_target_pairs={{0,2},{1,3},{2,0},{3,1},{4,6},{5,7},{6,4},{7,5},{8,10},{9,11},{10,... | collective-permute-start | bytes 1966088 | tf_op jit(solution)/shard_map/ppermute | solution.py:127
  237.8 258.3 %copy-start.39 = (bf16[2,200,320]{2,1,0:T(8,128)(2,1)}, bf16[2,200,320]{2,1,0:T(8,128)(2,1)S(1)}, u32[]{:S(2)}) copy-start(bf16[2,200,320]{2,1,0:T(8,128)(2,1)S(1)} %slice_bitcast_fusion.29) | copy-start | bytes 768004
  251.7 60.9 %collective-permute-start.21 = (bf16[2,80,2048]{2,1,0:T(8,128)(2,1)}, bf16[2,80,2048]{2,1,0:T(8,128)(2,1)S(1)}, u32[]{:S(2)}, u32[]{:S(2)}) collective-permute-start(bf16[2,80,2048]{2,1,0:T(8,128)(2,1)} %param.15), channel_id=1, source_target_pairs={{0,3},{1,0},{2,1},{3,2},{4,7},{5,4},{6,5},{7,6},{8,11},{9,8},{10,9... | collective-permute-start | bytes 1966088 | tf_op jit(solution)/shard_map/ppermute | solution.py:70
  293.0 31.9 %collective-permute-start.16 = (bf16[2,80,2048]{2,1,0:T(8,128)(2,1)S(1)}, bf16[2,80,2048]{2,1,0:T(8,128)(2,1)S(1)}, u32[]{:S(2)}, u32[]{:S(2)}) collective-permute-start(bf16[2,80,2048]{2,1,0:T(8,128)(2,1)S(1)} %get-tuple-element.143), channel_id=1, source_target_pairs={{0,1},{1,2},{2,3},{3,0},{4,5},{5,6},{6,7},{7,4},{8,9},{9,10},{10,1... | collective-permute-start | bytes 1966088 | tf_op jit(solution)/shard_map/ppermute | solution.py:70
  307.6 43.6 %collective-permute-start.17 = (bf16[2,80,2048]{2,1,0:T(8,128)(2,1)S(1)}, bf16[2,80,2048]{2,1,0:T(8,128)(2,1)S(1)}, u32[]{:S(2)}, u32[]{:S(2)}) collective-permute-start(bf16[2,80,2048]{2,1,0:T(8,128)(2,1)S(1)} %get-tuple-element.143), channel_id=1, source_target_pairs={{0,2},{1,3},{2,0},{3,1},{4,6},{5,7},{6,4},{7,5},{8,10},{9,11},{10,... | collective-permute-start | bytes 1966088 | tf_op jit(solution)/shard_map/ppermute | solution.py:70
  312.4 38.9 %collective-permute-start.18 = (bf16[2,80,2048]{2,1,0:T(8,128)(2,1)S(1)}, bf16[2,80,2048]{2,1,0:T(8,128)(2,1)S(1)}, u32[]{:S(2)}, u32[]{:S(2)}) collective-permute-start(bf16[2,80,2048]{2,1,0:T(8,128)(2,1)S(1)} %get-tuple-element.143), channel_id=1, source_target_pairs={{0,3},{1,0},{2,1},{3,2},{4,7},{5,4},{6,5},{7,6},{8,11},{9,8},{10,9... | collective-permute-start | bytes 1966088 | tf_op jit(solution)/shard_map/ppermute | solution.py:70
  490.6 437.8 %reduce-scatter.6.cloned.1.call-start = ((), (), s32[]{:S(2)}) async-start(), calls=%async_computation.6 | async-start | bytes 38928384 | tf_op jit(solution)/shard_map/reduce_scatter | solution.py:282
  588.5 433.9 %reduce-scatter.8.cloned.1.call-start = ((), (), s32[]{:S(2)}) async-start(), calls=%async_computation.7 | async-start | bytes 10027008 | tf_op jit(solution)/shard_map/reduce_scatter | solution.py:342
  631.5 74.0 %copy-start.78 = (f32[2048]{0:T(1024)S(1)}, f32[2048]{0:T(1024)}, u32[]{:S(2)}) copy-start(f32[2048]{0:T(1024)} %copy-done.77) | copy-start | bytes 24580
  631.5 74.0 %copy-start.90 = (f32[2,80]{1,0:T(2,128)S(1)}, f32[2,80]{1,0:T(2,128)}, u32[]{:S(2)}) copy-start(f32[2,80]{1,0:T(2,128)} %copy-done.89) | copy-start | bytes 1924
  631.5 32.6 %collective-permute-start.22 = (bf16[2,80,2176]{2,1,0:T(8,128)(2,1)}, bf16[2,80,2176]{2,1,0:T(8,128)(2,1)}, u32[]{:S(2)}, u32[]{:S(2)}) collective-permute-start(bf16[2,80,2176]{2,1,0:T(8,128)(2,1)} %get-tuple-element.196), channel_id=1, source_target_pairs={{0,1},{1,2},{2,3},{3,0},{4,5},{5,6},{6,7},{7,4},{8,9},{9,10},{10,1... | collective-permute-start | bytes 2088968 | tf_op jit(solution)/shard_map/ppermute | solution.py:127
  647.8 31.3 %collective-permute-start.24 = (bf16[2,80,2176]{2,1,0:T(8,128)(2,1)}, bf16[2,80,2176]{2,1,0:T(8,128)(2,1)}, u32[]{:S(2)}, u32[]{:S(2)}) collective-permute-start(bf16[2,80,2176]{2,1,0:T(8,128)(2,1)} %get-tuple-element.197), channel_id=1, source_target_pairs={{0,3},{1,0},{2,1},{3,2},{4,7},{5,4},{6,5},{7,6},{8,11},{9,8},{10,9... | collective-permute-start | bytes 2088968 | tf_op jit(solution)/shard_map/ppermute | solution.py:127
  648.0 55.2 %collective-permute-start.23 = (bf16[2,80,2176]{2,1,0:T(8,128)(2,1)S(1)}, bf16[2,80,2176]{2,1,0:T(8,128)(2,1)}, u32[]{:S(2)}, u32[]{:S(2)}) collective-permute-start(bf16[2,80,2176]{2,1,0:T(8,128)(2,1)S(1)} %get-tuple-element.198), channel_id=1, source_target_pairs={{0,2},{1,3},{2,0},{3,1},{4,6},{5,7},{6,4},{7,5},{8,10},{9,11},{10,... | collective-permute-start | bytes 2088968 | tf_op jit(solution)/shard_map/ppermute | solution.py:127
  708.8 46.7 %collective-permute-start.26 = (bf16[2,80,2048]{2,1,0:T(8,128)(2,1)S(1)}, bf16[2,80,2048]{2,1,0:T(8,128)(2,1)S(1)}, u32[]{:S(2)}, u32[]{:S(2)}) collective-permute-start(bf16[2,80,2048]{2,1,0:T(8,128)(2,1)S(1)} %get-tuple-element.137), channel_id=1, source_target_pairs={{0,2},{1,3},{2,0},{3,1},{4,6},{5,7},{6,4},{7,5},{8,10},{9,11},{10,... | collective-permute-start | bytes 1966088 | tf_op jit(solution)/shard_map/ppermute | solution.py:70
  708.9 38.0 %collective-permute-start.25 = (bf16[2,80,2048]{2,1,0:T(8,128)(2,1)S(1)}, bf16[2,80,2048]{2,1,0:T(8,128)(2,1)S(1)}, u32[]{:S(2)}, u32[]{:S(2)}) collective-permute-start(bf16[2,80,2048]{2,1,0:T(8,128)(2,1)S(1)} %get-tuple-element.137), channel_id=1, source_target_pairs={{0,1},{1,2},{2,3},{3,0},{4,5},{5,6},{6,7},{7,4},{8,9},{9,10},{10,1... | collective-permute-start | bytes 1966088 | tf_op jit(solution)/shard_map/ppermute | solution.py:70
  722.0 38.5 %collective-permute-start.27 = (bf16[2,80,2048]{2,1,0:T(8,128)(2,1)S(1)}, bf16[2,80,2048]{2,1,0:T(8,128)(2,1)S(1)}, u32[]{:S(2)}, u32[]{:S(2)}) collective-permute-start(bf16[2,80,2048]{2,1,0:T(8,128)(2,1)S(1)} %get-tuple-element.137), channel_id=1, source_target_pairs={{0,3},{1,0},{2,1},{3,2},{4,7},{5,4},{6,5},{7,6},{8,11},{9,8},{10,9... | collective-permute-start | bytes 1966088 | tf_op jit(solution)/shard_map/ppermute | solution.py:70
  773.9 38.5 %collective-permute-start.28 = (bf16[2,80,2048]{2,1,0:T(8,128)(2,1)}, bf16[2,80,2048]{2,1,0:T(8,128)(2,1)}, u32[]{:S(2)}, u32[]{:S(2)}) collective-permute-start(bf16[2,80,2048]{2,1,0:T(8,128)(2,1)} %get-tuple-element.202), channel_id=1, source_target_pairs={{0,1},{1,2},{2,3},{3,0},{4,5},{5,6},{6,7},{7,4},{8,9},{9,10},{10,1... | collective-permute-start | bytes 1966088 | tf_op jit(solution)/shard_map/ppermute | solution.py:127
  782.9 29.5 %collective-permute-start.30 = (bf16[2,80,2048]{2,1,0:T(8,128)(2,1)}, bf16[2,80,2048]{2,1,0:T(8,128)(2,1)}, u32[]{:S(2)}, u32[]{:S(2)}) collective-permute-start(bf16[2,80,2048]{2,1,0:T(8,128)(2,1)} %get-tuple-element.203), channel_id=1, source_target_pairs={{0,3},{1,0},{2,1},{3,2},{4,7},{5,4},{6,5},{7,6},{8,11},{9,8},{10,9... | collective-permute-start | bytes 1966088 | tf_op jit(solution)/shard_map/ppermute | solution.py:127
  783.3 50.2 %collective-permute-start.29 = (bf16[2,80,2048]{2,1,0:T(8,128)(2,1)}, bf16[2,80,2048]{2,1,0:T(8,128)(2,1)}, u32[]{:S(2)}, u32[]{:S(2)}) collective-permute-start(bf16[2,80,2048]{2,1,0:T(8,128)(2,1)} %get-tuple-element.204), channel_id=1, source_target_pairs={{0,2},{1,3},{2,0},{3,1},{4,6},{5,7},{6,4},{7,5},{8,10},{9,11},{10,... | collective-permute-start | bytes 1966088 | tf_op jit(solution)/shard_map/ppermute | solution.py:127
  934.1 19.8 %collective-permute-start.31 = (bf16[2,80,2048]{2,1,0:T(8,128)(2,1)}, bf16[2,80,2048]{2,1,0:T(8,128)(2,1)}, u32[]{:S(2)}, u32[]{:S(2)}) collective-permute-start(bf16[2,80,2048]{2,1,0:T(8,128)(2,1)} %get-tuple-element.199), channel_id=1, source_target_pairs={{0,1},{1,2},{2,3},{3,0},{4,5},{5,6},{6,7},{7,4},{8,9},{9,10},{10,1... | collective-permute-start | bytes 1966088 | tf_op jit(solution)/shard_map/ppermute | solution.py:127
  935.6 30.4 %collective-permute-start.33 = (bf16[2,80,2048]{2,1,0:T(8,128)(2,1)}, bf16[2,80,2048]{2,1,0:T(8,128)(2,1)}, u32[]{:S(2)}, u32[]{:S(2)}) collective-permute-start(bf16[2,80,2048]{2,1,0:T(8,128)(2,1)} %get-tuple-element.200), channel_id=1, source_target_pairs={{0,3},{1,0},{2,1},{3,2},{4,7},{5,4},{6,5},{7,6},{8,11},{9,8},{10,9... | collective-permute-start | bytes 1966088 | tf_op jit(solution)/shard_map/ppermute | solution.py:127
  937.9 56.7 %collective-permute-start.32 = (bf16[2,80,2048]{2,1,0:T(8,128)(2,1)}, bf16[2,80,2048]{2,1,0:T(8,128)(2,1)}, u32[]{:S(2)}, u32[]{:S(2)}) collective-permute-start(bf16[2,80,2048]{2,1,0:T(8,128)(2,1)} %get-tuple-element.201), channel_id=1, source_target_pairs={{0,2},{1,3},{2,0},{3,1},{4,6},{5,7},{6,4},{7,5},{8,10},{9,11},{10,... | collective-permute-start | bytes 1966088 | tf_op jit(solution)/shard_map/ppermute | solution.py:127
  1023.5 9.1 collective-permute-start.34
  1023.5 9.1 collective-permute-start.36
  1027.4 5.3 collective-permute-start.35
  (115 other events, 1153.6 us)
Sparse Core Ops, SparseCore 0:
  29.6 211.7 all-gather.2
  243.8 173.1 all-gather.4
  490.7 223.2 reduce-scatter.3
  717.6 210.7 reduce-scatter.5
  931.8 73.8 reduce-scatter.7

commit v2 on v1

--- a/solution.py
+++ b/solution.py
@@ -239,15 +239,7 @@
         down = weights[:, start + 2 * units : start + span]
         pick = picks_low[:, e]
         if e and e % PAIR == 0:
-            pick, packed, weighted_outs, gate_grad_slots, routed_grads = lax.optimization_barrier(
-                (
-                    pick,
-                    jnp.concatenate(pieces, axis=1),
-                    weighted_outs,
-                    gate_grad_slots,
-                    routed_grads,
-                )
-            )
+            pick, packed = lax.optimization_barrier((pick, jnp.concatenate(pieces, axis=1)))
             pair_grads.append(lax.psum_scatter(packed, "fsdp", scatter_dimension=0, tiled=True))
             pieces = []
         routed = dot("mst,mtd->msd", pick, hidden_two).astype(BF16).reshape(slots, width)
@@ -340,11 +332,19 @@
     )
     attn_packed, pair_grads, output = lax.optimization_barrier((attn_packed, pair_grads, output))
     attn_grads = lax.psum_scatter(attn_packed, "fsdp", scatter_dimension=0, tiled=True)
-    small_grads = tp_scatter(attn_grads[None, :, 4 * head_width :])[0]
-    attn_grads = attn_grads.astype(F32)
     expert_grads = [
         item[:, e * span : (e + 1) * span] for item in pair_grads for e in range(PAIR)
     ]
+    expert_grads = (
+        jnp.stack([item[:, :units] for item in expert_grads]).astype(F32),
+        jnp.stack([item[:, units : 2 * units] for item in expert_grads]).astype(F32),
+        jnp.stack([item[:, 2 * units :].T for item in expert_grads]).astype(F32),
+    )
+    small_grads, expert_grads = lax.optimization_barrier(
+        (attn_grads[None, :, 4 * head_width :], expert_grads)
+    )
+    small_grads = tp_scatter(small_grads)[0]
+    attn_grads = attn_grads.astype(F32)
     return (
         output,
         input_grad,
@@ -355,9 +355,7 @@
         attn_grads[:, 3 * head_width : 4 * head_width].T,
         small_grads[:, 1],
         small_grads[:, 2:small_width],
-        jnp.stack([item[:, :units] for item in expert_grads]).astype(F32),
-        jnp.stack([item[:, units : 2 * units] for item in expert_grads]).astype(F32),
-        jnp.stack([item[:, 2 * units :].T for item in expert_grads]).astype(F32),
+        *expert_grads,
     )
 
 

time: 1050 us -> 1010 us (0.962)
  waiting for transfers between devices: 448 us -> 417 us
    reduce_scatter x2, waiting for transfers between devices: 91.9 us -> 53.9 us  [per_device(): lax.psum_scatter(packed, 'fsdp', scatter_dimension=0, tiled=True)]
    unnamed x272 -> x286, local copies, waits for them, and re-layouts: 56.1 us -> 56.8 us
  transfers between devices with their start and end apart: 42 -> 42, of which waited for: 25 -> 24; matrix products, arithmetic and copies ran while one was open for 42% -> 43% of each run, Pallas kernels for 0% -> 0%
where the time goes in v2:
time: 1010 us; the launch traced here: 999 us
  waiting for transfers between devices  417 us (41%)
  matrix products  252 us (25%)
  local copies, waits for them, and re-layouts  115 us (11%)
  other arithmetic  104 us (10%)
  starting transfers between devices  95.2 us (9%)
  between operations  16.1 us (2%)
    dot_general x47, matrix products, dot(): return jnp.einsum(spec, a, b, preferred_element_type=F32)  245 us
    ppermute x15, waiting for transfers between devices, tp_scatter(): lax.ppermute(piece, 'tp', [(i, (i + k) % count) for i in range(count)])  184 us
    ppermute x12, waiting for transfers between devices, tp_gather(): lax.ppermute(own, 'tp', [(i, (i + k) % count) for i in range(count)])  100 us
    ppermute x7, waiting for transfers between devices, swap(): return lax.ppermute(value, 'fsdp', [(i, i ^ bits(i)) for i in range(count)])  69.9 us
    unnamed x286, local copies, waits for them, and re-layouts  56.8 us
    reduce_scatter x2, waiting for transfers between devices, per_device(): lax.psum_scatter(packed, 'fsdp', scatter_dimension=0, tiled=True)  53.9 us
    concatenate x2, other arithmetic, per_device(): jnp.concatenate(pieces, axis=1)  48 us
    ppermute x12, starting transfers between devices, tp_gather(): lax.ppermute(own, 'tp', [(i, (i + k) % count) for i in range(count)])  44.6 us
  transfers between devices with their start and end apart: 42, of which 24 were waited for; matrix products, arithmetic and copies ran while one was open for 43% of the time, Pallas kernels for 0%

profile of v2, /device:TPU:0, one launch (start us, length us, event | category | flops | bytes accessed | tf_op | source)
XLA Modules:
  0.0 998.7 jit_solution(8319804219602799)
XLA Ops:
  64.7 41.2 %collective-permute-done.1 = bf16[256,2176]{1,0:T(8,128)(2,1)S(1)} collective-permute-done((bf16[256,2176]{1,0:T(8,128)(2,1)}, bf16[256,2176]{1,0:T(8,128)(2,1)S(1)}, u32[]{:S(2)}, u32[]{:S(2)}) %collective-permute-start.1) | collective-permute-done | bytes 1114144 | tf_op jit(solution)/shard_map/ppermute | solution.py:104
  112.5 10.5 %collective-permute-done.2 = bf16[2,80,2048]{2,1,0:T(8,128)(2,1)S(1)} collective-permute-done((bf16[2,80,2048]{2,1,0:T(8,128)(2,1)S(1)}, bf16[2,80,2048]{2,1,0:T(8,128)(2,1)S(1)}, u32[]{:S(2)}, u32[]{:S(2)}) %collective-permute-start.2) | collective-permute-done | bytes 655392 | tf_op jit(solution)/shard_map/ppermute | solution.py:70
  123.0 14.4 %collective-permute-start.4 = (bf16[2,80,2048]{2,1,0:T(8,128)(2,1)S(1)}, bf16[2,80,2048]{2,1,0:T(8,128)(2,1)S(1)}, u32[]{:S(2)}, u32[]{:S(2)}) collective-permute-start(bf16[2,80,2048]{2,1,0:T(8,128)(2,1)S(1)} %copy-done.16), channel_id=1, source_target_pairs={{0,3},{1,0},{2,1},{3,2},{4,7},{5,4},{6,5},{7,6},{8,11},{9,8},{10,9... | collective-permute-start | bytes 1966088 | tf_op jit(solution)/shard_map/ppermute | solution.py:70
  140.5 10.5 %collective-permute-done.4 = bf16[2,80,2048]{2,1,0:T(8,128)(2,1)S(1)} collective-permute-done((bf16[2,80,2048]{2,1,0:T(8,128)(2,1)S(1)}, bf16[2,80,2048]{2,1,0:T(8,128)(2,1)S(1)}, u32[]{:S(2)}, u32[]{:S(2)}) %collective-permute-start.4) | collective-permute-done | bytes 655392 | tf_op jit(solution)/shard_map/ppermute | solution.py:70
  151.8 25.3 %collective-permute-done.8 = bf16[256,2176]{1,0:T(8,128)(2,1)S(1)} collective-permute-done((bf16[256,2176]{1,0:T(8,128)(2,1)S(1)}, bf16[256,2176]{1,0:T(8,128)(2,1)S(1)}, u32[]{:S(2)}, u32[]{:S(2)}) %collective-permute-start.8) | collective-permute-done | bytes 1114144 | tf_op jit(solution)/shard_map/ppermute | solution.py:104
  239.4 12.3 %collective-permute-done.13 = bf16[2,80,2048]{2,1,0:T(8,128)(2,1)S(1)} collective-permute-done((bf16[2,80,2048]{2,1,0:T(8,128)(2,1)S(1)}, bf16[2,80,2048]{2,1,0:T(8,128)(2,1)S(1)}, u32[]{:S(2)}, u32[]{:S(2)}) %collective-permute-start.13) | collective-permute-done | bytes 655392 | tf_op jit(solution)/shard_map/ppermute | solution.py:127
  252.6 11.4 %collective-permute-done.15 = bf16[2,80,2048]{2,1,0:T(8,128)(2,1)S(1)} collective-permute-done((bf16[2,80,2048]{2,1,0:T(8,128)(2,1)S(1)}, bf16[2,80,2048]{2,1,0:T(8,128)(2,1)S(1)}, u32[]{:S(2)}, u32[]{:S(2)}) %collective-permute-start.15) | collective-permute-done | bytes 655392 | tf_op jit(solution)/shard_map/ppermute | solution.py:127
  264.0 27.5 %collective-permute-done.14 = bf16[2,80,2048]{2,1,0:T(8,128)(2,1)S(1)} collective-permute-done((bf16[2,80,2048]{2,1,0:T(8,128)(2,1)S(1)}, bf16[2,80,2048]{2,1,0:T(8,128)(2,1)S(1)}, u32[]{:S(2)}, u32[]{:S(2)}) %collective-permute-start.14) | collective-permute-done | bytes 655392 | tf_op jit(solution)/shard_map/ppermute | solution.py:127
  293.0 13.4 %collective-permute-start.16 = (bf16[2,80,2048]{2,1,0:T(8,128)(2,1)S(1)}, bf16[2,80,2048]{2,1,0:T(8,128)(2,1)S(1)}, u32[]{:S(2)}, u32[]{:S(2)}) collective-permute-start(bf16[2,80,2048]{2,1,0:T(8,128)(2,1)S(1)} %get-tuple-element.139), channel_id=1, source_target_pairs={{0,1},{1,2},{2,3},{3,0},{4,5},{5,6},{6,7},{7,4},{8,9},{9,10},{10,1... | collective-permute-start | bytes 1966088 | tf_op jit(solution)/shard_map/ppermute | solution.py:70
  312.6 12.3 %collective-permute-done.16 = bf16[2,80,2048]{2,1,0:T(8,128)(2,1)S(1)} collective-permute-done((bf16[2,80,2048]{2,1,0:T(8,128)(2,1)S(1)}, bf16[2,80,2048]{2,1,0:T(8,128)(2,1)S(1)}, u32[]{:S(2)}, u32[]{:S(2)}) %collective-permute-start.16) | collective-permute-done | bytes 655392 | tf_op jit(solution)/shard_map/ppermute | solution.py:70
  325.0 26.1 %collective-permute-done.17 = bf16[2,80,2048]{2,1,0:T(8,128)(2,1)S(1)} collective-permute-done((bf16[2,80,2048]{2,1,0:T(8,128)(2,1)S(1)}, bf16[2,80,2048]{2,1,0:T(8,128)(2,1)S(1)}, u32[]{:S(2)}, u32[]{:S(2)}) %collective-permute-start.17) | collective-permute-done | bytes 655392 | tf_op jit(solution)/shard_map/ppermute | solution.py:70
  370.0 8.7 fusion.11
  378.7 6.1 multiply_convert_fusion.17
  384.9 5.3 convolution_convert_fusion.7
  390.2 8.9 fusion.15
  399.1 6.1 multiply_convert_fusion.20
  405.2 5.6 convolution_convert_fusion.8
  410.9 8.9 convolution_convert_fusion.3
  419.8 8.9 convolution_convert_fusion.2
  428.7 23.8 %pad_maximum_fusion = bf16[2048,8448]{1,0:T(8,128)(2,1)} fusion(bf16[2048,1408]{1,0:T(8,128)(2,1)} %convolution_convert_fusion.7, bf16[2048,2816]{1,0:T(8,128)(2,1)} %convolution_convert_fusion.2, bf16[2048,1408]{1,0:T(8,128)(2,1)} %convolution_convert_fusion.8, bf16[2048,2816]{1,0:T(8,128)(2,1)} %convolution_convert_fusion.3), kind=kLoop, calls=%fused_computation.1 | loop fusion | flops 138412032 | bytes 69206016 | tf_op jit(solution)/shard_map/concatenate | solution.py:242
  463.4 8.9 fusion.3
  472.3 8.3 multiply_convert_fusion.11
  480.6 5.3 convolution_convert_fusion.5
  485.9 9.6 fusion.7
  495.5 7.2 multiply_convert_fusion.14
  502.7 5.7 convolution_convert_fusion.6
  508.4 8.9 convolution_convert_fusion.1
  517.4 8.9 convolution_convert_fusion
  526.3 24.3 %pad_maximum_fusion.1 = bf16[2048,8448]{1,0:T(8,128)(2,1)} fusion(bf16[2048,1408]{1,0:T(8,128)(2,1)} %convolution_convert_fusion.5, bf16[2048,2816]{1,0:T(8,128)(2,1)} %convolution_convert_fusion, bf16[2048,1408]{1,0:T(8,128)(2,1)} %convolution_convert_fusion.6, bf16[2048,2816]{1,0:T(8,128)(2,1)} %convolution_convert_fusion.1), kind=kLoop, calls=%fused_computation.2 | loop fusion | flops 138412032 | bytes 69206016 | tf_op jit(solution)/shard_map/concatenate | solution.py:273
  579.7 10.0 %fusion.77 = bf16[400,2048]{1,0:T(8,128)(2,1)S(1)} fusion(bf16[2048,8448]{0,1:T(8,128)(2,1)} %all-gather.5.cloned.1.call-done, bf16[400,1408]{1,0:T(8,128)(2,1)S(1)} %copy-done.122, bf16[400,1408]{1,0:T(8,128)(2,1)S(1)} %copy-done.120), kind=kOutput, calls=%fused_computation.102 | convolution fusion | flops 4619059200 | bytes 15425536 | tf_op jit(solution)/shard_map/sf,df->sd/dot_general | solution.py:133
  589.8 9.8 fusion.71
  599.7 9.7 fusion.68
  609.3 9.6 fusion.74
  625.7 16.5 %collective-permute-start.22 = (bf16[2,80,2176]{2,1,0:T(8,128)(2,1)}, bf16[2,80,2176]{2,1,0:T(8,128)(2,1)}, u32[]{:S(2)}, u32[]{:S(2)}) collective-permute-start(bf16[2,80,2176]{2,1,0:T(8,128)(2,1)} %get-tuple-element.192), channel_id=1, source_target_pairs={{0,1},{1,2},{2,3},{3,0},{4,5},{5,6},{6,7},{7,4},{8,9},{9,10},{10,1... | collective-permute-start | bytes 2088968 | tf_op jit(solution)/shard_map/ppermute | solution.py:127
  645.4 13.1 %collective-permute-done.22 = bf16[2,80,2176]{2,1,0:T(8,128)(2,1)} collective-permute-done((bf16[2,80,2176]{2,1,0:T(8,128)(2,1)}, bf16[2,80,2176]{2,1,0:T(8,128)(2,1)}, u32[]{:S(2)}, u32[]{:S(2)}) %collective-permute-start.22) | collective-permute-done | bytes 696352 | tf_op jit(solution)/shard_map/ppermute | solution.py:127
  658.5 15.0 %collective-permute-done.24 = bf16[2,80,2176]{2,1,0:T(8,128)(2,1)} collective-permute-done((bf16[2,80,2176]{2,1,0:T(8,128)(2,1)}, bf16[2,80,2176]{2,1,0:T(8,128)(2,1)}, u32[]{:S(2)}, u32[]{:S(2)}) %collective-permute-start.24) | collective-permute-done | bytes 696352 | tf_op jit(solution)/shard_map/ppermute | solution.py:127
  673.4 27.8 %collective-permute-done.23 = bf16[2,80,2176]{2,1,0:T(8,128)(2,1)} collective-permute-done((bf16[2,80,2176]{2,1,0:T(8,128)(2,1)S(1)}, bf16[2,80,2176]{2,1,0:T(8,128)(2,1)}, u32[]{:S(2)}, u32[]{:S(2)}) %collective-permute-start.23) | collective-permute-done | bytes 696352 | tf_op jit(solution)/shard_map/ppermute | solution.py:127
  708.1 5.5 collective-permute-start.25
  718.8 24.0 %collective-permute-done.25 = bf16[2,80,2048]{2,1,0:T(8,128)(2,1)S(1)} collective-permute-done((bf16[2,80,2048]{2,1,0:T(8,128)(2,1)S(1)}, bf16[2,80,2048]{2,1,0:T(8,128)(2,1)S(1)}, u32[]{:S(2)}, u32[]{:S(2)}) %collective-permute-start.25) | collective-permute-done | bytes 655392 | tf_op jit(solution)/shard_map/ppermute | solution.py:70
  742.8 11.8 %collective-permute-done.26 = bf16[2,80,2048]{2,1,0:T(8,128)(2,1)S(1)} collective-permute-done((bf16[2,80,2048]{2,1,0:T(8,128)(2,1)S(1)}, bf16[2,80,2048]{2,1,0:T(8,128)(2,1)S(1)}, u32[]{:S(2)}, u32[]{:S(2)}) %collective-permute-start.26) | collective-permute-done | bytes 655392 | tf_op jit(solution)/shard_map/ppermute | solution.py:70
  772.8 8.8 collective-permute-start.28
  801.6 5.7 convolution_convert_fusion.4
  811.5 21.0 %collective-permute-done.29 = bf16[2,80,2048]{2,1,0:T(8,128)(2,1)} collective-permute-done((bf16[2,80,2048]{2,1,0:T(8,128)(2,1)}, bf16[2,80,2048]{2,1,0:T(8,128)(2,1)}, u32[]{:S(2)}, u32[]{:S(2)}) %collective-permute-start.29) | collective-permute-done | bytes 655392 | tf_op jit(solution)/shard_map/ppermute | solution.py:127
  835.5 53.9 %reduce-scatter.6.cloned.1.call-done = bf16[256,8448]{1,0:T(8,128)(2,1)} async-done(((bf16[2048,8448]{1,0:T(8,128)(2,1)}), bf16[256,8448]{1,0:T(8,128)(2,1)}) %reduce-scatter.6.cloned.1.call-update) | async-done | bytes 4325392 | tf_op jit(solution)/shard_map/reduce_scatter | solution.py:274
  899.6 15.3 %collective-permute-done.31 = bf16[2,80,2048]{2,1,0:T(8,128)(2,1)} collective-permute-done((bf16[2,80,2048]{2,1,0:T(8,128)(2,1)}, bf16[2,80,2048]{2,1,0:T(8,128)(2,1)}, u32[]{:S(2)}, u32[]{:S(2)}) %collective-permute-start.31) | collective-permute-done | bytes 655392 | tf_op jit(solution)/shard_map/ppermute | solution.py:127
  914.9 12.1 %collective-permute-done.33 = bf16[2,80,2048]{2,1,0:T(8,128)(2,1)} collective-permute-done((bf16[2,80,2048]{2,1,0:T(8,128)(2,1)}, bf16[2,80,2048]{2,1,0:T(8,128)(2,1)}, u32[]{:S(2)}, u32[]{:S(2)}) %collective-permute-start.33) | collective-permute-done | bytes 655392 | tf_op jit(solution)/shard_map/ppermute | solution.py:127
  927.0 28.7 %collective-permute-done.32 = bf16[2,80,2048]{2,1,0:T(8,128)(2,1)} collective-permute-done((bf16[2,80,2048]{2,1,0:T(8,128)(2,1)}, bf16[2,80,2048]{2,1,0:T(8,128)(2,1)}, u32[]{:S(2)}, u32[]{:S(2)}) %collective-permute-start.32) | collective-permute-done | bytes 655392 | tf_op jit(solution)/shard_map/ppermute | solution.py:127
  984.5 6.2 copy.420
  (510 shorter events, 304.0 us)
Async XLA Ops:
  7.2 362.8 %all-gather.3.cloned.1.call-start = ((), (), s32[]{:S(2)}) async-start(), calls=%async_computation.3 | async-start | bytes 38928384 | tf_op jit(solution)/shard_map/all_gather | solution.py:180
  29.4 434.0 %all-gather.5.cloned.1.call-start = ((), (), s32[]{:S(2)}) async-start(), calls=%async_computation.4 | async-start | bytes 38928384 | tf_op jit(solution)/shard_map/all_gather | solution.py:180
  45.3 790.2 %reduce-scatter.4.cloned.1.call-start = ((), (), s32[]{:S(2)}) async-start(), calls=%async_computation.5 | async-start | bytes 38928384 | tf_op jit(solution)/shard_map/reduce_scatter | solution.py:243
  45.3 265.6 %collective-permute-start.20 = (bf16[2,80,2048]{2,1,0:T(8,128)(2,1)}, bf16[2,80,2048]{2,1,0:T(8,128)(2,1)}, u32[]{:S(2)}, u32[]{:S(2)}) collective-permute-start(bf16[2,80,2048]{2,1,0:T(8,128)(2,1)} %param.15), channel_id=1, source_target_pairs={{0,2},{1,3},{2,0},{3,1},{4,6},{5,7},{6,4},{7,5},{8,10},{9,11},{10,... | collective-permute-start | bytes 1966088 | tf_op jit(solution)/shard_map/ppermute | solution.py:70
  49.5 256.9 %collective-permute-start.19 = (bf16[2,80,2048]{2,1,0:T(8,128)(2,1)}, bf16[2,80,2048]{2,1,0:T(8,128)(2,1)}, u32[]{:S(2)}, u32[]{:S(2)}) collective-permute-start(bf16[2,80,2048]{2,1,0:T(8,128)(2,1)} %param.15), channel_id=1, source_target_pairs={{0,1},{1,2},{2,3},{3,0},{4,5},{5,6},{6,7},{7,4},{8,9},{9,10},{10,1... | collective-permute-start | bytes 1966088 | tf_op jit(solution)/shard_map/ppermute | solution.py:70
  54.9 51.0 %collective-permute-start.1 = (bf16[256,2176]{1,0:T(8,128)(2,1)}, bf16[256,2176]{1,0:T(8,128)(2,1)S(1)}, u32[]{:S(2)}, u32[]{:S(2)}) collective-permute-start(bf16[256,2176]{1,0:T(8,128)(2,1)} %pad_dynamic-update-slice_fusion), channel_id=1, source_target_pairs={{0,16},{4,20},{8,24},{12,28},{16,0},{20,4},{24,8},{28,12},{1,17},{... | collective-permute-start | bytes 3342344 | tf_op jit(solution)/shard_map/ppermute | solution.py:104
  56.5 50.9 %collective-permute-start = (bf16[256,2176]{1,0:T(8,128)(2,1)}, bf16[256,2176]{1,0:T(8,128)(2,1)S(1)}, u32[]{:S(2)}, u32[]{:S(2)}) collective-permute-start(bf16[256,2176]{1,0:T(8,128)(2,1)} %pad_dynamic-update-slice_fusion), channel_id=1, source_target_pairs={{0,8},{4,12},{8,0},{12,4},{16,24},{20,28},{24,16},{28,20},{1,9},{5... | collective-permute-start | bytes 3342344 | tf_op jit(solution)/shard_map/ppermute | solution.py:104
  58.0 79.5 %collective-permute-start.3 = (bf16[2,80,2048]{2,1,0:T(8,128)(2,1)S(1)}, bf16[2,80,2048]{2,1,0:T(8,128)(2,1)}, u32[]{:S(2)}, u32[]{:S(2)}) collective-permute-start(bf16[2,80,2048]{2,1,0:T(8,128)(2,1)S(1)} %copy-done.16), channel_id=1, source_target_pairs={{0,2},{1,3},{2,0},{3,1},{4,6},{5,7},{6,4},{7,5},{8,10},{9,11},{10,... | collective-permute-start | bytes 1966088 | tf_op jit(solution)/shard_map/ppermute | solution.py:70
  60.0 297.7 %copy-start.77 = (s32[2,4,320]{2,0,1:T(2,128)}, s32[2,4,320]{2,0,1:T(2,128)S(1)}, u32[]{:S(2)}) copy-start(s32[2,4,320]{2,0,1:T(2,128)S(1)} %copy.382) | copy-start | bytes 30724
  105.9 17.1 %collective-permute-start.2 = (bf16[2,80,2048]{2,1,0:T(8,128)(2,1)S(1)}, bf16[2,80,2048]{2,1,0:T(8,128)(2,1)S(1)}, u32[]{:S(2)}, u32[]{:S(2)}) collective-permute-start(bf16[2,80,2048]{2,1,0:T(8,128)(2,1)S(1)} %copy-done.16), channel_id=1, source_target_pairs={{0,1},{1,2},{2,3},{3,0},{4,5},{5,6},{6,7},{7,4},{8,9},{9,10},{10,1... | collective-permute-start | bytes 1966088 | tf_op jit(solution)/shard_map/ppermute | solution.py:70
  107.4 32.9 %collective-permute-start.5 = (bf16[256,2176]{1,0:T(8,128)(2,1)}, bf16[256,2176]{1,0:T(8,128)(2,1)S(1)}, u32[]{:S(2)}, u32[]{:S(2)}) collective-permute-start(bf16[256,2176]{1,0:T(8,128)(2,1)} %pad_dynamic-update-slice_fusion), channel_id=1, source_target_pairs={{0,4},{4,0},{8,12},{12,8},{16,20},{20,16},{24,28},{28,24},{1,5},{5... | collective-permute-start | bytes 3342344 | tf_op jit(solution)/shard_map/ppermute | solution.py:104
  123.0 28.0 %collective-permute-start.4 = (bf16[2,80,2048]{2,1,0:T(8,128)(2,1)S(1)}, bf16[2,80,2048]{2,1,0:T(8,128)(2,1)S(1)}, u32[]{:S(2)}, u32[]{:S(2)}) collective-permute-start(bf16[2,80,2048]{2,1,0:T(8,128)(2,1)S(1)} %copy-done.16), channel_id=1, source_target_pairs={{0,3},{1,0},{2,1},{3,2},{4,7},{5,4},{6,5},{7,6},{8,11},{9,8},{10,9... | collective-permute-start | bytes 1966088 | tf_op jit(solution)/shard_map/ppermute | solution.py:70
  137.5 39.6 %collective-permute-start.8 = (bf16[256,2176]{1,0:T(8,128)(2,1)S(1)}, bf16[256,2176]{1,0:T(8,128)(2,1)S(1)}, u32[]{:S(2)}, u32[]{:S(2)}) collective-permute-start(bf16[256,2176]{1,0:T(8,128)(2,1)S(1)} %broadcast_select_fusion), channel_id=1, source_target_pairs={{0,8},{4,20},{8,0},{12,28},{16,24},{20,4},{24,16},{28,12},{1,9},{5... | collective-permute-start | bytes 3342344 | tf_op jit(solution)/shard_map/ppermute | solution.py:104
  140.2 37.1 %collective-permute-start.7 = (bf16[256,2176]{1,0:T(8,128)(2,1)S(1)}, bf16[256,2176]{1,0:T(8,128)(2,1)S(1)}, u32[]{:S(2)}, u32[]{:S(2)}) collective-permute-start(bf16[256,2176]{1,0:T(8,128)(2,1)S(1)} %copy-done.22), channel_id=1, source_target_pairs={{0,4},{4,0},{8,12},{12,8},{16,20},{20,16},{24,28},{28,24},{1,5},{5... | collective-permute-start | bytes 3342344 | tf_op jit(solution)/shard_map/ppermute | solution.py:104
  151.0 26.1 %collective-permute-start.6 = (bf16[256,2176]{1,0:T(8,128)(2,1)S(1)}, bf16[256,2176]{1,0:T(8,128)(2,1)S(1)}, u32[]{:S(2)}, u32[]{:S(2)}) collective-permute-start(bf16[256,2176]{1,0:T(8,128)(2,1)S(1)} %copy-done.24), channel_id=1, source_target_pairs={{0,4},{4,0},{8,12},{12,8},{16,20},{20,16},{24,28},{28,24},{1,5},{5... | collective-permute-start | bytes 3342344 | tf_op jit(solution)/shard_map/ppermute | solution.py:104
  177.1 2.8 collective-permute-start.9
  180.0 8.3 collective-permute-start.12
  180.1 12.9 %collective-permute-start.11 = (bf16[512,128]{1,0:T(8,128)(2,1)S(1)}, bf16[512,128]{1,0:T(8,128)(2,1)S(1)}, u32[]{:S(2)}, u32[]{:S(2)}) collective-permute-start(bf16[512,128]{1,0:T(8,128)(2,1)S(1)} %bitcast.322), channel_id=1, source_target_pairs={{0,2},{1,3},{2,0},{3,1},{4,6},{5,7},{6,4},{7,5},{8,10},{9,11},{10,... | collective-permute-start | bytes 393224 | tf_op jit(solution)/shard_map/ppermute | solution.py:83
  182.0 11.1 %collective-permute-start.10 = (bf16[512,128]{1,0:T(8,128)(2,1)S(1)}, bf16[512,128]{1,0:T(8,128)(2,1)S(1)}, u32[]{:S(2)}, u32[]{:S(2)}) collective-permute-start(bf16[512,128]{1,0:T(8,128)(2,1)S(1)} %bitcast.323), channel_id=1, source_target_pairs={{0,3},{1,0},{2,1},{3,2},{4,7},{5,4},{6,5},{7,6},{8,11},{9,8},{10,9... | collective-permute-start | bytes 393224 | tf_op jit(solution)/shard_map/ppermute | solution.py:83
  193.3 158.0 %copy-start.13 = (bf16[8,4,64,128]{3,2,1,0:T(8,128)(2,1)}, bf16[8,4,64,128]{3,2,1,0:T(8,128)(2,1)S(1)}, u32[]{:S(2)}) copy-start(bf16[8,4,64,128]{3,2,1,0:T(8,128)(2,1)S(1)} %copy.374) | copy-start | bytes 1572868
  193.8 99.0 %copy-start.75 = (f32[2048]{0:T(1024)}, f32[2048]{0:T(1024)S(1)}, u32[]{:S(2)}) copy-start(f32[2048]{0:T(1024)S(1)} %get-tuple-element.130) | copy-start | bytes 24580
  232.2 19.5 %collective-permute-start.13 = (bf16[2,80,2048]{2,1,0:T(8,128)(2,1)S(1)}, bf16[2,80,2048]{2,1,0:T(8,128)(2,1)S(1)}, u32[]{:S(2)}, u32[]{:S(2)}) collective-permute-start(bf16[2,80,2048]{2,1,0:T(8,128)(2,1)S(1)} %get-tuple-element.201), channel_id=1, source_target_pairs={{0,1},{1,2},{2,3},{3,0},{4,5},{5,6},{6,7},{7,4},{8,9},{9,10},{10,1... | collective-permute-start | bytes 1966088 | tf_op jit(solution)/shard_map/ppermute | solution.py:127
  234.8 29.2 %collective-permute-start.15 = (bf16[2,80,2048]{2,1,0:T(8,128)(2,1)S(1)}, bf16[2,80,2048]{2,1,0:T(8,128)(2,1)S(1)}, u32[]{:S(2)}, u32[]{:S(2)}) collective-permute-start(bf16[2,80,2048]{2,1,0:T(8,128)(2,1)S(1)} %get-tuple-element.202), channel_id=1, source_target_pairs={{0,3},{1,0},{2,1},{3,2},{4,7},{5,4},{6,5},{7,6},{8,11},{9,8},{10,9... | collective-permute-start | bytes 1966088 | tf_op jit(solution)/shard_map/ppermute | solution.py:127
  236.0 55.4 %collective-permute-start.14 = (bf16[2,80,2048]{2,1,0:T(8,128)(2,1)S(1)}, bf16[2,80,2048]{2,1,0:T(8,128)(2,1)S(1)}, u32[]{:S(2)}, u32[]{:S(2)}) collective-permute-start(bf16[2,80,2048]{2,1,0:T(8,128)(2,1)S(1)} %get-tuple-element.203), channel_id=1, source_target_pairs={{0,2},{1,3},{2,0},{3,1},{4,6},{5,7},{6,4},{7,5},{8,10},{9,11},{10,... | collective-permute-start | bytes 1966088 | tf_op jit(solution)/shard_map/ppermute | solution.py:127
  237.7 220.3 %copy-start.37 = (bf16[2,200,320]{2,1,0:T(8,128)(2,1)}, bf16[2,200,320]{2,1,0:T(8,128)(2,1)S(1)}, u32[]{:S(2)}) copy-start(bf16[2,200,320]{2,1,0:T(8,128)(2,1)S(1)} %slice_bitcast_fusion.29) | copy-start | bytes 768004
  251.7 60.9 %collective-permute-start.21 = (bf16[2,80,2048]{2,1,0:T(8,128)(2,1)}, bf16[2,80,2048]{2,1,0:T(8,128)(2,1)S(1)}, u32[]{:S(2)}, u32[]{:S(2)}) collective-permute-start(bf16[2,80,2048]{2,1,0:T(8,128)(2,1)} %param.15), channel_id=1, source_target_pairs={{0,3},{1,0},{2,1},{3,2},{4,7},{5,4},{6,5},{7,6},{8,11},{9,8},{10,9... | collective-permute-start | bytes 1966088 | tf_op jit(solution)/shard_map/ppermute | solution.py:70
  293.0 31.9 %collective-permute-start.16 = (bf16[2,80,2048]{2,1,0:T(8,128)(2,1)S(1)}, bf16[2,80,2048]{2,1,0:T(8,128)(2,1)S(1)}, u32[]{:S(2)}, u32[]{:S(2)}) collective-permute-start(bf16[2,80,2048]{2,1,0:T(8,128)(2,1)S(1)} %get-tuple-element.139), channel_id=1, source_target_pairs={{0,1},{1,2},{2,3},{3,0},{4,5},{5,6},{6,7},{7,4},{8,9},{9,10},{10,1... | collective-permute-start | bytes 1966088 | tf_op jit(solution)/shard_map/ppermute | solution.py:70
  307.5 43.6 %collective-permute-start.17 = (bf16[2,80,2048]{2,1,0:T(8,128)(2,1)S(1)}, bf16[2,80,2048]{2,1,0:T(8,128)(2,1)S(1)}, u32[]{:S(2)}, u32[]{:S(2)}) collective-permute-start(bf16[2,80,2048]{2,1,0:T(8,128)(2,1)S(1)} %get-tuple-element.139), channel_id=1, source_target_pairs={{0,2},{1,3},{2,0},{3,1},{4,6},{5,7},{6,4},{7,5},{8,10},{9,11},{10,... | collective-permute-start | bytes 1966088 | tf_op jit(solution)/shard_map/ppermute | solution.py:70
  312.3 38.9 %collective-permute-start.18 = (bf16[2,80,2048]{2,1,0:T(8,128)(2,1)S(1)}, bf16[2,80,2048]{2,1,0:T(8,128)(2,1)S(1)}, u32[]{:S(2)}, u32[]{:S(2)}) collective-permute-start(bf16[2,80,2048]{2,1,0:T(8,128)(2,1)S(1)} %get-tuple-element.139), channel_id=1, source_target_pairs={{0,3},{1,0},{2,1},{3,2},{4,7},{5,4},{6,5},{7,6},{8,11},{9,8},{10,9... | collective-permute-start | bytes 1966088 | tf_op jit(solution)/shard_map/ppermute | solution.py:70
  452.5 437.0 %reduce-scatter.6.cloned.1.call-start = ((), (), s32[]{:S(2)}) async-start(), calls=%async_computation.6 | async-start | bytes 38928384 | tf_op jit(solution)/shard_map/reduce_scatter | solution.py:274
  550.6 423.8 %reduce-scatter.8.cloned.1.call-start = ((), (), s32[]{:S(2)}) async-start(), calls=%async_computation.7 | async-start | bytes 10027008 | tf_op jit(solution)/shard_map/reduce_scatter | solution.py:334
  625.7 78.5 %copy-start.76 = (f32[2048]{0:T(1024)S(1)}, f32[2048]{0:T(1024)}, u32[]{:S(2)}) copy-start(f32[2048]{0:T(1024)} %copy-done.75) | copy-start | bytes 24580
  625.7 78.5 %copy-start.91 = (f32[2,80]{1,0:T(2,128)S(1)}, f32[2,80]{1,0:T(2,128)}, u32[]{:S(2)}) copy-start(f32[2,80]{1,0:T(2,128)} %copy-done.90) | copy-start | bytes 1924
  625.7 32.8 %collective-permute-start.22 = (bf16[2,80,2176]{2,1,0:T(8,128)(2,1)}, bf16[2,80,2176]{2,1,0:T(8,128)(2,1)}, u32[]{:S(2)}, u32[]{:S(2)}) collective-permute-start(bf16[2,80,2176]{2,1,0:T(8,128)(2,1)} %get-tuple-element.192), channel_id=1, source_target_pairs={{0,1},{1,2},{2,3},{3,0},{4,5},{5,6},{6,7},{7,4},{8,9},{9,10},{10,1... | collective-permute-start | bytes 2088968 | tf_op jit(solution)/shard_map/ppermute | solution.py:127
  642.1 31.3 %collective-permute-start.24 = (bf16[2,80,2176]{2,1,0:T(8,128)(2,1)}, bf16[2,80,2176]{2,1,0:T(8,128)(2,1)}, u32[]{:S(2)}, u32[]{:S(2)}) collective-permute-start(bf16[2,80,2176]{2,1,0:T(8,128)(2,1)} %get-tuple-element.193), channel_id=1, source_target_pairs={{0,3},{1,0},{2,1},{3,2},{4,7},{5,4},{6,5},{7,6},{8,11},{9,8},{10,9... | collective-permute-start | bytes 2088968 | tf_op jit(solution)/shard_map/ppermute | solution.py:127
  642.2 59.1 %collective-permute-start.23 = (bf16[2,80,2176]{2,1,0:T(8,128)(2,1)S(1)}, bf16[2,80,2176]{2,1,0:T(8,128)(2,1)}, u32[]{:S(2)}, u32[]{:S(2)}) collective-permute-start(bf16[2,80,2176]{2,1,0:T(8,128)(2,1)S(1)} %get-tuple-element.194), channel_id=1, source_target_pairs={{0,2},{1,3},{2,0},{3,1},{4,6},{5,7},{6,4},{7,5},{8,10},{9,11},{10,... | collective-permute-start | bytes 2088968 | tf_op jit(solution)/shard_map/ppermute | solution.py:127
  708.0 46.7 %collective-permute-start.26 = (bf16[2,80,2048]{2,1,0:T(8,128)(2,1)S(1)}, bf16[2,80,2048]{2,1,0:T(8,128)(2,1)S(1)}, u32[]{:S(2)}, u32[]{:S(2)}) collective-permute-start(bf16[2,80,2048]{2,1,0:T(8,128)(2,1)S(1)} %get-tuple-element.133), channel_id=1, source_target_pairs={{0,2},{1,3},{2,0},{3,1},{4,6},{5,7},{6,4},{7,5},{8,10},{9,11},{10,... | collective-permute-start | bytes 1966088 | tf_op jit(solution)/shard_map/ppermute | solution.py:70
  708.1 34.7 %collective-permute-start.25 = (bf16[2,80,2048]{2,1,0:T(8,128)(2,1)S(1)}, bf16[2,80,2048]{2,1,0:T(8,128)(2,1)S(1)}, u32[]{:S(2)}, u32[]{:S(2)}) collective-permute-start(bf16[2,80,2048]{2,1,0:T(8,128)(2,1)S(1)} %get-tuple-element.133), channel_id=1, source_target_pairs={{0,1},{1,2},{2,3},{3,0},{4,5},{5,6},{6,7},{7,4},{8,9},{9,10},{10,1... | collective-permute-start | bytes 1966088 | tf_op jit(solution)/shard_map/ppermute | solution.py:70
  717.8 41.9 %collective-permute-start.27 = (bf16[2,80,2048]{2,1,0:T(8,128)(2,1)S(1)}, bf16[2,80,2048]{2,1,0:T(8,128)(2,1)S(1)}, u32[]{:S(2)}, u32[]{:S(2)}) collective-permute-start(bf16[2,80,2048]{2,1,0:T(8,128)(2,1)S(1)} %get-tuple-element.133), channel_id=1, source_target_pairs={{0,3},{1,0},{2,1},{3,2},{4,7},{5,4},{6,5},{7,6},{8,11},{9,8},{10,9... | collective-permute-start | bytes 1966088 | tf_op jit(solution)/shard_map/ppermute | solution.py:70
  772.8 38.7 %collective-permute-start.28 = (bf16[2,80,2048]{2,1,0:T(8,128)(2,1)}, bf16[2,80,2048]{2,1,0:T(8,128)(2,1)}, u32[]{:S(2)}, u32[]{:S(2)}) collective-permute-start(bf16[2,80,2048]{2,1,0:T(8,128)(2,1)} %get-tuple-element.198), channel_id=1, source_target_pairs={{0,1},{1,2},{2,3},{3,0},{4,5},{5,6},{6,7},{7,4},{8,9},{9,10},{10,1... | collective-permute-start | bytes 1966088 | tf_op jit(solution)/shard_map/ppermute | solution.py:127
  781.6 29.9 %collective-permute-start.30 = (bf16[2,80,2048]{2,1,0:T(8,128)(2,1)}, bf16[2,80,2048]{2,1,0:T(8,128)(2,1)}, u32[]{:S(2)}, u32[]{:S(2)}) collective-permute-start(bf16[2,80,2048]{2,1,0:T(8,128)(2,1)} %get-tuple-element.199), channel_id=1, source_target_pairs={{0,3},{1,0},{2,1},{3,2},{4,7},{5,4},{6,5},{7,6},{8,11},{9,8},{10,9... | collective-permute-start | bytes 1966088 | tf_op jit(solution)/shard_map/ppermute | solution.py:127
  782.0 50.5 %collective-permute-start.29 = (bf16[2,80,2048]{2,1,0:T(8,128)(2,1)}, bf16[2,80,2048]{2,1,0:T(8,128)(2,1)}, u32[]{:S(2)}, u32[]{:S(2)}) collective-permute-start(bf16[2,80,2048]{2,1,0:T(8,128)(2,1)} %get-tuple-element.200), channel_id=1, source_target_pairs={{0,2},{1,3},{2,0},{3,1},{4,6},{5,7},{6,4},{7,5},{8,10},{9,11},{10,... | collective-permute-start | bytes 1966088 | tf_op jit(solution)/shard_map/ppermute | solution.py:127
  895.2 19.8 %collective-permute-start.31 = (bf16[2,80,2048]{2,1,0:T(8,128)(2,1)}, bf16[2,80,2048]{2,1,0:T(8,128)(2,1)}, u32[]{:S(2)}, u32[]{:S(2)}) collective-permute-start(bf16[2,80,2048]{2,1,0:T(8,128)(2,1)} %get-tuple-element.195), channel_id=1, source_target_pairs={{0,1},{1,2},{2,3},{3,0},{4,5},{5,6},{6,7},{7,4},{8,9},{9,10},{10,1... | collective-permute-start | bytes 1966088 | tf_op jit(solution)/shard_map/ppermute | solution.py:127
  896.6 30.4 %collective-permute-start.33 = (bf16[2,80,2048]{2,1,0:T(8,128)(2,1)}, bf16[2,80,2048]{2,1,0:T(8,128)(2,1)}, u32[]{:S(2)}, u32[]{:S(2)}) collective-permute-start(bf16[2,80,2048]{2,1,0:T(8,128)(2,1)} %get-tuple-element.196), channel_id=1, source_target_pairs={{0,3},{1,0},{2,1},{3,2},{4,7},{5,4},{6,5},{7,6},{8,11},{9,8},{10,9... | collective-permute-start | bytes 1966088 | tf_op jit(solution)/shard_map/ppermute | solution.py:127
  899.0 56.7 %collective-permute-start.32 = (bf16[2,80,2048]{2,1,0:T(8,128)(2,1)}, bf16[2,80,2048]{2,1,0:T(8,128)(2,1)}, u32[]{:S(2)}, u32[]{:S(2)}) collective-permute-start(bf16[2,80,2048]{2,1,0:T(8,128)(2,1)} %get-tuple-element.197), channel_id=1, source_target_pairs={{0,2},{1,3},{2,0},{3,1},{4,6},{5,7},{6,4},{7,5},{8,10},{9,11},{10,... | collective-permute-start | bytes 1966088 | tf_op jit(solution)/shard_map/ppermute | solution.py:127
  975.4 15.3 %collective-permute-start.34 = (bf16[1,64,128]{1,2,0:T(8,128)(2,1)S(1)}, bf16[1,64,128]{1,2,0:T(8,128)(2,1)S(1)}, u32[]{:S(2)}, u32[]{:S(2)}) collective-permute-start(bf16[1,64,128]{1,2,0:T(8,128)(2,1)S(1)} %get-tuple-element.225), channel_id=1, source_target_pairs={{0,1},{1,2},{2,3},{3,0},{4,5},{5,6},{6,7},{7,4},{8,9},{9,10},{10,1... | collective-permute-start | bytes 49160 | tf_op jit(solution)/shard_map/ppermute | solution.py:127
  975.5 15.3 %collective-permute-start.36 = (bf16[1,64,128]{1,2,0:T(8,128)(2,1)S(1)}, bf16[1,64,128]{1,2,0:T(8,128)(2,1)S(1)}, u32[]{:S(2)}, u32[]{:S(2)}) collective-permute-start(bf16[1,64,128]{1,2,0:T(8,128)(2,1)S(1)} %get-tuple-element.226), channel_id=1, source_target_pairs={{0,3},{1,0},{2,1},{3,2},{4,7},{5,4},{6,5},{7,6},{8,11},{9,8},{10,9... | collective-permute-start | bytes 49160 | tf_op jit(solution)/shard_map/ppermute | solution.py:127
  979.3 11.5 %collective-permute-start.35 = (bf16[1,64,128]{1,2,0:T(8,128)(2,1)S(1)}, bf16[1,64,128]{1,2,0:T(8,128)(2,1)S(1)}, u32[]{:S(2)}, u32[]{:S(2)}) collective-permute-start(bf16[1,64,128]{1,2,0:T(8,128)(2,1)S(1)} %get-tuple-element.227), channel_id=1, source_target_pairs={{0,2},{1,3},{2,0},{3,1},{4,6},{5,7},{6,4},{7,5},{8,10},{9,11},{10,... | collective-permute-start | bytes 49160 | tf_op jit(solution)/shard_map/ppermute | solution.py:127
  (122 other events, 1256.3 us)
Sparse Core Ops, SparseCore 0:
  29.5 211.7 all-gather.2
  243.7 173.1 all-gather.4
  452.6 222.4 reduce-scatter.3
  678.6 210.7 reduce-scatter.5
  892.9 73.8 reduce-scatter.7

commit v3 on v2

--- a/solution.py
+++ b/solution.py
@@ -114,6 +114,45 @@
         other = swap(value, lambda i: 1)
         full = lax.dynamic_update_index_in_dim(full, other, rank ^ (bits | 1), 0)
     return full.reshape(count * own.shape[0], own.shape[1]), passed
+
+
+def fsdp_scatter(part):
+    count = lax.axis_size("fsdp")
+    if count != 8:
+        return lax.psum_scatter(part, "fsdp", scatter_dimension=0, tiled=True)
+    rank = lax.axis_index("fsdp")
+    core = lax.rem(rank, 2)
+    across = lax.rem(rank // 2, 2)
+    along = rank // 4
+    even = core == 0
+
+    def swap(value, bits):
+        return lax.ppermute(value, "fsdp", [(i, i ^ bits(i)) for i in range(count)])
+
+    def add(a, b):
+        return (a.astype(F32) + b.astype(F32)).astype(BF16)
+
+    rows = part.shape[0] // count
+    halves = part.reshape(4, 2, rows, part.shape[1])
+    sums = add(
+        lax.dynamic_index_in_dim(halves, core, 1, keepdims=False),
+        swap(lax.dynamic_index_in_dim(halves, 1 - core, 1, keepdims=False), lambda i: 1),
+    )
+    chosen = jnp.where(even, along, across)
+    joined = []
+    for kept in (1 - chosen, chosen):
+        own = jnp.where(even, kept * 2 + across, along * 2 + kept)
+        sent = jnp.where(even, kept * 2 + 1 - across, (1 - along) * 2 + kept)
+        joined.append(
+            add(
+                lax.dynamic_index_in_dim(sums, own, 0, keepdims=False),
+                swap(
+                    lax.dynamic_index_in_dim(sums, sent, 0, keepdims=False),
+                    lambda i: 4 if i % 2 else 2,
+                ),
+            )
+        )
+    return add(joined[1], swap(joined[0], lambda i: 2 if i % 2 else 4))
 
 
 def tp_scatter(part):
@@ -330,8 +369,11 @@
         ],
         axis=1,
     )
-    attn_packed, pair_grads, output = lax.optimization_barrier((attn_packed, pair_grads, output))
-    attn_grads = lax.psum_scatter(attn_packed, "fsdp", scatter_dimension=0, tiled=True)
+    attn_grads = fsdp_scatter(attn_packed)
+    small_grads, pair_grads, output, input_grad = lax.optimization_barrier(
+        (attn_grads[None, :, 4 * head_width :], pair_grads, output, input_grad)
+    )
+    small_grads = tp_scatter(small_grads)[0]
     expert_grads = [
         item[:, e * span : (e + 1) * span] for item in pair_grads for e in range(PAIR)
     ]
@@ -340,10 +382,6 @@
         jnp.stack([item[:, units : 2 * units] for item in expert_grads]).astype(F32),
         jnp.stack([item[:, 2 * units :].T for item in expert_grads]).astype(F32),
     )
-    small_grads, expert_grads = lax.optimization_barrier(
-        (attn_grads[None, :, 4 * head_width :], expert_grads)
-    )
-    small_grads = tp_scatter(small_grads)[0]
     attn_grads = attn_grads.astype(F32)
     return (
         output,

time: 1010 us -> 1030 us (1.020)
  waiting for transfers between devices: 417 us -> 361 us
  local copies, waits for them, and re-layouts: 115 us -> 157 us
  starting transfers between devices: 95.2 us -> 114 us
    reduce_scatter x2, waiting for transfers between devices: 53.9 us -> 0.01 us  [per_device(): lax.psum_scatter(packed, 'fsdp', scatter_dimension=0, tiled=True)]
    dynamic_slice x0 -> x2, local copies, waits for them, and re-layouts: none -> 24.7 us  [the longest x1 21.1 us: fsdp_scatter(): lax.dynamic_index_in_dim(halves, core, 1, keepdims=False)]
    ppermute x15, starting transfers between devices: 41.4 us -> 58.5 us  [tp_scatter(): lax.ppermute(piece, 'tp', [(i, (i + k) % count) for i in range(count)])]
    reshape x0 -> x1, local copies, waits for them, and re-layouts: none -> 15.6 us  [fsdp_scatter(): halves = part.reshape(4, 2, rows, part.shape[1])]
    unnamed x286 -> x270, local copies, waits for them, and re-layouts: 56.8 us -> 55.7 us
    ppermute x7 -> x11, waiting for transfers between devices: 69.9 us -> 69.9 us  [swap(): return lax.ppermute(value, 'fsdp', [(i, i ^ bits(i)) for i in range(count)])]
  transfers between devices with their start and end apart: 42 -> 45, of which waited for: 24 -> 20; matrix products, arithmetic and copies ran while one was open for 43% -> 48% of each run, Pallas kernels for 0% -> 0%
where the time goes in v3:
time: 1030 us; the launch traced here: 1020 us
  waiting for transfers between devices  361 us (35%)
  matrix products  257 us (25%)
  local copies, waits for them, and re-layouts  157 us (15%)
  starting transfers between devices  114 us (11%)
  other arithmetic  110 us (11%)
  between operations  16.3 us (2%)
    dot_general x47, matrix products, dot(): return jnp.einsum(spec, a, b, preferred_element_type=F32)  249 us
    ppermute x15, waiting for transfers between devices, tp_scatter(): lax.ppermute(piece, 'tp', [(i, (i + k) % count) for i in range(count)])  184 us
    ppermute x12, waiting for transfers between devices, tp_gather(): lax.ppermute(own, 'tp', [(i, (i + k) % count) for i in range(count)])  98.1 us
    ppermute x11, waiting for transfers between devices, swap(): return lax.ppermute(value, 'fsdp', [(i, i ^ bits(i)) for i in range(count)])  69.9 us
    ppermute x15, starting transfers between devices, tp_scatter(): lax.ppermute(piece, 'tp', [(i, (i + k) % count) for i in range(count)])  58.5 us
    unnamed x270, local copies, waits for them, and re-layouts  55.7 us
    concatenate x2, other arithmetic, per_device(): jnp.concatenate(pieces, axis=1)  48.6 us
    ppermute x12, starting transfers between devices, tp_gather(): lax.ppermute(own, 'tp', [(i, (i + k) % count) for i in range(count)])  43 us
  transfers between devices with their start and end apart: 45, of which 20 were waited for; matrix products, arithmetic and copies ran while one was open for 48% of the time, Pallas kernels for 0%

profile of v3, /device:TPU:0, one launch (start us, length us, event | category | flops | bytes accessed | tf_op | source)
XLA Modules:
  0.0 1015.8 jit_solution(8726800612436287782)
XLA Ops:
  64.8 41.2 %collective-permute-done.1 = bf16[256,2176]{1,0:T(8,128)(2,1)S(1)} collective-permute-done((bf16[256,2176]{1,0:T(8,128)(2,1)}, bf16[256,2176]{1,0:T(8,128)(2,1)S(1)}, u32[]{:S(2)}, u32[]{:S(2)}) %collective-permute-start.1) | collective-permute-done | bytes 1114144 | tf_op jit(solution)/shard_map/ppermute | solution.py:104
  112.5 10.5 %collective-permute-done.2 = bf16[2,80,2048]{2,1,0:T(8,128)(2,1)S(1)} collective-permute-done((bf16[2,80,2048]{2,1,0:T(8,128)(2,1)S(1)}, bf16[2,80,2048]{2,1,0:T(8,128)(2,1)S(1)}, u32[]{:S(2)}, u32[]{:S(2)}) %collective-permute-start.2) | collective-permute-done | bytes 655392 | tf_op jit(solution)/shard_map/ppermute | solution.py:70
  123.0 14.4 %collective-permute-start.4 = (bf16[2,80,2048]{2,1,0:T(8,128)(2,1)S(1)}, bf16[2,80,2048]{2,1,0:T(8,128)(2,1)S(1)}, u32[]{:S(2)}, u32[]{:S(2)}) collective-permute-start(bf16[2,80,2048]{2,1,0:T(8,128)(2,1)S(1)} %copy-done.15), channel_id=1, source_target_pairs={{0,3},{1,0},{2,1},{3,2},{4,7},{5,4},{6,5},{7,6},{8,11},{9,8},{10,9... | collective-permute-start | bytes 1966088 | tf_op jit(solution)/shard_map/ppermute | solution.py:70
  140.5 10.5 %collective-permute-done.4 = bf16[2,80,2048]{2,1,0:T(8,128)(2,1)S(1)} collective-permute-done((bf16[2,80,2048]{2,1,0:T(8,128)(2,1)S(1)}, bf16[2,80,2048]{2,1,0:T(8,128)(2,1)S(1)}, u32[]{:S(2)}, u32[]{:S(2)}) %collective-permute-start.4) | collective-permute-done | bytes 655392 | tf_op jit(solution)/shard_map/ppermute | solution.py:70
  151.8 25.3 %collective-permute-done.8 = bf16[256,2176]{1,0:T(8,128)(2,1)S(1)} collective-permute-done((bf16[256,2176]{1,0:T(8,128)(2,1)S(1)}, bf16[256,2176]{1,0:T(8,128)(2,1)S(1)}, u32[]{:S(2)}, u32[]{:S(2)}) %collective-permute-start.8) | collective-permute-done | bytes 1114144 | tf_op jit(solution)/shard_map/ppermute | solution.py:104
  239.4 12.3 %collective-permute-done.13 = bf16[2,80,2048]{2,1,0:T(8,128)(2,1)S(1)} collective-permute-done((bf16[2,80,2048]{2,1,0:T(8,128)(2,1)S(1)}, bf16[2,80,2048]{2,1,0:T(8,128)(2,1)S(1)}, u32[]{:S(2)}, u32[]{:S(2)}) %collective-permute-start.13) | collective-permute-done | bytes 655392 | tf_op jit(solution)/shard_map/ppermute | solution.py:166
  252.5 11.5 %collective-permute-done.15 = bf16[2,80,2048]{2,1,0:T(8,128)(2,1)S(1)} collective-permute-done((bf16[2,80,2048]{2,1,0:T(8,128)(2,1)S(1)}, bf16[2,80,2048]{2,1,0:T(8,128)(2,1)S(1)}, u32[]{:S(2)}, u32[]{:S(2)}) %collective-permute-start.15) | collective-permute-done | bytes 655392 | tf_op jit(solution)/shard_map/ppermute | solution.py:166
  264.0 27.5 %collective-permute-done.14 = bf16[2,80,2048]{2,1,0:T(8,128)(2,1)S(1)} collective-permute-done((bf16[2,80,2048]{2,1,0:T(8,128)(2,1)S(1)}, bf16[2,80,2048]{2,1,0:T(8,128)(2,1)S(1)}, u32[]{:S(2)}, u32[]{:S(2)}) %collective-permute-start.14) | collective-permute-done | bytes 655392 | tf_op jit(solution)/shard_map/ppermute | solution.py:166
  292.9 13.4 %collective-permute-start.16 = (bf16[2,80,2048]{2,1,0:T(8,128)(2,1)S(1)}, bf16[2,80,2048]{2,1,0:T(8,128)(2,1)S(1)}, u32[]{:S(2)}, u32[]{:S(2)}) collective-permute-start(bf16[2,80,2048]{2,1,0:T(8,128)(2,1)S(1)} %get-tuple-element.135), channel_id=1, source_target_pairs={{0,1},{1,2},{2,3},{3,0},{4,5},{5,6},{6,7},{7,4},{8,9},{9,10},{10,1... | collective-permute-start | bytes 1966088 | tf_op jit(solution)/shard_map/ppermute | solution.py:70
  312.8 12.0 %collective-permute-done.16 = bf16[2,80,2048]{2,1,0:T(8,128)(2,1)S(1)} collective-permute-done((bf16[2,80,2048]{2,1,0:T(8,128)(2,1)S(1)}, bf16[2,80,2048]{2,1,0:T(8,128)(2,1)S(1)}, u32[]{:S(2)}, u32[]{:S(2)}) %collective-permute-start.16) | collective-permute-done | bytes 655392 | tf_op jit(solution)/shard_map/ppermute | solution.py:70
  325.0 26.1 %collective-permute-done.17 = bf16[2,80,2048]{2,1,0:T(8,128)(2,1)S(1)} collective-permute-done((bf16[2,80,2048]{2,1,0:T(8,128)(2,1)S(1)}, bf16[2,80,2048]{2,1,0:T(8,128)(2,1)S(1)}, u32[]{:S(2)}, u32[]{:S(2)}) %collective-permute-start.17) | collective-permute-done | bytes 655392 | tf_op jit(solution)/shard_map/ppermute | solution.py:70
  370.0 8.7 fusion.11
  378.7 6.1 multiply_convert_fusion.17
  384.9 5.3 convolution_convert_fusion.7
  390.2 8.6 fusion.15
  398.9 6.1 multiply_convert_fusion.20
  405.0 5.7 convolution_convert_fusion.8
  410.7 8.9 convolution_convert_fusion.3
  419.6 8.9 convolution_convert_fusion.2
  428.5 23.8 %pad_maximum_fusion = bf16[2048,8448]{1,0:T(8,128)(2,1)} fusion(bf16[2048,1408]{1,0:T(8,128)(2,1)} %convolution_convert_fusion.7, bf16[2048,2816]{1,0:T(8,128)(2,1)} %convolution_convert_fusion.2, bf16[2048,1408]{1,0:T(8,128)(2,1)} %convolution_convert_fusion.8, bf16[2048,2816]{1,0:T(8,128)(2,1)} %convolution_convert_fusion.3), kind=kLoop, calls=%fused_computation.1 | loop fusion | flops 138412032 | bytes 69206016 | tf_op jit(solution)/shard_map/concatenate | solution.py:281
  463.2 9.1 fusion.3
  472.3 8.3 multiply_convert_fusion.11
  480.6 5.4 convolution_convert_fusion.5
  486.0 9.6 fusion.7
  495.6 7.2 multiply_convert_fusion.14
  502.8 5.5 convolution_convert_fusion.6
  508.3 8.9 convolution_convert_fusion.1
  517.3 8.9 convolution_convert_fusion
  526.2 24.9 %pad_maximum_fusion.1 = bf16[2048,8448]{1,0:T(8,128)(2,1)} fusion(bf16[2048,1408]{1,0:T(8,128)(2,1)} %convolution_convert_fusion.5, bf16[2048,2816]{1,0:T(8,128)(2,1)} %convolution_convert_fusion, bf16[2048,1408]{1,0:T(8,128)(2,1)} %convolution_convert_fusion.6, bf16[2048,2816]{1,0:T(8,128)(2,1)} %convolution_convert_fusion.1), kind=kLoop, calls=%fused_computation.2 | loop fusion | flops 138412032 | bytes 69206016 | tf_op jit(solution)/shard_map/concatenate | solution.py:312
  580.5 10.1 fusion.78
  590.6 9.8 fusion.72
  600.4 9.6 fusion.69
  610.1 9.8 fusion.75
  626.7 16.2 %collective-permute-start.22 = (bf16[2,80,2176]{2,1,0:T(8,128)(2,1)}, bf16[2,80,2176]{2,1,0:T(8,128)(2,1)}, u32[]{:S(2)}, u32[]{:S(2)}) collective-permute-start(bf16[2,80,2176]{2,1,0:T(8,128)(2,1)} %get-tuple-element.192), channel_id=1, source_target_pairs={{0,1},{1,2},{2,3},{3,0},{4,5},{5,6},{6,7},{7,4},{8,9},{9,10},{10,1... | collective-permute-start | bytes 2088968 | tf_op jit(solution)/shard_map/ppermute | solution.py:166
  646.1 13.2 %collective-permute-done.22 = bf16[2,80,2176]{2,1,0:T(8,128)(2,1)} collective-permute-done((bf16[2,80,2176]{2,1,0:T(8,128)(2,1)}, bf16[2,80,2176]{2,1,0:T(8,128)(2,1)}, u32[]{:S(2)}, u32[]{:S(2)}) %collective-permute-start.22) | collective-permute-done | bytes 696352 | tf_op jit(solution)/shard_map/ppermute | solution.py:166
  659.3 14.9 %collective-permute-done.24 = bf16[2,80,2176]{2,1,0:T(8,128)(2,1)} collective-permute-done((bf16[2,80,2176]{2,1,0:T(8,128)(2,1)}, bf16[2,80,2176]{2,1,0:T(8,128)(2,1)}, u32[]{:S(2)}, u32[]{:S(2)}) %collective-permute-start.24) | collective-permute-done | bytes 696352 | tf_op jit(solution)/shard_map/ppermute | solution.py:166
  674.2 28.2 %collective-permute-done.23 = bf16[2,80,2176]{2,1,0:T(8,128)(2,1)} collective-permute-done((bf16[2,80,2176]{2,1,0:T(8,128)(2,1)S(1)}, bf16[2,80,2176]{2,1,0:T(8,128)(2,1)}, u32[]{:S(2)}, u32[]{:S(2)}) %collective-permute-start.23) | collective-permute-done | bytes 696352 | tf_op jit(solution)/shard_map/ppermute | solution.py:166
  715.1 13.9 %collective-permute-done.25 = bf16[2,80,2048]{2,1,0:T(8,128)(2,1)} collective-permute-done((bf16[2,80,2048]{2,1,0:T(8,128)(2,1)}, bf16[2,80,2048]{2,1,0:T(8,128)(2,1)}, u32[]{:S(2)}, u32[]{:S(2)}) %collective-permute-start.25) | collective-permute-done | bytes 655392 | tf_op jit(solution)/shard_map/ppermute | solution.py:70
  731.0 25.1 %collective-permute-done.26 = bf16[2,80,2048]{2,1,0:T(8,128)(2,1)} collective-permute-done((bf16[2,80,2048]{2,1,0:T(8,128)(2,1)}, bf16[2,80,2048]{2,1,0:T(8,128)(2,1)}, u32[]{:S(2)}, u32[]{:S(2)}) %collective-permute-start.26) | collective-permute-done | bytes 655392 | tf_op jit(solution)/shard_map/ppermute | solution.py:70
  789.0 5.5 convolution_convert_fusion.4
  798.7 15.6 %reshape.274 = bf16[4,2,256,2176]{2,1,0,3:T(2,128)(2,1)} reshape(bf16[2048,2176]{0,1:T(8,128)(2,1)} %pad_maximum_fusion.2) | data formatting | bytes 17825792 | tf_op jit(solution)/shard_map/reshape | solution.py:136
  814.3 21.1 %constant_dynamic-slice_fusion.11 = (bf16[4,1,256,2176]{2,1,0,3:T(2,128)(2,1)}, bf16[4,1,256,2176]{2,1,0,3:T(2,128)(2,1)S(1)}) fusion(bf16[4,2,256,2176]{2,1,0,3:T(2,128)(2,1)} %reshape.274, s32[]{:T(128)S(6)} %select_n.286, s32[]{:T(128)S(6)} %select_n.287), kind=kLoop, calls=%fused_computation.303 | loop fusion | bytes 17825800 | tf_op jit(solution)/shard_map/jit(dynamic_index_in_dim)/dynamic_slice | solution.py:138
  843.4 12.6 %collective-permute-start.35 = (bf16[2,80,2048]{2,1,0:T(8,128)(2,1)}, bf16[2,80,2048]{2,1,0:T(8,128)(2,1)}, u32[]{:S(2)}, u32[]{:S(2)}) collective-permute-start(bf16[2,80,2048]{2,1,0:T(8,128)(2,1)} %get-tuple-element.195), channel_id=1, source_target_pairs={{0,1},{1,2},{2,3},{3,0},{4,5},{5,6},{6,7},{7,4},{8,9},{9,10},{10,1... | collective-permute-start | bytes 1966088 | tf_op jit(solution)/shard_map/ppermute | solution.py:166
  857.5 7.0 fusion.17
  874.0 16.3 %collective-permute-start.34 = (bf16[2,80,2048]{2,1,0:T(8,128)(2,1)S(1)}, bf16[2,80,2048]{2,1,0:T(8,128)(2,1)S(1)}, u32[]{:S(2)}, u32[]{:S(2)}) collective-permute-start(bf16[2,80,2048]{2,1,0:T(8,128)(2,1)S(1)} %get-tuple-element.199), channel_id=1, source_target_pairs={{0,3},{1,0},{2,1},{3,2},{4,7},{5,4},{6,5},{7,6},{8,11},{9,8},{10,9... | collective-permute-start | bytes 1966088 | tf_op jit(solution)/shard_map/ppermute | solution.py:166
  890.3 38.7 %collective-permute-done.36 = bf16[2,80,2048]{2,1,0:T(8,128)(2,1)} collective-permute-done((bf16[2,80,2048]{2,1,0:T(8,128)(2,1)}, bf16[2,80,2048]{2,1,0:T(8,128)(2,1)}, u32[]{:S(2)}, u32[]{:S(2)}) %collective-permute-start.36) | collective-permute-done | bytes 655392 | tf_op jit(solution)/shard_map/ppermute | solution.py:166
  933.4 37.6 %collective-permute-done.33 = bf16[2,80,2048]{2,1,0:T(8,128)(2,1)S(1)} collective-permute-done((bf16[2,80,2048]{2,1,0:T(8,128)(2,1)S(1)}, bf16[2,80,2048]{2,1,0:T(8,128)(2,1)S(1)}, u32[]{:S(2)}, u32[]{:S(2)}) %collective-permute-start.33) | collective-permute-done | bytes 655392 | tf_op jit(solution)/shard_map/ppermute | solution.py:166
  1001.4 6.2 copy.432
  (505 shorter events, 313.5 us)
Async XLA Ops:
  7.2 362.8 %all-gather.3.cloned.1.call-start = ((), (), s32[]{:S(2)}) async-start(), calls=%async_computation.2 | async-start | bytes 38928384 | tf_op jit(solution)/shard_map/all_gather | solution.py:219
  29.4 433.8 %all-gather.5.cloned.1.call-start = ((), (), s32[]{:S(2)}) async-start(), calls=%async_computation.3 | async-start | bytes 38928384 | tf_op jit(solution)/shard_map/all_gather | solution.py:219
  45.3 939.3 %reduce-scatter.3.cloned.1.call-start = ((), (), s32[]{:S(2)}) async-start(), calls=%async_computation.4 | async-start | bytes 38928384 | tf_op jit(solution)/shard_map/reduce_scatter | solution.py:282
  45.3 265.6 %collective-permute-start.20 = (bf16[2,80,2048]{2,1,0:T(8,128)(2,1)}, bf16[2,80,2048]{2,1,0:T(8,128)(2,1)}, u32[]{:S(2)}, u32[]{:S(2)}) collective-permute-start(bf16[2,80,2048]{2,1,0:T(8,128)(2,1)} %param.15), channel_id=1, source_target_pairs={{0,2},{1,3},{2,0},{3,1},{4,6},{5,7},{6,4},{7,5},{8,10},{9,11},{10,... | collective-permute-start | bytes 1966088 | tf_op jit(solution)/shard_map/ppermute | solution.py:70
  49.5 256.8 %collective-permute-start.19 = (bf16[2,80,2048]{2,1,0:T(8,128)(2,1)}, bf16[2,80,2048]{2,1,0:T(8,128)(2,1)}, u32[]{:S(2)}, u32[]{:S(2)}) collective-permute-start(bf16[2,80,2048]{2,1,0:T(8,128)(2,1)} %param.15), channel_id=1, source_target_pairs={{0,1},{1,2},{2,3},{3,0},{4,5},{5,6},{6,7},{7,4},{8,9},{9,10},{10,1... | collective-permute-start | bytes 1966088 | tf_op jit(solution)/shard_map/ppermute | solution.py:70
  55.0 51.0 %collective-permute-start.1 = (bf16[256,2176]{1,0:T(8,128)(2,1)}, bf16[256,2176]{1,0:T(8,128)(2,1)S(1)}, u32[]{:S(2)}, u32[]{:S(2)}) collective-permute-start(bf16[256,2176]{1,0:T(8,128)(2,1)} %pad_dynamic-update-slice_fusion), channel_id=1, source_target_pairs={{0,16},{4,20},{8,24},{12,28},{16,0},{20,4},{24,8},{28,12},{1,17},{... | collective-permute-start | bytes 3342344 | tf_op jit(solution)/shard_map/ppermute | solution.py:104
  56.5 50.9 %collective-permute-start = (bf16[256,2176]{1,0:T(8,128)(2,1)}, bf16[256,2176]{1,0:T(8,128)(2,1)S(1)}, u32[]{:S(2)}, u32[]{:S(2)}) collective-permute-start(bf16[256,2176]{1,0:T(8,128)(2,1)} %pad_dynamic-update-slice_fusion), channel_id=1, source_target_pairs={{0,8},{4,12},{8,0},{12,4},{16,24},{20,28},{24,16},{28,20},{1,9},{5... | collective-permute-start | bytes 3342344 | tf_op jit(solution)/shard_map/ppermute | solution.py:104
  58.0 79.5 %collective-permute-start.3 = (bf16[2,80,2048]{2,1,0:T(8,128)(2,1)S(1)}, bf16[2,80,2048]{2,1,0:T(8,128)(2,1)}, u32[]{:S(2)}, u32[]{:S(2)}) collective-permute-start(bf16[2,80,2048]{2,1,0:T(8,128)(2,1)S(1)} %copy-done.15), channel_id=1, source_target_pairs={{0,2},{1,3},{2,0},{3,1},{4,6},{5,7},{6,4},{7,5},{8,10},{9,11},{10,... | collective-permute-start | bytes 1966088 | tf_op jit(solution)/shard_map/ppermute | solution.py:70
  60.0 297.7 %copy-start.69 = (s32[2,4,320]{2,0,1:T(2,128)}, s32[2,4,320]{2,0,1:T(2,128)S(1)}, u32[]{:S(2)}) copy-start(s32[2,4,320]{2,0,1:T(2,128)S(1)} %copy.392) | copy-start | bytes 30724
  105.9 17.1 %collective-permute-start.2 = (bf16[2,80,2048]{2,1,0:T(8,128)(2,1)S(1)}, bf16[2,80,2048]{2,1,0:T(8,128)(2,1)S(1)}, u32[]{:S(2)}, u32[]{:S(2)}) collective-permute-start(bf16[2,80,2048]{2,1,0:T(8,128)(2,1)S(1)} %copy-done.15), channel_id=1, source_target_pairs={{0,1},{1,2},{2,3},{3,0},{4,5},{5,6},{6,7},{7,4},{8,9},{9,10},{10,1... | collective-permute-start | bytes 1966088 | tf_op jit(solution)/shard_map/ppermute | solution.py:70
  107.4 32.9 %collective-permute-start.5 = (bf16[256,2176]{1,0:T(8,128)(2,1)}, bf16[256,2176]{1,0:T(8,128)(2,1)S(1)}, u32[]{:S(2)}, u32[]{:S(2)}) collective-permute-start(bf16[256,2176]{1,0:T(8,128)(2,1)} %pad_dynamic-update-slice_fusion), channel_id=1, source_target_pairs={{0,4},{4,0},{8,12},{12,8},{16,20},{20,16},{24,28},{28,24},{1,5},{5... | collective-permute-start | bytes 3342344 | tf_op jit(solution)/shard_map/ppermute | solution.py:104
  123.0 27.9 %collective-permute-start.4 = (bf16[2,80,2048]{2,1,0:T(8,128)(2,1)S(1)}, bf16[2,80,2048]{2,1,0:T(8,128)(2,1)S(1)}, u32[]{:S(2)}, u32[]{:S(2)}) collective-permute-start(bf16[2,80,2048]{2,1,0:T(8,128)(2,1)S(1)} %copy-done.15), channel_id=1, source_target_pairs={{0,3},{1,0},{2,1},{3,2},{4,7},{5,4},{6,5},{7,6},{8,11},{9,8},{10,9... | collective-permute-start | bytes 1966088 | tf_op jit(solution)/shard_map/ppermute | solution.py:70
  137.5 39.6 %collective-permute-start.8 = (bf16[256,2176]{1,0:T(8,128)(2,1)S(1)}, bf16[256,2176]{1,0:T(8,128)(2,1)S(1)}, u32[]{:S(2)}, u32[]{:S(2)}) collective-permute-start(bf16[256,2176]{1,0:T(8,128)(2,1)S(1)} %broadcast_select_fusion), channel_id=1, source_target_pairs={{0,8},{4,20},{8,0},{12,28},{16,24},{20,4},{24,16},{28,12},{1,9},{5... | collective-permute-start | bytes 3342344 | tf_op jit(solution)/shard_map/ppermute | solution.py:104
  140.3 37.1 %collective-permute-start.7 = (bf16[256,2176]{1,0:T(8,128)(2,1)S(1)}, bf16[256,2176]{1,0:T(8,128)(2,1)S(1)}, u32[]{:S(2)}, u32[]{:S(2)}) collective-permute-start(bf16[256,2176]{1,0:T(8,128)(2,1)S(1)} %copy-done.21), channel_id=1, source_target_pairs={{0,4},{4,0},{8,12},{12,8},{16,20},{20,16},{24,28},{28,24},{1,5},{5... | collective-permute-start | bytes 3342344 | tf_op jit(solution)/shard_map/ppermute | solution.py:104
  151.0 26.1 %collective-permute-start.6 = (bf16[256,2176]{1,0:T(8,128)(2,1)S(1)}, bf16[256,2176]{1,0:T(8,128)(2,1)S(1)}, u32[]{:S(2)}, u32[]{:S(2)}) collective-permute-start(bf16[256,2176]{1,0:T(8,128)(2,1)S(1)} %copy-done.23), channel_id=1, source_target_pairs={{0,4},{4,0},{8,12},{12,8},{16,20},{20,16},{24,28},{28,24},{1,5},{5... | collective-permute-start | bytes 3342344 | tf_op jit(solution)/shard_map/ppermute | solution.py:104
  177.1 2.8 collective-permute-start.9
  180.1 8.3 collective-permute-start.12
  180.1 13.0 %collective-permute-start.11 = (bf16[512,128]{1,0:T(8,128)(2,1)S(1)}, bf16[512,128]{1,0:T(8,128)(2,1)S(1)}, u32[]{:S(2)}, u32[]{:S(2)}) collective-permute-start(bf16[512,128]{1,0:T(8,128)(2,1)S(1)} %bitcast.341), channel_id=1, source_target_pairs={{0,2},{1,3},{2,0},{3,1},{4,6},{5,7},{6,4},{7,5},{8,10},{9,11},{10,... | collective-permute-start | bytes 393224 | tf_op jit(solution)/shard_map/ppermute | solution.py:83
  182.0 11.1 %collective-permute-start.10 = (bf16[512,128]{1,0:T(8,128)(2,1)S(1)}, bf16[512,128]{1,0:T(8,128)(2,1)S(1)}, u32[]{:S(2)}, u32[]{:S(2)}) collective-permute-start(bf16[512,128]{1,0:T(8,128)(2,1)S(1)} %bitcast.342), channel_id=1, source_target_pairs={{0,3},{1,0},{2,1},{3,2},{4,7},{5,4},{6,5},{7,6},{8,11},{9,8},{10,9... | collective-permute-start | bytes 393224 | tf_op jit(solution)/shard_map/ppermute | solution.py:83
  193.3 158.0 %copy-start.12 = (bf16[8,4,64,128]{3,2,1,0:T(8,128)(2,1)}, bf16[8,4,64,128]{3,2,1,0:T(8,128)(2,1)S(1)}, u32[]{:S(2)}) copy-start(bf16[8,4,64,128]{3,2,1,0:T(8,128)(2,1)S(1)} %copy.384) | copy-start | bytes 1572868
  232.2 19.5 %collective-permute-start.13 = (bf16[2,80,2048]{2,1,0:T(8,128)(2,1)S(1)}, bf16[2,80,2048]{2,1,0:T(8,128)(2,1)S(1)}, u32[]{:S(2)}, u32[]{:S(2)}) collective-permute-start(bf16[2,80,2048]{2,1,0:T(8,128)(2,1)S(1)} %get-tuple-element.201), channel_id=1, source_target_pairs={{0,1},{1,2},{2,3},{3,0},{4,5},{5,6},{6,7},{7,4},{8,9},{9,10},{10,1... | collective-permute-start | bytes 1966088 | tf_op jit(solution)/shard_map/ppermute | solution.py:166
  234.8 29.2 %collective-permute-start.15 = (bf16[2,80,2048]{2,1,0:T(8,128)(2,1)S(1)}, bf16[2,80,2048]{2,1,0:T(8,128)(2,1)S(1)}, u32[]{:S(2)}, u32[]{:S(2)}) collective-permute-start(bf16[2,80,2048]{2,1,0:T(8,128)(2,1)S(1)} %get-tuple-element.202), channel_id=1, source_target_pairs={{0,3},{1,0},{2,1},{3,2},{4,7},{5,4},{6,5},{7,6},{8,11},{9,8},{10,9... | collective-permute-start | bytes 1966088 | tf_op jit(solution)/shard_map/ppermute | solution.py:166
  236.0 55.4 %collective-permute-start.14 = (bf16[2,80,2048]{2,1,0:T(8,128)(2,1)S(1)}, bf16[2,80,2048]{2,1,0:T(8,128)(2,1)S(1)}, u32[]{:S(2)}, u32[]{:S(2)}) collective-permute-start(bf16[2,80,2048]{2,1,0:T(8,128)(2,1)S(1)} %get-tuple-element.203), channel_id=1, source_target_pairs={{0,2},{1,3},{2,0},{3,1},{4,6},{5,7},{6,4},{7,5},{8,10},{9,11},{10,... | collective-permute-start | bytes 1966088 | tf_op jit(solution)/shard_map/ppermute | solution.py:166
  237.7 220.1 %copy-start.36 = (bf16[2,200,320]{2,1,0:T(8,128)(2,1)}, bf16[2,200,320]{2,1,0:T(8,128)(2,1)S(1)}, u32[]{:S(2)}) copy-start(bf16[2,200,320]{2,1,0:T(8,128)(2,1)S(1)} %slice_bitcast_fusion.29) | copy-start | bytes 768004
  251.7 61.1 %collective-permute-start.21 = (bf16[2,80,2048]{2,1,0:T(8,128)(2,1)}, bf16[2,80,2048]{2,1,0:T(8,128)(2,1)S(1)}, u32[]{:S(2)}, u32[]{:S(2)}) collective-permute-start(bf16[2,80,2048]{2,1,0:T(8,128)(2,1)} %param.15), channel_id=1, source_target_pairs={{0,3},{1,0},{2,1},{3,2},{4,7},{5,4},{6,5},{7,6},{8,11},{9,8},{10,9... | collective-permute-start | bytes 1966088 | tf_op jit(solution)/shard_map/ppermute | solution.py:70
  292.9 31.9 %collective-permute-start.16 = (bf16[2,80,2048]{2,1,0:T(8,128)(2,1)S(1)}, bf16[2,80,2048]{2,1,0:T(8,128)(2,1)S(1)}, u32[]{:S(2)}, u32[]{:S(2)}) collective-permute-start(bf16[2,80,2048]{2,1,0:T(8,128)(2,1)S(1)} %get-tuple-element.135), channel_id=1, source_target_pairs={{0,1},{1,2},{2,3},{3,0},{4,5},{5,6},{6,7},{7,4},{8,9},{9,10},{10,1... | collective-permute-start | bytes 1966088 | tf_op jit(solution)/shard_map/ppermute | solution.py:70
  307.5 43.6 %collective-permute-start.17 = (bf16[2,80,2048]{2,1,0:T(8,128)(2,1)S(1)}, bf16[2,80,2048]{2,1,0:T(8,128)(2,1)S(1)}, u32[]{:S(2)}, u32[]{:S(2)}) collective-permute-start(bf16[2,80,2048]{2,1,0:T(8,128)(2,1)S(1)} %get-tuple-element.135), channel_id=1, source_target_pairs={{0,2},{1,3},{2,0},{3,1},{4,6},{5,7},{6,4},{7,5},{8,10},{9,11},{10,... | collective-permute-start | bytes 1966088 | tf_op jit(solution)/shard_map/ppermute | solution.py:70
  312.3 38.9 %collective-permute-start.18 = (bf16[2,80,2048]{2,1,0:T(8,128)(2,1)S(1)}, bf16[2,80,2048]{2,1,0:T(8,128)(2,1)S(1)}, u32[]{:S(2)}, u32[]{:S(2)}) collective-permute-start(bf16[2,80,2048]{2,1,0:T(8,128)(2,1)S(1)} %get-tuple-element.135), channel_id=1, source_target_pairs={{0,3},{1,0},{2,1},{3,2},{4,7},{5,4},{6,5},{7,6},{8,11},{9,8},{10,9... | collective-permute-start | bytes 1966088 | tf_op jit(solution)/shard_map/ppermute | solution.py:70
  452.3 532.3 %reduce-scatter.5.cloned.1.call-start = ((), (), s32[]{:S(2)}) async-start(), calls=%async_computation.5 | async-start | bytes 38928384 | tf_op jit(solution)/shard_map/reduce_scatter | solution.py:313
  626.7 32.6 %collective-permute-start.22 = (bf16[2,80,2176]{2,1,0:T(8,128)(2,1)}, bf16[2,80,2176]{2,1,0:T(8,128)(2,1)}, u32[]{:S(2)}, u32[]{:S(2)}) collective-permute-start(bf16[2,80,2176]{2,1,0:T(8,128)(2,1)} %get-tuple-element.192), channel_id=1, source_target_pairs={{0,1},{1,2},{2,3},{3,0},{4,5},{5,6},{6,7},{7,4},{8,9},{9,10},{10,1... | collective-permute-start | bytes 2088968 | tf_op jit(solution)/shard_map/ppermute | solution.py:166
  642.9 31.3 %collective-permute-start.24 = (bf16[2,80,2176]{2,1,0:T(8,128)(2,1)}, bf16[2,80,2176]{2,1,0:T(8,128)(2,1)}, u32[]{:S(2)}, u32[]{:S(2)}) collective-permute-start(bf16[2,80,2176]{2,1,0:T(8,128)(2,1)} %get-tuple-element.193), channel_id=1, source_target_pairs={{0,3},{1,0},{2,1},{3,2},{4,7},{5,4},{6,5},{7,6},{8,11},{9,8},{10,9... | collective-permute-start | bytes 2088968 | tf_op jit(solution)/shard_map/ppermute | solution.py:166
  642.9 59.5 %collective-permute-start.23 = (bf16[2,80,2176]{2,1,0:T(8,128)(2,1)S(1)}, bf16[2,80,2176]{2,1,0:T(8,128)(2,1)}, u32[]{:S(2)}, u32[]{:S(2)}) collective-permute-start(bf16[2,80,2176]{2,1,0:T(8,128)(2,1)S(1)} %get-tuple-element.194), channel_id=1, source_target_pairs={{0,2},{1,3},{2,0},{3,1},{4,6},{5,7},{6,4},{7,5},{8,10},{9,11},{10,... | collective-permute-start | bytes 2088968 | tf_op jit(solution)/shard_map/ppermute | solution.py:166
  709.1 19.9 %collective-permute-start.25 = (bf16[2,80,2048]{2,1,0:T(8,128)(2,1)}, bf16[2,80,2048]{2,1,0:T(8,128)(2,1)}, u32[]{:S(2)}, u32[]{:S(2)}) collective-permute-start(bf16[2,80,2048]{2,1,0:T(8,128)(2,1)} %get-tuple-element.129), channel_id=1, source_target_pairs={{0,1},{1,2},{2,3},{3,0},{4,5},{5,6},{6,7},{7,4},{8,9},{9,10},{10,1... | collective-permute-start | bytes 1966088 | tf_op jit(solution)/shard_map/ppermute | solution.py:70
  710.1 46.1 %collective-permute-start.26 = (bf16[2,80,2048]{2,1,0:T(8,128)(2,1)}, bf16[2,80,2048]{2,1,0:T(8,128)(2,1)}, u32[]{:S(2)}, u32[]{:S(2)}) collective-permute-start(bf16[2,80,2048]{2,1,0:T(8,128)(2,1)} %get-tuple-element.129), channel_id=1, source_target_pairs={{0,2},{1,3},{2,0},{3,1},{4,6},{5,7},{6,4},{7,5},{8,10},{9,11},{10,... | collective-permute-start | bytes 1966088 | tf_op jit(solution)/shard_map/ppermute | solution.py:70
  713.5 44.6 %collective-permute-start.27 = (bf16[2,80,2048]{2,1,0:T(8,128)(2,1)}, bf16[2,80,2048]{2,1,0:T(8,128)(2,1)S(1)}, u32[]{:S(2)}, u32[]{:S(2)}) collective-permute-start(bf16[2,80,2048]{2,1,0:T(8,128)(2,1)} %get-tuple-element.129), channel_id=1, source_target_pairs={{0,3},{1,0},{2,1},{3,2},{4,7},{5,4},{6,5},{7,6},{8,11},{9,8},{10,9... | collective-permute-start | bytes 1966088 | tf_op jit(solution)/shard_map/ppermute | solution.py:70
  839.0 18.6 %collective-permute-start.28 = (bf16[4,256,2176]{1,2,0:T(8,128)(2,1)}, bf16[4,256,2176]{1,2,0:T(8,128)(2,1)}, u32[]{:S(2)}, u32[]{:S(2)}) collective-permute-start(bf16[4,256,2176]{1,2,0:T(8,128)(2,1)} %bitcast.288), channel_id=1, source_target_pairs={{0,4},{4,0},{8,12},{12,8},{16,20},{20,16},{24,28},{28,24},{1,5},{5... | collective-permute-start | bytes 13369352 | tf_op jit(solution)/shard_map/ppermute | solution.py:130
  843.4 30.5 %collective-permute-start.35 = (bf16[2,80,2048]{2,1,0:T(8,128)(2,1)}, bf16[2,80,2048]{2,1,0:T(8,128)(2,1)}, u32[]{:S(2)}, u32[]{:S(2)}) collective-permute-start(bf16[2,80,2048]{2,1,0:T(8,128)(2,1)} %get-tuple-element.195), channel_id=1, source_target_pairs={{0,1},{1,2},{2,3},{3,0},{4,5},{5,6},{6,7},{7,4},{8,9},{9,10},{10,1... | collective-permute-start | bytes 1966088 | tf_op jit(solution)/shard_map/ppermute | solution.py:166
  856.0 34.3 %collective-permute-start.37 = (bf16[2,80,2048]{2,1,0:T(8,128)(2,1)}, bf16[2,80,2048]{2,1,0:T(8,128)(2,1)}, u32[]{:S(2)}, u32[]{:S(2)}) collective-permute-start(bf16[2,80,2048]{2,1,0:T(8,128)(2,1)} %get-tuple-element.196), channel_id=1, source_target_pairs={{0,3},{1,0},{2,1},{3,2},{4,7},{5,4},{6,5},{7,6},{8,11},{9,8},{10,9... | collective-permute-start | bytes 1966088 | tf_op jit(solution)/shard_map/ppermute | solution.py:166
  857.0 72.1 %collective-permute-start.36 = (bf16[2,80,2048]{2,1,0:T(8,128)(2,1)}, bf16[2,80,2048]{2,1,0:T(8,128)(2,1)}, u32[]{:S(2)}, u32[]{:S(2)}) collective-permute-start(bf16[2,80,2048]{2,1,0:T(8,128)(2,1)} %get-tuple-element.197), channel_id=1, source_target_pairs={{0,2},{1,3},{2,0},{3,1},{4,6},{5,7},{6,4},{7,5},{8,10},{9,11},{10,... | collective-permute-start | bytes 1966088 | tf_op jit(solution)/shard_map/ppermute | solution.py:166
  864.7 68.3 %collective-permute-start.30 = (bf16[256,2176]{0,1:T(8,128)(2,1)S(1)}, bf16[256,2176]{0,1:T(8,128)(2,1)S(1)}, u32[]{:S(2)}, u32[]{:S(2)}) collective-permute-start(bf16[256,2176]{0,1:T(8,128)(2,1)S(1)} %get-tuple-element.155), channel_id=1, source_target_pairs={{0,8},{4,20},{8,0},{12,28},{16,24},{20,4},{24,16},{28,12},{1,9},{5... | collective-permute-start | bytes 3342344 | tf_op jit(solution)/shard_map/ppermute | solution.py:130
  871.7 61.7 %collective-permute-start.32 = (bf16[2,80,2048]{2,1,0:T(8,128)(2,1)S(1)}, bf16[2,80,2048]{2,1,0:T(8,128)(2,1)S(1)}, u32[]{:S(2)}, u32[]{:S(2)}) collective-permute-start(bf16[2,80,2048]{2,1,0:T(8,128)(2,1)S(1)} %get-tuple-element.198), channel_id=1, source_target_pairs={{0,1},{1,2},{2,3},{3,0},{4,5},{5,6},{6,7},{7,4},{8,9},{9,10},{10,1... | collective-permute-start | bytes 1966088 | tf_op jit(solution)/shard_map/ppermute | solution.py:166
  874.0 59.5 %collective-permute-start.34 = (bf16[2,80,2048]{2,1,0:T(8,128)(2,1)S(1)}, bf16[2,80,2048]{2,1,0:T(8,128)(2,1)S(1)}, u32[]{:S(2)}, u32[]{:S(2)}) collective-permute-start(bf16[2,80,2048]{2,1,0:T(8,128)(2,1)S(1)} %get-tuple-element.199), channel_id=1, source_target_pairs={{0,3},{1,0},{2,1},{3,2},{4,7},{5,4},{6,5},{7,6},{8,11},{9,8},{10,9... | collective-permute-start | bytes 1966088 | tf_op jit(solution)/shard_map/ppermute | solution.py:166
  890.3 80.8 %collective-permute-start.33 = (bf16[2,80,2048]{2,1,0:T(8,128)(2,1)S(1)}, bf16[2,80,2048]{2,1,0:T(8,128)(2,1)S(1)}, u32[]{:S(2)}, u32[]{:S(2)}) collective-permute-start(bf16[2,80,2048]{2,1,0:T(8,128)(2,1)S(1)} %get-tuple-element.200), channel_id=1, source_target_pairs={{0,2},{1,3},{2,0},{3,1},{4,6},{5,7},{6,4},{7,5},{8,10},{9,11},{10,... | collective-permute-start | bytes 1966088 | tf_op jit(solution)/shard_map/ppermute | solution.py:166
  931.2 44.7 %collective-permute-start.29 = (bf16[256,2176]{0,1:T(8,128)(2,1)S(1)}, bf16[256,2176]{0,1:T(8,128)(2,1)S(1)}, u32[]{:S(2)}, u32[]{:S(2)}) collective-permute-start(bf16[256,2176]{0,1:T(8,128)(2,1)S(1)} %get-tuple-element.154), channel_id=1, source_target_pairs={{0,8},{4,20},{8,0},{12,28},{16,24},{20,4},{24,16},{28,12},{1,9},{5... | collective-permute-start | bytes 3342344 | tf_op jit(solution)/shard_map/ppermute | solution.py:130
  933.3 42.6 %collective-permute-start.31 = (bf16[256,2176]{0,1:T(8,128)(2,1)S(1)}, bf16[256,2176]{0,1:T(8,128)(2,1)S(1)}, u32[]{:S(2)}, u32[]{:S(2)}) collective-permute-start(bf16[256,2176]{0,1:T(8,128)(2,1)S(1)} %fusion.86), channel_id=1, source_target_pairs={{0,16},{4,12},{8,24},{12,4},{16,0},{20,28},{24,8},{28,20},{1,17},{... | collective-permute-start | bytes 3342344 | tf_op jit(solution)/shard_map/ppermute | solution.py:130
  984.7 22.9 %collective-permute-start.38 = (bf16[1,64,128]{1,2,0:T(8,128)(2,1)S(1)}, bf16[1,64,128]{1,2,0:T(8,128)(2,1)S(1)}, u32[]{:S(2)}, u32[]{:S(2)}) collective-permute-start(bf16[1,64,128]{1,2,0:T(8,128)(2,1)S(1)} %get-tuple-element.225), channel_id=1, source_target_pairs={{0,1},{1,2},{2,3},{3,0},{4,5},{5,6},{6,7},{7,4},{8,9},{9,10},{10,1... | collective-permute-start | bytes 49160 | tf_op jit(solution)/shard_map/ppermute | solution.py:166
  984.7 22.9 %collective-permute-start.40 = (bf16[1,64,128]{1,2,0:T(8,128)(2,1)S(1)}, bf16[1,64,128]{1,2,0:T(8,128)(2,1)S(1)}, u32[]{:S(2)}, u32[]{:S(2)}) collective-permute-start(bf16[1,64,128]{1,2,0:T(8,128)(2,1)S(1)} %get-tuple-element.226), channel_id=1, source_target_pairs={{0,3},{1,0},{2,1},{3,2},{4,7},{5,4},{6,5},{7,6},{8,11},{9,8},{10,9... | collective-permute-start | bytes 49160 | tf_op jit(solution)/shard_map/ppermute | solution.py:166
  988.5 19.0 %collective-permute-start.39 = (bf16[1,64,128]{1,2,0:T(8,128)(2,1)S(1)}, bf16[1,64,128]{1,2,0:T(8,128)(2,1)S(1)}, u32[]{:S(2)}, u32[]{:S(2)}) collective-permute-start(bf16[1,64,128]{1,2,0:T(8,128)(2,1)S(1)} %get-tuple-element.227), channel_id=1, source_target_pairs={{0,2},{1,3},{2,0},{3,1},{4,6},{5,7},{6,4},{7,5},{8,10},{9,11},{10,... | collective-permute-start | bytes 49160 | tf_op jit(solution)/shard_map/ppermute | solution.py:166
  (117 other events, 1467.6 us)
Sparse Core Ops, SparseCore 0:
  29.5 211.7 all-gather.2
  243.8 173.1 all-gather.4
  452.4 222.3 reduce-scatter.2
  678.4 220.8 reduce-scatter.4
